TPU v7x, 32 devices: a whole 2x2x4 slice. The times are simulated.
32 devices in a mesh: fsdp: 4 (over x, core), seq: 8 (over z, y).
Axes of the slice: x: 2, y: 2, z: 4, core: 2. Of those that a mesh axis runs over, the one named last changes fastest.
Arguments:
- tokens: bfloat16 [8, 2048, 1024], P('fsdp', 'seq'), may hold values from -6 to 6
- cotangent: bfloat16 [8, 2048, 1024], P('fsdp', 'seq'), may hold values from -6 to 6
- w_query: bfloat16 [1024, 1024], P(('fsdp', 'seq')), may hold values from -0.25 to 0.25
- w_key: bfloat16 [1024, 1024], P(('fsdp', 'seq')), may hold values from -0.25 to 0.25
- w_value: bfloat16 [1024, 1024], P(('fsdp', 'seq')), may hold values from -0.1875 to 0.1875
- w_output: bfloat16 [1024, 1024], P(('fsdp', 'seq')), may hold values from -0.1875 to 0.1875
- w_up: bfloat16 [1024, 4096], P(('fsdp', 'seq')), may hold values from -0.1875 to 0.1875
- w_down: bfloat16 [4096, 1024], P(('fsdp', 'seq')), may hold values from -0.09375 to 0.09375
- attn_in_gain: bfloat16 [1024], P(('fsdp', 'seq')), may hold values from 0.5 to 1.5
- attn_in_bias: bfloat16 [1024], P(('fsdp', 'seq')), may hold values from -2 to 2
- attn_out_gain: bfloat16 [1024], P(('fsdp', 'seq')), may hold values from 0.5 to 1.5
- attn_out_bias: bfloat16 [1024], P(('fsdp', 'seq')), may hold values from -2 to 2
- mlp_in_gain: bfloat16 [1024], P(('fsdp', 'seq')), may hold values from 0.5 to 1.5
- mlp_in_bias: bfloat16 [1024], P(('fsdp', 'seq')), may hold values from -2 to 2
- mlp_out_gain: bfloat16 [1024], P(('fsdp', 'seq')), may hold values from 0.5 to 1.5
- mlp_out_bias: bfloat16 [1024], P(('fsdp', 'seq')), may hold values from -2 to 2
Outputs:
- block_out: bfloat16 [8, 2048, 1024], P('fsdp', 'seq')
- grad_tokens: bfloat16 [8, 2048, 1024], P('fsdp', 'seq')
- grad_query: float32 [1024, 1024], P(('fsdp', 'seq'))
- grad_key: float32 [1024, 1024], P(('fsdp', 'seq'))
- grad_value: float32 [1024, 1024], P(('fsdp', 'seq'))
- grad_output: float32 [1024, 1024], P(('fsdp', 'seq'))
- grad_up: float32 [1024, 4096], P(('fsdp', 'seq'))
- grad_down: float32 [4096, 1024], P(('fsdp', 'seq'))
- grad_attn_in_gain: float32 [1024], P(('fsdp', 'seq'))
- grad_attn_in_bias: float32 [1024], P(('fsdp', 'seq'))
- grad_attn_out_gain: float32 [1024], P(('fsdp', 'seq'))
- grad_attn_out_bias: float32 [1024], P(('fsdp', 'seq'))
- grad_mlp_in_gain: float32 [1024], P(('fsdp', 'seq'))
- grad_mlp_in_bias: float32 [1024], P(('fsdp', 'seq'))
- grad_mlp_out_gain: float32 [1024], P(('fsdp', 'seq'))
- grad_mlp_out_bias: float32 [1024], P(('fsdp', 'seq'))
All inputs are finite; a program needn't handle non-finite values.
Results may differ from a plain program's by a relative error of at most 0.015.
Values may be sent and summed in bfloat16 or wider, within the bound.
No kernel may reach another device: no remote copies, remote signals or barrier semaphores. Data moves between devices by JAX's collectives and lax.ppermute only.
A program may use at most 192 MiB of HBM per device.

v0:
```python
import math

import jax
import jax.numpy as jnp
from jax import lax
from jax.sharding import PartitionSpec as P

HEADS = 16
HEAD_DIM = 64


EPSILON = 1e-05
NEGATIVE = -1e30


def layer_norm(values, gain_vec, shift_vec):
    center = values - jnp.mean(values, axis=-1, keepdims=True)
    spread = jnp.mean(center * center, axis=-1, keepdims=True)
    return center * lax.rsqrt(spread + EPSILON) * gain_vec + shift_vec


def norm_backward(values, gain_vec, shift_vec, grad_out):
    unused, pullback = jax.vjp(layer_norm, values, gain_vec, shift_vec)
    return pullback(grad_out)


def rotary_tables(positions, head_size):
    frequency = jnp.exp(
        jnp.arange(head_size // 2, dtype=jnp.float32) * (-2.0 * math.log(10000.0) / head_size)
    )
    angles = positions.astype(jnp.float32)[:, None] * frequency[None, :]
    return (jnp.cos(angles)[:, None, :], jnp.sin(angles)[:, None, :])


def rotary(tensor, cosine, sine_tab):
    middle = tensor.shape[-1] // 2
    leading = tensor[..., :middle]
    trailing = tensor[..., middle:]
    return jnp.concatenate(
        [leading * cosine - trailing * sine_tab, trailing * cosine + leading * sine_tab], axis=-1
    )


def masked_scores(q_blk, key_rows, offset, factor):
    span_rows = q_blk.shape[0]
    scores = (
        jnp.einsum("qhd,khd->hqk", q_blk, key_rows, preferred_element_type=jnp.float32) * factor
    )
    key_pos = jnp.arange(key_rows.shape[0], dtype=jnp.int32)
    allowed = key_pos[None, :] <= (offset + jnp.arange(span_rows, dtype=jnp.int32))[:, None]
    return jnp.where(allowed[None], scores, NEGATIVE)


def attend_forward(query_rows, key_rows, value_rows, span_rows):
    length = key_rows.shape[0]
    factor = query_rows.shape[-1] ** (-0.5)

    def one_block(block_id):
        offset = block_id * span_rows
        q_blk = lax.dynamic_slice_in_dim(query_rows, offset, span_rows, 0)
        scores = masked_scores(q_blk, key_rows, offset, factor)
        maxima = jnp.max(scores, axis=-1, keepdims=True)
        exponent = jnp.exp(scores - maxima)
        totals = jnp.sum(exponent, axis=-1, keepdims=True)
        attn_prob = (exponent / totals).astype(jnp.bfloat16)
        result = jnp.einsum(
            "hqk,khd->qhd", attn_prob, value_rows, preferred_element_type=jnp.float32
        )
        return (result, (maxima + jnp.log(totals))[..., 0])

    results, log_sums = lax.map(one_block, jnp.arange(length // span_rows, dtype=jnp.int32))
    return (results.reshape(key_rows.shape), log_sums)


def attend_backward(query_rows, key_rows, value_rows, grad_rows, log_sums, span_rows):
    length = key_rows.shape[0]
    factor = query_rows.shape[-1] ** (-0.5)

    def one_block(running, block_id):
        key_acc, value_acc = running
        offset = block_id * span_rows
        q_blk = lax.dynamic_slice_in_dim(query_rows, offset, span_rows, 0)
        g_blk = lax.dynamic_slice_in_dim(grad_rows, offset, span_rows, 0)
        scores = masked_scores(q_blk, key_rows, offset, factor)
        attn_prob = jnp.exp(scores - log_sums[block_id][..., None])
        grad_prob = jnp.einsum(
            "qhd,khd->hqk", g_blk, value_rows, preferred_element_type=jnp.float32
        )
        inner = jnp.sum(attn_prob * grad_prob, axis=-1, keepdims=True)
        score_low = (attn_prob * (grad_prob - inner) * factor).astype(jnp.bfloat16)
        grad_q = jnp.einsum("hqk,khd->qhd", score_low, key_rows, preferred_element_type=jnp.float32)
        key_acc = key_acc + jnp.einsum(
            "hqk,qhd->khd", score_low, q_blk, preferred_element_type=jnp.float32
        )
        value_acc = value_acc + jnp.einsum(
            "hqk,qhd->khd",
            attn_prob.astype(jnp.bfloat16),
            g_blk,
            preferred_element_type=jnp.float32,
        )
        return ((key_acc, value_acc), grad_q)

    initial = jnp.zeros(key_rows.shape, jnp.float32)
    (grad_k, grad_v), grad_blocks = lax.scan(
        one_block, (initial, initial), jnp.arange(length // span_rows, dtype=jnp.int32)
    )
    return (grad_blocks.reshape(key_rows.shape), grad_k, grad_v)


def body(
    tokens,
    cotangent,
    w_query,
    w_key,
    w_value,
    w_output,
    w_up,
    w_down,
    attn_in_gain,
    attn_in_bias,
    attn_out_gain,
    attn_out_bias,
    mlp_in_gain,
    mlp_in_bias,
    mlp_out_gain,
    mlp_out_bias,
):
    seq_count, piece_len, model_width = tokens.shape
    groups = lax.axis_size("seq")
    length = piece_len * groups
    head_count = HEADS // groups
    span_rows = min(512, length)
    head_shape = (length, head_count, HEAD_DIM)
    attn_set = (
        lax.all_gather(w_query, ("fsdp", "seq"), axis=0, tiled=True),
        lax.all_gather(w_key, ("fsdp", "seq"), axis=0, tiled=True),
        lax.all_gather(w_value, ("fsdp", "seq"), axis=0, tiled=True),
        lax.all_gather(w_output, ("fsdp", "seq"), axis=0, tiled=True),
        lax.all_gather(attn_in_gain, ("fsdp", "seq"), axis=0, tiled=True),
        lax.all_gather(attn_in_bias, ("fsdp", "seq"), axis=0, tiled=True),
        lax.all_gather(attn_out_gain, ("fsdp", "seq"), axis=0, tiled=True),
        lax.all_gather(attn_out_bias, ("fsdp", "seq"), axis=0, tiled=True),
    )
    wq_full, wk_full, wv_full, wo_full = (attn_set[0], attn_set[1], attn_set[2], attn_set[3])
    gain_ai, bias_ai, gain_ao, bias_ao = [vector.astype(jnp.float32) for vector in attn_set[4:]]
    inputs = tokens.astype(jnp.float32)
    normed = layer_norm(inputs, gain_ai, bias_ai).astype(jnp.bfloat16)
    positions = lax.axis_index("seq") * piece_len + jnp.arange(piece_len, dtype=jnp.int32)
    cosine, sine_tab = rotary_tables(positions, HEAD_DIM)

    def project(weight):
        return jnp.einsum("spd,de->spe", normed, weight, preferred_element_type=jnp.float32)

    def turned(weight):
        split_heads = project(weight).reshape(seq_count, piece_len, HEADS, HEAD_DIM)
        return (
            rotary(split_heads, cosine, sine_tab)
            .reshape(seq_count, piece_len, model_width)
            .astype(jnp.bfloat16)
        )

    query_loc = turned(wq_full)
    key_loc = turned(wk_full)
    value_loc = project(wv_full).astype(jnp.bfloat16)
    query_heads, key_heads, value_heads = (
        lax.all_to_all(query_loc, "seq", split_axis=2, concat_axis=1, tiled=True),
        lax.all_to_all(key_loc, "seq", split_axis=2, concat_axis=1, tiled=True),
        lax.all_to_all(value_loc, "seq", split_axis=2, concat_axis=1, tiled=True),
    )
    attended = []
    log_table = []
    for member in range(seq_count):
        result, log_sums = attend_forward(
            query_heads[member].reshape(head_shape),
            key_heads[member].reshape(head_shape),
            value_heads[member].reshape(head_shape),
            span_rows,
        )
        attended.append(result.reshape(length, head_count * HEAD_DIM).astype(jnp.bfloat16))
        log_table.append(log_sums)
    attn_heads = jnp.stack(attended)
    attn_seq = lax.all_to_all(attn_heads, "seq", split_axis=1, concat_axis=2, tiled=True)
    projected = jnp.einsum("spe,ed->spd", attn_seq, wo_full, preferred_element_type=jnp.float32)
    residual = inputs + layer_norm(projected, gain_ao, bias_ao)
    mlp_set = (
        lax.all_gather(w_up, ("fsdp", "seq"), axis=0, tiled=True),
        lax.all_gather(w_down, ("fsdp", "seq"), axis=0, tiled=True),
        lax.all_gather(mlp_in_gain, ("fsdp", "seq"), axis=0, tiled=True),
        lax.all_gather(mlp_in_bias, ("fsdp", "seq"), axis=0, tiled=True),
        lax.all_gather(mlp_out_gain, ("fsdp", "seq"), axis=0, tiled=True),
        lax.all_gather(mlp_out_bias, ("fsdp", "seq"), axis=0, tiled=True),
    )
    wu_full, wd_full = (mlp_set[0], mlp_set[1])
    gain_mi, bias_mi, gain_mo, bias_mo = [vector.astype(jnp.float32) for vector in mlp_set[2:]]
    mlp_normed = layer_norm(residual, gain_mi, bias_mi).astype(jnp.bfloat16)
    pre_act = jnp.einsum("spd,df->spf", mlp_normed, wu_full, preferred_element_type=jnp.float32)
    activated = jax.nn.gelu(pre_act).astype(jnp.bfloat16)
    branch = jnp.einsum("spf,fd->spd", activated, wd_full, preferred_element_type=jnp.float32)
    block_out = (residual + layer_norm(branch, gain_mo, bias_mo)).astype(jnp.bfloat16)
    mlp_back = (
        lax.all_gather(w_up, ("fsdp", "seq"), axis=0, tiled=True),
        lax.all_gather(w_down, ("fsdp", "seq"), axis=0, tiled=True),
        lax.all_gather(mlp_in_gain, ("fsdp", "seq"), axis=0, tiled=True),
        lax.all_gather(mlp_in_bias, ("fsdp", "seq"), axis=0, tiled=True),
        lax.all_gather(mlp_out_gain, ("fsdp", "seq"), axis=0, tiled=True),
        lax.all_gather(mlp_out_bias, ("fsdp", "seq"), axis=0, tiled=True),
    )
    wu_back, wd_back = (mlp_back[0], mlp_back[1])
    gain_mi_b, bias_mi_b, gain_mo_b, bias_mo_b = [
        vector.astype(jnp.float32) for vector in mlp_back[2:]
    ]
    grad_in = cotangent.astype(jnp.float32)
    grad_branch, grad_mo_gain, grad_mo_bias = norm_backward(branch, gain_mo_b, bias_mo_b, grad_in)
    branch_low = grad_branch.astype(jnp.bfloat16)
    grad_down_full = jnp.einsum(
        "spf,spd->fd", activated, branch_low, preferred_element_type=jnp.float32
    )
    grad_act = jnp.einsum("spd,fd->spf", branch_low, wd_back, preferred_element_type=jnp.float32)
    unused, gelu_pull = jax.vjp(jax.nn.gelu, pre_act)
    pre_low = gelu_pull(grad_act)[0].astype(jnp.bfloat16)
    grad_up_full = jnp.einsum(
        "spd,spf->df", mlp_normed, pre_low, preferred_element_type=jnp.float32
    )
    grad_mlp_normed = jnp.einsum(
        "spf,df->spd", pre_low, wu_back, preferred_element_type=jnp.float32
    )
    grad_from_mlp, grad_mi_gain, grad_mi_bias = norm_backward(
        residual, gain_mi_b, bias_mi_b, grad_mlp_normed
    )
    grad_residual = grad_in + grad_from_mlp
    mlp_shards = (
        lax.psum_scatter(grad_up_full, ("fsdp", "seq"), scatter_dimension=0, tiled=True),
        lax.psum_scatter(grad_down_full, ("fsdp", "seq"), scatter_dimension=0, tiled=True),
        lax.psum_scatter(grad_mi_gain, ("fsdp", "seq"), scatter_dimension=0, tiled=True),
        lax.psum_scatter(grad_mi_bias, ("fsdp", "seq"), scatter_dimension=0, tiled=True),
        lax.psum_scatter(grad_mo_gain, ("fsdp", "seq"), scatter_dimension=0, tiled=True),
        lax.psum_scatter(grad_mo_bias, ("fsdp", "seq"), scatter_dimension=0, tiled=True),
    )
    attn_back = (
        lax.all_gather(w_query, ("fsdp", "seq"), axis=0, tiled=True),
        lax.all_gather(w_key, ("fsdp", "seq"), axis=0, tiled=True),
        lax.all_gather(w_value, ("fsdp", "seq"), axis=0, tiled=True),
        lax.all_gather(w_output, ("fsdp", "seq"), axis=0, tiled=True),
        lax.all_gather(attn_in_gain, ("fsdp", "seq"), axis=0, tiled=True),
        lax.all_gather(attn_in_bias, ("fsdp", "seq"), axis=0, tiled=True),
        lax.all_gather(attn_out_gain, ("fsdp", "seq"), axis=0, tiled=True),
        lax.all_gather(attn_out_bias, ("fsdp", "seq"), axis=0, tiled=True),
    )
    wq_back, wk_back, wv_back, wo_back = (attn_back[0], attn_back[1], attn_back[2], attn_back[3])
    gain_ai_b, bias_ai_b, gain_ao_b, bias_ao_b = [
        vector.astype(jnp.float32) for vector in attn_back[4:]
    ]
    grad_projected, grad_ao_gain, grad_ao_bias = norm_backward(
        projected, gain_ao_b, bias_ao_b, grad_residual
    )
    projected_low = grad_projected.astype(jnp.bfloat16)
    grad_output_full = jnp.einsum(
        "spe,spd->ed", attn_seq, projected_low, preferred_element_type=jnp.float32
    )
    attended_low = jnp.einsum(
        "spd,ed->spe", projected_low, wo_back, preferred_element_type=jnp.float32
    ).astype(jnp.bfloat16)
    grad_heads = lax.all_to_all(attended_low, "seq", split_axis=2, concat_axis=1, tiled=True)
    cosine_all, sine_all = rotary_tables(jnp.arange(length, dtype=jnp.int32), HEAD_DIM)
    query_grads = []
    key_grads = []
    value_grads = []
    for member in range(seq_count):
        grad_q, grad_k, grad_v = attend_backward(
            query_heads[member].reshape(head_shape),
            key_heads[member].reshape(head_shape),
            value_heads[member].reshape(head_shape),
            grad_heads[member].reshape(head_shape),
            log_table[member],
            span_rows,
        )
        query_grads.append(
            rotary(grad_q, cosine_all, -sine_all)
            .reshape(length, head_count * HEAD_DIM)
            .astype(jnp.bfloat16)
        )
        key_grads.append(
            rotary(grad_k, cosine_all, -sine_all)
            .reshape(length, head_count * HEAD_DIM)
            .astype(jnp.bfloat16)
        )
        value_grads.append(grad_v.reshape(length, head_count * HEAD_DIM).astype(jnp.bfloat16))
    query_seq, key_seq, value_seq = (
        lax.all_to_all(jnp.stack(query_grads), "seq", split_axis=1, concat_axis=2, tiled=True),
        lax.all_to_all(jnp.stack(key_grads), "seq", split_axis=1, concat_axis=2, tiled=True),
        lax.all_to_all(jnp.stack(value_grads), "seq", split_axis=1, concat_axis=2, tiled=True),
    )
    grad_query_full = jnp.einsum(
        "spd,spe->de", normed, query_seq, preferred_element_type=jnp.float32
    )
    grad_key_full = jnp.einsum("spd,spe->de", normed, key_seq, preferred_element_type=jnp.float32)
    grad_value_full = jnp.einsum(
        "spd,spe->de", normed, value_seq, preferred_element_type=jnp.float32
    )
    grad_normed = jnp.einsum("spe,de->spd", query_seq, wq_back, preferred_element_type=jnp.float32)
    grad_normed = grad_normed + jnp.einsum(
        "spe,de->spd", key_seq, wk_back, preferred_element_type=jnp.float32
    )
    grad_normed = grad_normed + jnp.einsum(
        "spe,de->spd", value_seq, wv_back, preferred_element_type=jnp.float32
    )
    grad_input, grad_ai_gain, grad_ai_bias = norm_backward(
        inputs, gain_ai_b, bias_ai_b, grad_normed
    )
    grad_tokens = (grad_residual + grad_input).astype(jnp.bfloat16)
    attn_shards = (
        lax.psum_scatter(grad_query_full, ("fsdp", "seq"), scatter_dimension=0, tiled=True),
        lax.psum_scatter(grad_key_full, ("fsdp", "seq"), scatter_dimension=0, tiled=True),
        lax.psum_scatter(grad_value_full, ("fsdp", "seq"), scatter_dimension=0, tiled=True),
        lax.psum_scatter(grad_output_full, ("fsdp", "seq"), scatter_dimension=0, tiled=True),
        lax.psum_scatter(grad_ai_gain, ("fsdp", "seq"), scatter_dimension=0, tiled=True),
        lax.psum_scatter(grad_ai_bias, ("fsdp", "seq"), scatter_dimension=0, tiled=True),
        lax.psum_scatter(grad_ao_gain, ("fsdp", "seq"), scatter_dimension=0, tiled=True),
        lax.psum_scatter(grad_ao_bias, ("fsdp", "seq"), scatter_dimension=0, tiled=True),
    )
    return (
        block_out,
        grad_tokens,
        attn_shards[0],
        attn_shards[1],
        attn_shards[2],
        attn_shards[3],
        mlp_shards[0],
        mlp_shards[1],
        attn_shards[4],
        attn_shards[5],
        attn_shards[6],
        attn_shards[7],
        mlp_shards[2],
        mlp_shards[3],
        mlp_shards[4],
        mlp_shards[5],
    )


def solution(mesh):
    return jax.shard_map(
        body,
        mesh=mesh,
        in_specs=(
            P("fsdp", "seq", None),
            P("fsdp", "seq", None),
            P(("fsdp", "seq"), None),
            P(("fsdp", "seq"), None),
            P(("fsdp", "seq"), None),
            P(("fsdp", "seq"), None),
            P(("fsdp", "seq"), None),
            P(("fsdp", "seq"), None),
            P(("fsdp", "seq")),
            P(("fsdp", "seq")),
            P(("fsdp", "seq")),
            P(("fsdp", "seq")),
            P(("fsdp", "seq")),
            P(("fsdp", "seq")),
            P(("fsdp", "seq")),
            P(("fsdp", "seq")),
        ),
        out_specs=(
            P("fsdp", "seq", None),
            P("fsdp", "seq", None),
            P(("fsdp", "seq"), None),
            P(("fsdp", "seq"), None),
            P(("fsdp", "seq"), None),
            P(("fsdp", "seq"), None),
            P(("fsdp", "seq"), None),
            P(("fsdp", "seq"), None),
            P(("fsdp", "seq")),
            P(("fsdp", "seq")),
            P(("fsdp", "seq")),
            P(("fsdp", "seq")),
            P(("fsdp", "seq")),
            P(("fsdp", "seq")),
            P(("fsdp", "seq")),
            P(("fsdp", "seq")),
        ),
        check_vma=False,
    )
```

profile of v0, /device:TPU:1, one launch (start us, length us, event | category | flops | bytes accessed | tf_op | source)
XLA Modules:
  0.0 2165.6 jit_solution(5647619602144988988)
XLA Ops:
  17.3 42.3 %all-reduce.17 = (bf16[1024]{0:T(1024)(128)(2,1)S(1)}, bf16[1024]{0:T(1024)(128)(2,1)S(1)}, bf16[1024]{0:T(1024)(128)(2,1)}, bf16[1024]{0:T(1024)(128)(2,1)}, bf...) all-reduce(bf16[1024]{0:T(1024)(128)(2,1)S(1)} %dynamic-update-slic, ...), channel_id=1, replica_groups=mesh['fsdp'=4,'seq'=8] {'fsdp','seq'}, use_global_device_ids=true, to_apply=%add.1 | all-reduce | flops 8192 | bytes 32768
  73.2 55.4 %all-gather.7.cloned.1.call-done = bf16[1024,1024]{1,0:T(8,128)(2,1)} async-done(((bf16[32,1024]{1,0:T(8,128)(2,1)}), bf16[1024,1024]{1,0:T(8,128)(2,1)}) %all-gather.7.cloned.1.call-update) | async-done | bytes 2097168 | tf_op jit(solution)/shard_map/all_gather | solution.py:135
  140.7 25.6 %all-to-all-done = bf16[2,256,1024]{1,0,2:T(2,128)(2,1)S(1)} async-done(((bf16[2,256,1024]{1,0,2:T(2,128)(2,1)}), bf16[2,256,1024]{1,0,2:T(2,128)(2,1)S(1)}, u32[]{:S(2)}, u32[]{:S(2)}) %all-to-all-start) | async-done | bytes 1048608 | tf_op jit(solution)/shard_map/all_to_all | solution.py:166
  170.6 31.4 %all-gather.11.cloned.1.call-done = bf16[1024,1024]{1,0:T(8,128)(2,1)} async-done(((bf16[32,1024]{1,0:T(8,128)(2,1)}), bf16[1024,1024]{1,0:T(8,128)(2,1)}) %all-gather.11.cloned.1.call-update) | async-done | bytes 2097168 | tf_op jit(solution)/shard_map/all_gather | solution.py:137
  217.5 24.1 %all-to-all-done.2 = bf16[2,256,1024]{1,0,2:T(2,128)(2,1)S(1)} async-done(((bf16[2,256,1024]{1,0,2:T(2,128)(2,1)}), bf16[2,256,1024]{1,0,2:T(2,128)(2,1)S(1)}, u32[]{:S(2)}, u32[]{:S(2)}) %all-to-all-start.2) | async-done | bytes 1048608 | tf_op jit(solution)/shard_map/all_to_all | solution.py:168
  244.8 43.3 %while.55 = (s32[]{:T(128)}, bf16[4,512,2,64]{1,3,2,0:T(8,128)(2,1)}, f32[4,2,512]{2,1,0:T(2,128)S(1)}, s32[4]{0:T(128)S(1)}, bf16[2048,2,64]{0,2,1:T(8,128)(2,1...) while((s32[]{:T(128)}, ...), condition=%wide.region_9.10_spmd, body=%wide.region_6.9_spmd.sunk | while | flops 563084800 | bytes 35033332 | solution.py:71
  295.6 42.9 %while.54 = (s32[]{:T(128)}, bf16[4,512,2,64]{1,3,2,0:T(8,128)(2,1)S(1)}, f32[4,2,512]{2,1,0:T(2,128)}, s32[4]{0:T(128)S(1)}, bf16[2048,2,64]{0,2,1:T(8,128)(2,1...) while((s32[]{:T(128)}, ...), condition=%wide.region_5.6_spmd, body=%wide.region_2.5_spmd.sunk | while | flops 563084800 | bytes 30838976 | solution.py:71
  346.1 30.5 %all-to-all-done.3 = bf16[2,2048,128]{2,0,1:T(2,128)(2,1)S(1)} async-done(((bf16[2,2048,128]{2,0,1:T(2,128)(2,1)}), bf16[2,2048,128]{2,0,1:T(2,128)(2,1)S(1)}, u32[]{:S(2)}, u32[]{:S(2)}) %all-to-all-start.3) | async-done | bytes 1048608 | tf_op jit(solution)/shard_map/all_to_all | solution.py:182
  393.8 37.5 %all-gather.17.cloned.1.call-done = bf16[4096,1024]{1,0:T(8,128)(2,1)} async-done(((bf16[128,1024]{1,0:T(8,128)(2,1)}), bf16[4096,1024]{1,0:T(8,128)(2,1)}) %all-gather.17.cloned.1.call-update) | async-done | bytes 8388624 | tf_op jit(solution)/shard_map/all_gather | solution.py:187
  486.0 22.1 %all-to-all-done.4 = bf16[2,256,1024]{1,0,2:T(2,128)(2,1)S(1)} async-done(((bf16[2,256,1024]{1,0,2:T(2,128)(2,1)}), bf16[2,256,1024]{1,0,2:T(2,128)(2,1)S(1)}, u32[]{:S(2)}, u32[]{:S(2)}) %all-to-all-start.4) | async-done | bytes 1048608 | tf_op jit(solution)/shard_map/all_to_all | solution.py:263
  512.2 218.1 %while.57 = (s32[]{:T(128)}, f32[2048,2,64]{0,2,1:T(8,128)}, f32[2048,2,64]{0,2,1:T(8,128)}, f32[4,512,2,64]{1,0,3,2:T(4,128)S(1)}, s32[4]{0:T(128)S(1)}, /*inde...) while((s32[]{:T(128)}, f32[2048,2,64]{0,2,1:T(8,128)}, ...), condition=%wide.region_27.28_spmd.clone, body=%wide.region_25.27_spmd.clone.sunk | while | flops 1398807040 | bytes 88371472 | solution.py:104
  582.1 15.5 fusion.341
  636.8 15.4 fusion.341
  691.3 15.4 fusion.341
  733.7 218.4 %while.56 = (s32[]{:T(128)}, f32[2048,2,64]{0,2,1:T(8,128)}, f32[2048,2,64]{0,2,1:T(8,128)}, f32[4,512,2,64]{1,0,3,2:T(4,128)S(1)}, s32[4]{0:T(128)S(1)}, /*inde...) while((s32[]{:T(128)}, f32[2048,2,64]{0,2,1:T(8,128)}, ...), condition=%wide.region_24.25_spmd.clone, body=%wide.region_22.24_spmd.clone.sunk | while | flops 1398807040 | bytes 88371472 | solution.py:104
  803.6 15.4 fusion.326
  961.7 29.4 %all_to_all.132 = bf16[2,2048,128]{2,0,1:T(2,128)(2,1)S(1)} all-to-all(bf16[2,2048,128]{2,0,1:T(2,128)(2,1)S(1)} %pad_maximum_fusion.3), channel_id=1, replica_groups=mesh['fsdp'=4,'seq'=8] {'seq'}, dimensions={1} | all-to-all | bytes 2097152 | tf_op jit(solution)/shard_map/all_to_all | solution.py:289
  1003.2 37.9 %all_to_all.133 = bf16[2,2048,128]{2,0,1:T(2,128)(2,1)S(1)} all-to-all(bf16[2,2048,128]{2,0,1:T(2,128)(2,1)S(1)} %pad_maximum_fusion.4), channel_id=1, replica_groups=mesh['fsdp'=4,'seq'=8] {'seq'}, dimensions={1} | all-to-all | bytes 2097152 | tf_op jit(solution)/shard_map/all_to_all | solution.py:290
  1048.2 34.4 %all_to_all.134 = bf16[2,2048,128]{2,0,1:T(2,128)(2,1)S(1)} all-to-all(bf16[2,2048,128]{2,0,1:T(2,128)(2,1)S(1)} %copy.131), channel_id=1, replica_groups=mesh['fsdp'=4,'seq'=8] {'seq'}, dimensions={1} | all-to-all | bytes 2097152 | tf_op jit(solution)/shard_map/all_to_all | solution.py:291
  1125.8 43.7 %all-reduce.16 = (f32[1024]{0:T(1024)S(1)}, f32[1024]{0:T(1024)S(1)}, f32[1024]{0:T(1024)S(1)}, f32[1024]{0:T(1024)S(1)}, f32[1024]{0:T(1024)S(1)}, /*index=5*/f...) all-reduce(f32[1024]{0:T(1024)S(1)} %get-tuple-element.282, ...), channel_id=8, replica_groups=mesh['fsdp'=4,'seq'=8] {'fsdp','seq'}, use_global_device_ids=true, to_apply=%region_37.38.clone | all-reduce | flops 8192 | bytes 65536
  1177.5 111.8 %reduce-scatter.9.cloned.1.call-done = f32[32,1024]{1,0:T(8,128)} async-done(((f32[1024,1024]{1,0:T(8,128)}), f32[32,1024]{1,0:T(8,128)}) %reduce-scatter.9.cloned.1.call-update) | async-done | bytes 131088 | tf_op jit(solution)/shard_map/reduce_scatter | solution.py:313
  1289.3 146.0 %reduce-scatter.11.cloned.1.call-done = f32[32,1024]{1,0:T(8,128)} async-done(((f32[1024,1024]{1,0:T(8,128)}), f32[32,1024]{1,0:T(8,128)}) %reduce-scatter.11.cloned.1.call-update) | async-done | bytes 131088 | tf_op jit(solution)/shard_map/reduce_scatter | solution.py:314
  1435.2 363.0 %reduce-scatter.15.cloned.1.call-done = f32[32,4096]{1,0:T(8,128)} async-done(((f32[1024,4096]{1,0:T(8,128)}), f32[32,4096]{1,0:T(8,128)}) %reduce-scatter.15.cloned.1.call-update) | async-done | bytes 524304 | tf_op jit(solution)/shard_map/reduce_scatter | solution.py:232
  1798.3 360.1 %reduce-scatter.17.cloned.1.call-done = f32[128,1024]{1,0:T(8,128)} async-done(((f32[4096,1024]{1,0:T(8,128)}), f32[128,1024]{1,0:T(8,128)}) %reduce-scatter.17.cloned.1.call-update) | async-done | bytes 524304 | tf_op jit(solution)/shard_map/reduce_scatter | solution.py:233
  (502 shorter events, 665.0 us)
Async XLA Ops:
  7.2 63.0 %all-gather.9.cloned.1.call-start = ((), (), s32[]{:S(2)}) async-start(), calls=%async_computation.15 | async-start | bytes 2162688 | tf_op jit(solution)/shard_map/all_gather | solution.py:136
  7.9 120.7 %all-gather.7.cloned.1.call-start = ((), (), s32[]{:S(2)}) async-start(), calls=%async_computation.14 | async-start | bytes 2162688 | tf_op jit(solution)/shard_map/all_gather | solution.py:135
  8.7 193.3 %all-gather.11.cloned.1.call-start = ((), (), s32[]{:S(2)}) async-start(), calls=%async_computation.16 | async-start | bytes 2162688 | tf_op jit(solution)/shard_map/all_gather | solution.py:137
  9.4 367.4 %all-gather.13.cloned.1.call-start = ((), (), s32[]{:S(2)}) async-start(), calls=%async_computation.17 | async-start | bytes 2162688 | tf_op jit(solution)/shard_map/all_gather | solution.py:138
  10.0 373.2 %all-gather.15.cloned.1.call-start = ((), (), s32[]{:S(2)}) async-start(), calls=%async_computation.18 | async-start | bytes 8650752 | tf_op jit(solution)/shard_map/all_gather | solution.py:186
  59.6 142.3 %copy-start.63 = (f32[1024]{0:T(1024)}, f32[1024]{0:T(1024)S(1)}, u32[]{:S(2)}) copy-start(f32[1024]{0:T(1024)S(1)} %convert_element_type.232) | copy-start | bytes 12292
  59.6 142.3 %copy-start.43 = (f32[1024]{0:T(1024)}, f32[1024]{0:T(1024)S(1)}, u32[]{:S(2)}) copy-start(f32[1024]{0:T(1024)S(1)} %convert_element_type.231) | copy-start | bytes 12292
  61.1 140.8 %copy-start.46 = (f32[2,256]{1,0:T(2,128)}, f32[2,256]{1,0:T(2,128)S(1)}, u32[]{:S(2)}) copy-start(f32[2,256]{1,0:T(2,128)S(1)} %broadcast_multiply_fusion.3) | copy-start | bytes 6148
  61.6 140.4 %copy-start.52 = (f32[2,256]{1,0:T(2,128)}, f32[2,256]{1,0:T(2,128)S(1)}, u32[]{:S(2)}) copy-start(f32[2,256]{1,0:T(2,128)S(1)} %fusion.230) | copy-start | bytes 6148
  134.6 31.7 %all-to-all-start = ((bf16[2,256,1024]{1,0,2:T(2,128)(2,1)}), bf16[2,256,1024]{1,0,2:T(2,128)(2,1)S(1)}, u32[]{:S(2)}, u32[]{:S(2)}) async-start(bf16[2,256,1024]{1,0,2:T(2,128)(2,1)} %copy.101), calls=%async_computation | async-start | bytes 2097152 | tf_op jit(solution)/shard_map/all_to_all | solution.py:166
  166.3 43.2 %all-to-all-start.1 = ((bf16[2,256,1024]{1,0,2:T(2,128)(2,1)}), bf16[2,256,1024]{1,0,2:T(2,128)(2,1)S(1)}, u32[]{:S(2)}, u32[]{:S(2)}) async-start(bf16[2,256,1024]{1,0,2:T(2,128)(2,1)} %copy.105), calls=%async_computation.1 | async-start | bytes 2097152 | tf_op jit(solution)/shard_map/all_to_all | solution.py:167
  209.5 32.1 %all-to-all-start.2 = ((bf16[2,256,1024]{1,0,2:T(2,128)(2,1)}), bf16[2,256,1024]{1,0,2:T(2,128)(2,1)S(1)}, u32[]{:S(2)}, u32[]{:S(2)}) async-start(bf16[2,256,1024]{1,0,2:T(2,128)(2,1)} %copy.108), calls=%async_computation.2 | async-start | bytes 2097152 | tf_op jit(solution)/shard_map/all_to_all | solution.py:168
  213.0 218.2 %all-gather.17.cloned.1.call-start = ((), (), s32[]{:S(2)}) async-start(), calls=%async_computation.19 | async-start | bytes 8650752 | tf_op jit(solution)/shard_map/all_gather | solution.py:187
  342.0 34.6 %all-to-all-start.3 = ((bf16[2,2048,128]{2,0,1:T(2,128)(2,1)}), bf16[2,2048,128]{2,0,1:T(2,128)(2,1)S(1)}, u32[]{:S(2)}, u32[]{:S(2)}) async-start(bf16[2,2048,128]{2,0,1:T(2,128)(2,1)} %copy.115), calls=%async_computation.3 | async-start | bytes 2097152 | tf_op jit(solution)/shard_map/all_to_all | solution.py:182
  346.1 121.4 %copy-start.48 = (f32[1024]{0:T(1024)}, f32[1024]{0:T(1024)S(1)}, u32[]{:S(2)}) copy-start(f32[1024]{0:T(1024)S(1)} %convert_element_type.244) | copy-start | bytes 12292
  382.8 84.7 %copy-start = (f32[2,256,1024]{2,1,0:T(8,128)}, f32[2,256,1024]{2,1,0:T(8,128)S(1)}, u32[]{:S(2)}) copy-start(f32[2,256,1024]{2,1,0:T(8,128)S(1)} %get-tuple-element.380) | copy-start | bytes 6291460
  382.8 84.7 %copy-start.50 = (f32[2,256]{1,0:T(2,128)}, f32[2,256]{1,0:T(2,128)S(1)}, u32[]{:S(2)}) copy-start(f32[2,256]{1,0:T(2,128)S(1)} %broadcast_multiply_fusion.1) | copy-start | bytes 6148
  475.7 32.4 %all-to-all-start.4 = ((bf16[2,256,1024]{1,0,2:T(2,128)(2,1)}), bf16[2,256,1024]{1,0,2:T(2,128)(2,1)S(1)}, u32[]{:S(2)}, u32[]{:S(2)}) async-start(bf16[2,256,1024]{1,0,2:T(2,128)(2,1)} %copy.118), calls=%async_computation.4 | async-start | bytes 2097152 | tf_op jit(solution)/shard_map/all_to_all | solution.py:263
  479.5 698.0 %reduce-scatter.13.cloned.1.call-start = ((), (), s32[]{:S(2)}) async-start(), calls=%async_computation.23 | async-start | bytes 4325376 | tf_op jit(solution)/shard_map/reduce_scatter | solution.py:315
  485.9 691.5 %reduce-scatter.7.cloned.1.call-start = ((), (), s32[]{:S(2)}) async-start(), calls=%async_computation.20 | async-start | bytes 4325376 | tf_op jit(solution)/shard_map/reduce_scatter | solution.py:312
  995.8 293.5 %reduce-scatter.9.cloned.1.call-start = ((), (), s32[]{:S(2)}) async-start(), calls=%async_computation.21 | async-start | bytes 4325376 | tf_op jit(solution)/shard_map/reduce_scatter | solution.py:313
  1045.7 389.5 %reduce-scatter.11.cloned.1.call-start = ((), (), s32[]{:S(2)}) async-start(), calls=%async_computation.22 | async-start | bytes 4325376 | tf_op jit(solution)/shard_map/reduce_scatter | solution.py:314
  1087.3 711.0 %reduce-scatter.15.cloned.1.call-start = ((), (), s32[]{:S(2)}) async-start(), calls=%async_computation.24 | async-start | bytes 17301504 | tf_op jit(solution)/shard_map/reduce_scatter | solution.py:232
  1099.4 1059.0 %reduce-scatter.17.cloned.1.call-start = ((), (), s32[]{:S(2)}) async-start(), calls=%async_computation.25 | async-start | bytes 17301504 | tf_op jit(solution)/shard_map/reduce_scatter | solution.py:233
  (80 other events, 619.6 us)
Sparse Core Ops, SparseCore 0:
  11.0 59.1 all-gather.8
  73.1 55.4 all-gather.6
  131.6 70.3 all-gather.10
  204.8 61.3 all-gather.12
  269.0 76.3 all-gather.14
  348.2 83.0 all-gather.16
  486.1 139.2 reduce-scatter.12
  995.9 147.3 reduce-scatter.6
  1146.1 143.1 reduce-scatter.8
  1292.0 143.2 reduce-scatter.10
  1438.1 360.0 reduce-scatter.14
  1801.0 357.3 reduce-scatter.16
where the time goes:
time: 2180 us; the launch traced here: 2170 us
  waiting for transfers between devices  1220 us (56%)
  matrix products  521 us (24%)
  blocking collectives  188 us (9%)
  local copies, waits for them, and re-layouts  109 us (5%)
  other arithmetic  64.3 us (3%)
  loops' own time  28 us (1%)
    reduce_scatter x1, waiting for transfers between devices, body(): lax.psum_scatter(grad_up_full, ('fsdp', 'seq'), scatter_dimension=0, tile...  363 us
    reduce_scatter x1, waiting for transfers between devices, body(): lax.psum_scatter(grad_down_full, ('fsdp', 'seq'), scatter_dimension=0, ti...  360 us
    reduce_scatter x1, waiting for transfers between devices, body(): lax.psum_scatter(grad_value_full, ('fsdp', 'seq'), scatter_dimension=0, t...  146 us
    dot_general x8, matrix products, one_block(): jnp.einsum('hqk,qhd->khd', score_low, q_blk, preferred_element_type=jnp.f...  123 us
    reduce_scatter x1, waiting for transfers between devices, body(): lax.psum_scatter(grad_key_full, ('fsdp', 'seq'), scatter_dimension=0, til...  112 us
    dot_general x8, matrix products, one_block(): jnp.einsum('hqk,khd->qhd', score_low, key_rows, preferred_element_type=jn...  109 us
    unnamed x2, blocking collectives  86 us
    dot_general x16, matrix products, masked_scores(): jnp.einsum('qhd,khd->hqk', q_blk, key_rows, preferred_element_type=jnp.fl...  66.4 us
  transfers between devices with their start and end apart: 17, of which 12 were waited for; matrix products, arithmetic and copies ran while one was open for 29% of the time, Pallas kernels for 0%

commit v1 on v0

v1 whole, which is shorter than its diff:
```python
import functools
import math

import jax
import jax.numpy as jnp
from jax import lax
from jax.experimental import pallas as pl
from jax.experimental.pallas import tpu as pltpu
from jax.sharding import Mesh
from jax.sharding import PartitionSpec as P

HEADS = 16
HEAD_DIM = 64
EPSILON = 1e-05
NEGATIVE = -1e30
LOG2E = math.log2(math.e)
AXES = ("j", "h", "c", "a", "b")
BF = jnp.bfloat16
F32 = jnp.float32
NT = (((1,), (1,)), ((), ()))
NN = (((1,), (0,)), ((), ()))
TN = (((0,), (0,)), ((), ()))


def cost(us):
    return pl.CostEstimate(flops=int(us * 1e6), bytes_accessed=1 << 10, transcendentals=0)


def dot(left, right, dims=NN):
    return lax.dot_general(left, right, dims, preferred_element_type=F32)


def qkv_kernel(table, *refs, pieces):
    x_refs = refs[:pieces]
    w_ref, vec_ref, cos_ref, sin_ref, n_ref, q_ref, k_ref, v_ref, held = refs[pieces:]
    step = pl.program_id(0)
    for n in range(pieces):

        @pl.when(step == n)
        def _(n=n):
            held[...] = x_refs[n][...]

    x = held[...].astype(F32)
    center = x - jnp.mean(x, axis=1, keepdims=True)
    rstd = lax.rsqrt(jnp.mean(center * center, axis=1, keepdims=True) + EPSILON)
    normed = (center * rstd * vec_ref[0:1] + vec_ref[1:2]).astype(BF)
    n_ref[...] = normed
    full = dot(normed, w_ref[...])
    lane = lax.broadcasted_iota(jnp.int32, (1, 128), 1)
    first = (lane % HEAD_DIM) < HEAD_DIM // 2
    cosine, sine = cos_ref[...], sin_ref[...]
    for pair in range(q_ref.shape[1] // 128):
        at = slice(pair * 128, (pair + 1) * 128)
        for which, out, scale in ((0, q_ref, LOG2E * HEAD_DIM**-0.5), (1, k_ref, 1.0)):
            t = full[:, (3 * pair + which) * 128 : (3 * pair + which + 1) * 128]
            other = jnp.where(first, pltpu.roll(t, 96, 1), pltpu.roll(t, 32, 1))
            out[:, at] = ((t * cosine + other * sine) * scale).astype(BF)
        v_ref[:, at] = full[:, (3 * pair + 2) * 128 : (3 * pair + 3) * 128].astype(BF)


def qkv_call(table, pieces, w, vec, cosine, sine):
    blocks = len(pieces)
    rows, model = pieces[0].shape
    width = w.shape[1] // 3
    length = blocks * rows
    at = lambda i, t: (t[i], 0)
    fixed = lambda i, t: (0, 0)
    return pl.pallas_call(
        functools.partial(qkv_kernel, pieces=blocks),
        out_shape=[jax.ShapeDtypeStruct((length, model), BF)]
        + [jax.ShapeDtypeStruct((length, width), BF)] * 3,
        grid_spec=pltpu.PrefetchScalarGridSpec(
            num_scalar_prefetch=1,
            grid=(blocks,),
            in_specs=[pl.BlockSpec((rows, model), fixed)] * blocks
            + [
                pl.BlockSpec(w.shape, fixed),
                pl.BlockSpec(vec.shape, fixed),
                pl.BlockSpec((rows, 128), at),
                pl.BlockSpec((rows, 128), at),
            ],
            out_specs=[pl.BlockSpec((rows, model), at)] + [pl.BlockSpec((rows, width), at)] * 3,
            scratch_shapes=[pltpu.VMEM((rows, model), BF)],
        ),
        compiler_params=pltpu.CompilerParams(
            dimension_semantics=("arbitrary",), vmem_limit_bytes=48 << 20
        ),
        cost_estimate=cost(11),
        name="qkv",
    )(table, *pieces, w, vec, cosine, sine)


def forward_kernel(table, q_ref, k_ref, v_ref, o_ref, lse_ref, vaug, *, bq, bk, rows):
    i = pl.program_id(1)
    lane = lax.broadcasted_iota(jnp.int32, (1, 128), 1)
    low = lane < HEAD_DIM

    @pl.when(i == 0)
    def _():
        v = v_ref[...]
        one = jnp.ones_like(v)
        vaug[0] = jnp.where(low, v, one)
        vaug[1] = jnp.where(low, one, v)

    q = q_ref[...]
    zero = jnp.zeros_like(q)
    heads = (jnp.where(low, q, zero), jnp.where(low, zero, q))

    def step(kb, carry, masked):
        start = pl.multiple_of(kb * bk, bk)
        k_blk = k_ref[pl.ds(start, bk), :]
        out = []
        for h in range(2):
            top, acc = carry[h]
            s = dot(heads[h], k_blk, NT)
            if masked:
                row = lax.broadcasted_iota(jnp.int32, s.shape, 0) + i * bq
                col = lax.broadcasted_iota(jnp.int32, s.shape, 1) + start
                s = jnp.where(col <= row, s, NEGATIVE)
            new = jnp.maximum(top, jnp.max(s, axis=1, keepdims=True))
            p = jnp.exp2(s - new)
            acc = acc * jnp.exp2(top - new) + dot(p.astype(BF), vaug[h, pl.ds(start, bk), :])
            out.append((new, acc))
        return tuple(out)

    init = tuple(
        (jnp.full((bq, 1), NEGATIVE, F32), jnp.zeros((bq, 128), F32)) for _ in range(2)
    )
    full = (i * bq) // bk
    carry = lax.fori_loop(0, full, lambda kb, c: step(kb, c, False), init)
    for d in range(bq // bk):
        carry = step(full + d, carry, True)
    (top0, acc0), (top1, acc1) = carry
    total = pltpu.roll(jnp.where(low, acc1, acc0), HEAD_DIM, 1)
    o = (jnp.where(low, acc0, acc1) / total).astype(BF)
    for d in range(bq // rows):
        o_ref[table[i * (bq // rows) + d]] = o[d * rows : (d + 1) * rows]
    lse_ref[...] = jnp.where(low, top0, top1) + jnp.log2(total)


def attention_forward(table, q, k, v, rows):
    length, width = q.shape
    bq, bk = min(1024, length), min(512, length)
    blocks = length // rows
    return pl.pallas_call(
        functools.partial(forward_kernel, bq=bq, bk=bk, rows=rows),
        out_shape=[
            jax.ShapeDtypeStruct((blocks, rows, width), BF),
            jax.ShapeDtypeStruct((length, width), F32),
        ],
        grid_spec=pltpu.PrefetchScalarGridSpec(
            num_scalar_prefetch=1,
            grid=(width // 128, length // bq),
            in_specs=[
                pl.BlockSpec((bq, 128), lambda p, i, t: (i, p)),
                pl.BlockSpec((length, 128), lambda p, i, t: (0, p)),
                pl.BlockSpec((length, 128), lambda p, i, t: (0, p)),
            ],
            out_specs=[
                pl.BlockSpec((blocks, rows, 128), lambda p, i, t: (0, 0, p)),
                pl.BlockSpec((bq, 128), lambda p, i, t: (i, p)),
            ],
            scratch_shapes=[pltpu.VMEM((2, length, 128), BF)],
        ),
        compiler_params=pltpu.CompilerParams(
            dimension_semantics=("arbitrary", "arbitrary"), vmem_limit_bytes=48 << 20
        ),
        cost_estimate=cost(23),
        name="attention_forward",
    )(table, q, k, v)


def split3(x):
    high = x.astype(BF)
    rest = x - high.astype(F32)
    mid = rest.astype(BF)
    return high, mid, (rest - mid.astype(F32)).astype(BF)


def backward_kernel(
    table, q_ref, k_ref, v_ref, o_ref, do_ref, lse_ref, cos_ref, sin_ref, ck_ref, sk_ref,
    d_ref, qa, da, dqt, *, bq, bk, rows
):
    j = pl.program_id(0)
    length = q_ref.shape[0]
    lane = lax.broadcasted_iota(jnp.int32, (1, 128), 1)
    low = lane < HEAD_DIM
    first = (lane % HEAD_DIM) < HEAD_DIM // 2

    def unturn(t, cosine, sine):
        other = jnp.where(first, pltpu.roll(t, 96, 1), pltpu.roll(t, 32, 1))
        return t * cosine - other * sine

    @pl.when(j == 0)
    def _():
        dqt[...] = jnp.zeros_like(dqt)

        def prep(b, _):
            r = pl.ds(pl.multiple_of(b * rows, rows), rows)
            q, do = q_ref[r, :], do_ref[table[b]]
            product = o_ref[table[b]].astype(F32) * do.astype(F32)
            for h in range(2):
                mine = low if h == 0 else jnp.logical_not(low)
                base = HEAD_DIM if h == 0 else 0
                delta = -jnp.sum(jnp.where(mine, product, 0.0), axis=1, keepdims=True)
                lse = -lse_ref[r, HEAD_DIM * h : HEAD_DIM * h + 1]
                for source, value, target in ((q, lse, qa), (do, delta, da)):
                    x = jnp.where(mine, source, jnp.zeros_like(source))
                    for n, part in enumerate(split3(value)):
                        x = jnp.where(lane == base + n, part, x)
                    target[h, r, :] = x
            return 0

        lax.fori_loop(0, length // rows, prep, 0)

    k, v = k_ref[...], v_ref[...]
    one, zero = jnp.ones_like(k), jnp.zeros_like(k)
    ka, va, kt = [], [], []
    for h in range(2):
        mine = low if h == 0 else jnp.logical_not(low)
        base = HEAD_DIM if h == 0 else 0
        extra = jnp.where(jnp.logical_and(lane >= base, lane < base + 3), one, zero)
        ka.append(jnp.where(mine, k, extra))
        va.append(jnp.where(mine, v, extra))
        kt.append(jnp.where(mine, k, zero).T)

    def step(qb, carry, masked):
        start = pl.multiple_of(qb * bq, bq)
        r = pl.ds(start, bq)
        out, low_scores = [], []
        for h in range(2):
            dk, dv = carry[h]
            qh, dh = qa[h, r, :], da[h, r, :]
            st = dot(ka[h], qh, NT)
            if masked:
                key = lax.broadcasted_iota(jnp.int32, st.shape, 0) + j * bk
                query = lax.broadcasted_iota(jnp.int32, st.shape, 1) + start
                st = jnp.where(key <= query, st, NEGATIVE)
            p = jnp.exp2(st)
            ds = (p * dot(va[h], dh, NT)).astype(BF)
            out.append((dk + dot(ds, qh), dv + dot(p.astype(BF), dh)))
            low_scores.append(ds)
        dqt[:, r] += dot(kt[0], low_scores[0]) + dot(kt[1], low_scores[1])
        return tuple(out)

    z = jnp.zeros((bk, 128), F32)
    carry = ((z, z), (z, z))
    begin, diagonal = (j * bk) // bq, max(bk // bq, 1)
    for d in range(diagonal):
        carry = step(begin + d, carry, True)
    carry = lax.fori_loop(
        begin + diagonal, length // bq, lambda qb, c: step(qb, c, False), carry
    )
    (dk0, dv0), (dk1, dv1) = carry
    dk = unturn(jnp.where(low, dk0, dk1) * (1.0 / LOG2E), ck_ref[...], sk_ref[...])
    mine = pl.ds(pl.multiple_of(j * bk, bk), bk)
    d_ref[mine, 128:256] = dk.astype(BF)
    d_ref[mine, 256:384] = jnp.where(low, dv0, dv1).astype(BF)

    @pl.when(j == pl.num_programs(0) - 1)
    def _():
        dq = dqt[...].T * HEAD_DIM**-0.5
        d_ref[:, 0:128] = unturn(dq, cos_ref[...], sin_ref[...]).astype(BF)


def attention_backward(table, pair, q, k, v, o, do, lse, cosine, sine):
    length = q.shape[0]
    blocks, rows, _ = o.shape
    bq, bk = min(512, length), min(512, length)
    full = pl.BlockSpec((length, 128), lambda j, t: (0, pair))
    block = pl.BlockSpec((bk, 128), lambda j, t: (j, pair))
    loose = pl.BlockSpec((blocks, rows, 128), lambda j, t: (0, 0, pair))
    return pl.pallas_call(
        functools.partial(backward_kernel, bq=bq, bk=bk, rows=rows),
        out_shape=jax.ShapeDtypeStruct((length, 384), BF),
        grid_spec=pltpu.PrefetchScalarGridSpec(
            num_scalar_prefetch=1,
            grid=(length // bk,),
            in_specs=[
                full, block, block, loose, loose, full,
                pl.BlockSpec((length, 128), lambda j, t: (0, 0)),
                pl.BlockSpec((length, 128), lambda j, t: (0, 0)),
                pl.BlockSpec((bk, 128), lambda j, t: (j, 0)),
                pl.BlockSpec((bk, 128), lambda j, t: (j, 0)),
            ],
            out_specs=pl.BlockSpec((length, 384), lambda j, t: (0, 0)),
            scratch_shapes=[
                pltpu.VMEM((2, length, 128), BF),
                pltpu.VMEM((2, length, 128), BF),
                pltpu.VMEM((128, length), F32),
            ],
        ),
        compiler_params=pltpu.CompilerParams(
            dimension_semantics=("arbitrary",), vmem_limit_bytes=56 << 20
        ),
        cost_estimate=cost(44),
        name="attention_backward",
    )(table, q, k, v, o, do, lse, cosine, sine, cosine, sine)


def gelu(v):
    return 0.5 * v * (1.0 + jnp.tanh(0.7978845608 * (v + 0.044715 * v * v * v)))


def gelu_slope(v):
    square = v * v
    t = jnp.tanh(0.7978845608 * v * (1.0 + 0.044715 * square))
    inner = 0.7978845608 * (1.0 + 3.0 * 0.044715 * square)
    return 0.5 * (1.0 + t) + 0.5 * v * (1.0 - t * t) * inner


def load_weights(order, weight_refs, up, down):
    if order is None:
        up[...], down[...] = weight_refs[0][...], weight_refs[1][...]
        return
    half = pl.program_id(0)
    ups, downs = weight_refs[:2], weight_refs[2:]
    sources, rows, _ = ups[0].shape
    part, cut = rows // 2, downs[0].shape[1]
    per = down.shape[0] // (2 * cut)
    for which in range(2):

        @pl.when(half == which)
        def _(which=which):
            for n in range(sources):
                source = order[which, n]
                base = (source // per) * 2 * per + source % per
                for c in range(2):
                    start = pl.multiple_of((base + c * per) * part, part)
                    up[pl.ds(start, part), :] = ups[which][n, c * part : (c + 1) * part, :]

        for n in range(sources):
            source = order[which, n]

            @pl.when(source // per == half)
            def _(n=n, source=source, which=which):
                start = pl.multiple_of(((source % per) * 2 + which) * cut, cut)
                down[pl.ds(start, cut), :] = downs[which][n]


def mlp_forward_kernel(*refs):
    order = refs[0] if len(refs) == 11 else None
    pre_ref, act_ref, sum_ref, up, down = refs[-5:]
    x_ref, *weight_refs = refs[order is not None : -5]
    half, tile = pl.program_id(0), pl.program_id(1)

    @pl.when(tile == 0)
    def _():
        load_weights(order, weight_refs, up, down)

    tm = pre_ref.shape[0]
    rows = pl.ds(pl.multiple_of(tile * tm, tm), tm)
    pre = dot(x_ref[...], up[...])
    act = gelu(pre).astype(BF)
    pre_ref[...] = pre.astype(BF)
    act_ref[...] = act
    term = dot(act, down[...])

    @pl.when(half == 0)
    def _():
        sum_ref[rows, :] = term

    @pl.when(half != 0)
    def _():
        sum_ref[rows, :] += term


def mlp_backward_kernel(*refs):
    order = refs[0] if len(refs) == 11 else None
    low_ref, sum_ref, up, down = refs[-4:]
    g_ref, pre_ref, *weight_refs = refs[order is not None : -4]
    half, tile = pl.program_id(0), pl.program_id(1)

    @pl.when(tile == 0)
    def _():
        load_weights(order, weight_refs, up, down)

    tm = pre_ref.shape[0]
    rows = pl.ds(pl.multiple_of(tile * tm, tm), tm)
    slope = gelu_slope(pre_ref[...].astype(F32))
    low = (slope * dot(g_ref[...], down[...], NT)).astype(BF)
    low_ref[...] = low
    term = dot(low, up[...], NT)

    @pl.when(half == 0)
    def _():
        sum_ref[rows, :] = term

    @pl.when(half != 0)
    def _():
        sum_ref[rows, :] += term


def mlp_call(kernel, name, us, acts, weights, halves, wide_outs):
    count, model = acts[0].shape
    tables = weights[4:]
    if tables:
        sources, rows, _ = weights[0].shape
        unit = model
        fixed = pl.BlockSpec((sources, rows, model), lambda f, m, *t: (0, 0, 0))
        specs = [fixed] * 4
    else:
        unit = weights[1].shape[0] // halves
        specs = [
            pl.BlockSpec((model, unit), lambda f, m, *t: (0, f)),
            pl.BlockSpec((unit, model), lambda f, m, *t: (f, 0)),
        ]
    tm = min(256, count)
    narrow = pl.BlockSpec((tm, model), lambda f, m, *t: (m, 0))
    wide = pl.BlockSpec((tm, unit), lambda f, m, *t: (m, f))
    return pl.pallas_call(
        kernel,
        out_shape=[jax.ShapeDtypeStruct((count, halves * unit), BF)] * wide_outs
        + [jax.ShapeDtypeStruct((count, model), F32)],
        grid_spec=pltpu.PrefetchScalarGridSpec(
            num_scalar_prefetch=len(tables),
            grid=(halves, count // tm),
            in_specs=[narrow] + [wide] * (len(acts) - 1) + specs,
            out_specs=[wide] * wide_outs
            + [pl.BlockSpec((count, model), lambda f, m, *t: (0, 0))],
            scratch_shapes=[pltpu.VMEM((model, unit), BF), pltpu.VMEM((unit, model), BF)],
        ),
        compiler_params=pltpu.CompilerParams(
            dimension_semantics=("arbitrary", "arbitrary"), vmem_limit_bytes=56 << 20
        ),
        cost_estimate=cost(us),
        name=name,
    )(*tables, *acts, *weights[: 4 if tables else 2])


def mlp_forward(x, weights, halves):
    return mlp_call(mlp_forward_kernel, "mlp_forward", 18, [x], weights, halves, 2)


def mlp_backward(grad, pre, weights, halves):
    return mlp_call(mlp_backward_kernel, "mlp_backward", 20, [grad, pre], weights, halves, 1)


def input_grad_kernel(table, *refs):
    w_ref, out_ref = refs[-2:]
    total = None
    for n, ref in enumerate(refs[:-2]):
        term = dot(ref[...], w_ref[:, n * 384 : (n + 1) * 384], NT)
        total = term if total is None else total + term
    out_ref[0] = total.astype(BF)


def input_grad(table, grads, w, rows):
    model = w.shape[0]
    blocks = grads[0].shape[0] // rows
    return pl.pallas_call(
        input_grad_kernel,
        out_shape=jax.ShapeDtypeStruct((blocks, rows, model), BF),
        grid_spec=pltpu.PrefetchScalarGridSpec(
            num_scalar_prefetch=1,
            grid=(blocks,),
            in_specs=[pl.BlockSpec((rows, 384), lambda i, t: (t[i], 0))] * len(grads)
            + [pl.BlockSpec(w.shape, lambda i, t: (0, 0))],
            out_specs=pl.BlockSpec((1, rows, model), lambda i, t: (i, 0, 0)),
        ),
        compiler_params=pltpu.CompilerParams(
            dimension_semantics=("arbitrary",), vmem_limit_bytes=40 << 20
        ),
        cost_estimate=cost(6),
        name="input_grad",
    )(table, *grads, w)


def head_sum_kernel(*refs, group, spread):
    x_refs, outs = refs[:-3], refs[-3:]
    width = outs[0].shape[1] // group
    for m in range(group):
        for pair, ref in enumerate(x_refs):
            total = None
            for n in spread(m):
                term = ref[n].astype(F32)
                total = term if total is None else total + term
            at = slice(m * width + pair * 128, m * width + (pair + 1) * 128)
            for which, out in enumerate(outs):
                out[:, at] = total[:, which * 128 : (which + 1) * 128]


def head_sum(parts, group, spread):
    _, rows, wide = parts[0].shape
    return pl.pallas_call(
        functools.partial(head_sum_kernel, group=group, spread=spread),
        out_shape=[jax.ShapeDtypeStruct((rows, group * len(parts) * wide // 3), F32)] * 3,
        cost_estimate=cost(2),
        name="head_sum",
    )(*parts)


def standardize(values):
    center = values - jnp.mean(values, axis=-1, keepdims=True)
    rstd = lax.rsqrt(jnp.mean(center * center, axis=-1, keepdims=True) + EPSILON)
    return center * rstd, rstd


def norm_backward(xhat, rstd, gain, grad):
    scaled = grad * gain
    inner = scaled - jnp.mean(scaled, axis=-1, keepdims=True)
    inner = inner - xhat * jnp.mean(scaled * xhat, axis=-1, keepdims=True)
    return rstd * inner, jnp.sum(grad * xhat, axis=0), jnp.sum(grad, axis=0)


def flip(x, axis, bit):
    size = lax.axis_size(axis)
    return lax.ppermute(x, axis, [(i, i ^ bit) for i in range(size)])


def scatter_sends(x, axis, dim, bit):
    here = (lax.axis_index(axis) // bit) % 2
    shape = x.shape
    x = x.reshape(shape[:dim] + (shape[dim] // 2, 2) + shape[dim + 1 :])
    mine = lax.dynamic_index_in_dim(x, here, dim + 1, keepdims=False)
    return mine, lax.dynamic_index_in_dim(x, 1 - here, dim + 1, keepdims=False)


def join(mine, came):
    return (mine.astype(F32) + came.astype(F32)).astype(BF)


def scatter_axis(x, axis, dim, bit=1):
    size = lax.axis_size(axis)
    while bit < size:
        mine, theirs = scatter_sends(x, axis, dim, bit)
        x = join(mine, flip(theirs, axis, bit))
        bit *= 2
    return x.reshape(x.shape[:dim] + x.shape[dim + 1 :])


def together(*groups):
    flat, tree = jax.tree.flatten(groups)
    return jax.tree.unflatten(tree, lax.optimization_barrier(tuple(flat)))


def place_in(order):
    index = jnp.arange(order.shape[0], dtype=jnp.int32)
    return jnp.sum(jnp.where(order[:, None] == index[None, :], index[:, None], 0), axis=0)


def gather_order(axes):
    masks = {axis: [0] for axis in AXES}
    for axis in axes:
        bit = lax.axis_size(axis) // 2
        while bit:
            for name in AXES:
                step = bit if name == axis else 0
                masks[name] = masks[name] + [m ^ step for m in masks[name]]
            bit //= 2
    return {axis: jnp.array(masks[axis], jnp.int32) for axis in AXES}


def source_of(axes):
    masks, total = gather_order(axes), 0
    for axis in ("j", "h", "a", "b"):
        total = total * lax.axis_size(axis) + (lax.axis_index(axis) ^ masks[axis])
    return total


def stages_of(axes):
    stages = []
    for axis in axes:
        bit = lax.axis_size(axis) // 2
        while bit:
            stages.append((axis, bit))
            bit //= 2
    return stages


def after(x, *others):
    return lax.optimization_barrier((x,) + others)[0]


def body(
    tokens, cotangent, w_query, w_key, w_value, w_output, w_up, w_down,
    attn_in_gain, attn_in_bias, attn_out_gain, attn_out_bias,
    mlp_in_gain, mlp_in_bias, mlp_out_gain, mlp_out_bias,
):
    _, rows, model = tokens.shape
    nh, na, nb = lax.axis_size("h"), lax.axis_size("a"), lax.axis_size("b")
    jh = 2 * nh
    devices = 4 * nh * na * nb
    group = 2 * nh * nb
    half = na // 2
    length = rows * na * nb
    width = model // group
    pairs = width // 128
    part = w_query.shape[0]
    ij, ih, ic, ia, ib = (lax.axis_index(axis) for axis in AXES)
    slot, parity = ia // half, ia % 2
    member = (ih * 2 + ic) * nb + ib

    def place(j, h, c, a, b):
        return (((j * nh + h) * 2 + c) * na + a) * nb + b

    everyone = [
        (j, h, c, a, b)
        for j in range(2)
        for h in range(nh)
        for c in range(2)
        for a in range(na)
        for b in range(nb)
    ]
    moves = ([], [])
    for turn in range(2):
        for j, h, c, a, b in everyone:
            to_h, to_c = divmod(a % half, 2)
            plane = (h * 2 + c) * 2 + (turn + a // half) % 2
            target = place(j, to_h, to_c, plane, b)
            moves[turn].append((place(j, h, c, a, b), target))

    def regroup(x, turn):
        x = lax.dynamic_index_in_dim(x, (turn + slot) % 2, 0, keepdims=False)
        return lax.ppermute(x, AXES, moves[turn])

    def restore(x, turn):
        return lax.ppermute(x, AXES, [(there, here) for here, there in moves[turn]])

    def ordered(first, second):
        swap = slot == 1
        return jnp.stack([jnp.where(swap, second, first), jnp.where(swap, first, second)])

    def by_offset(x, offset):
        sends = []
        for j, h, c, a, b in everyone:
            to_hc, to_b = divmod(((h * 2 + c) * nb + b) ^ offset, nb)
            sends.append((place(j, h, c, a, b), place(j, to_hc // 2, to_hc % 2, a, to_b)))
        return lax.ppermute(x, AXES, sends)

    core_bit = nb
    far_bits = [1 << n for n in range(group.bit_length() - 1) if (1 << n) != core_bit]

    packed = jnp.stack(
        [attn_in_gain, attn_in_bias, attn_out_gain, attn_out_bias,
         mlp_in_gain, mlp_in_bias, mlp_out_gain, mlp_out_bias]
    )
    vectors = lax.all_to_all(
        jnp.broadcast_to(packed[None], (devices,) + packed.shape), AXES, 0, 0, tiled=True
    )
    vectors = vectors.transpose(1, 0, 2).reshape(8, model).astype(F32)
    gain_ai, bias_ai, gain_ao, bias_ao, gain_mi, bias_mi, gain_mo, bias_mo = [
        vectors[n] for n in range(8)
    ]

    ff = w_up.shape[1]
    unit = ff // (2 * jh)
    up_split = w_up.reshape(part, jh, 2, unit)
    up_mine = lax.dynamic_index_in_dim(up_split, ic, 2, keepdims=False)
    up_other = flip(lax.dynamic_index_in_dim(up_split, 1 - ic, 2, keepdims=False), "c", 1)
    up_rows = jnp.stack(
        [jnp.where(ic == 0, up_mine, up_other), jnp.where(ic == 0, up_other, up_mine)]
    )
    n_up, n_down = 2 * part * jh * unit // model, w_down.shape[0]
    views = unit == model and part % 32 == 0 and n_up == n_down
    up_rows = up_rows.transpose(2, 0, 1, 3).reshape(n_up, model)
    cut, cut_up, cut_out = n_down // 2, n_up // 2, part // 2

    line_stages = stages_of(("a",))
    low_axes, high_axes = ("b", "h", "j"), ("h", "j", "b")

    def grow(x, came):
        return jnp.concatenate([x, came])

    def grow_all(x, stages):
        for axis, bit in stages:
            x = grow(x, flip(x, axis, bit))
        return x

    first = jnp.concatenate([w_down[:cut], w_output[:cut_out], w_down[cut:], w_output[cut_out:]])
    first, second = first[None], up_rows[None]

    own = [regroup(tokens, turn) for turn in range(2)]
    came = flip(first, *line_stages[0])
    own, came, second = together(own, came, second)
    first = grow_all(grow(first, came), line_stages[1:-1])

    columns = jnp.stack(
        [w.reshape(part, group, pairs, 128) for w in (w_query, w_key, w_value)], axis=3
    ).reshape(part, group, 3 * width)
    columns = columns.transpose(1, 0, 2).reshape(1, nh, 2, 1, nb, part, 3 * width)
    columns = jnp.broadcast_to(columns, (2, nh, 2, na, nb, part, 3 * width))
    columns = after(columns.reshape(devices, part, 3 * width), *own)
    w_heads = lax.all_to_all(columns, AXES, 0, 0, tiled=True).reshape(model, 3 * width)

    pieces = {0: own}
    for bit in far_bits:
        for offset in list(pieces):
            pieces[offset ^ bit] = [by_offset(x, bit) for x in pieces[offset]]
    first_came, second_came = flip(first, *line_stages[-1]), flip(second, *line_stages[0])
    pieces, first_came, second_came = together(pieces, first_came, second_came)
    first = grow(first, first_came)
    second = grow_all(grow(second, second_came), line_stages[1:-1])

    wide = cut + cut_out
    low_stages, high_stages = stages_of(low_axes), stages_of(high_axes)
    first_low, first_high = first[:, :wide], first[:, wide:]
    low_came, high_came = flip(first_low, *low_stages[0]), flip(first_high, *high_stages[0])
    for offset in list(pieces):
        pieces[offset ^ core_bit] = [by_offset(x, core_bit) for x in pieces[offset]]
    pieces, w_heads, low_came, high_came, second = together(
        pieces, w_heads, low_came, high_came, second
    )
    first_low = grow_all(grow(first_low, low_came), low_stages[1:-1])
    first_high = grow_all(grow(first_high, high_came), high_stages[1:-1])
    pieces = [pieces[d][r] for d in range(group) for r in range(2)]

    blocks = 2 * group
    index = jnp.arange(blocks, dtype=jnp.int32)
    table = (member ^ (index % group)) * 2 + (parity ^ (index // group))
    positions_of = (parity ^ (index % 2)) * group + (member ^ (index // 2))
    frequency = jnp.exp(
        jnp.arange(HEAD_DIM // 2, dtype=F32) * (-2.0 * math.log(10000.0) / HEAD_DIM)
    )
    angles = jnp.arange(length, dtype=jnp.int32).astype(F32)[:, None] * frequency[None, :]
    cosine = jnp.tile(jnp.cos(angles), (1, 4))
    sine = jnp.tile(jnp.concatenate([-jnp.sin(angles), jnp.sin(angles)], axis=1), (1, 2))

    pieces, first_low, first_high = together(pieces, first_low, first_high)
    second_came = flip(second, *line_stages[-1])
    low_came, high_came = flip(first_low, *low_stages[-1]), flip(first_high, *high_stages[-1])
    normed, queries, keys, values = qkv_call(
        positions_of, pieces, w_heads, vectors, cosine, sine
    )
    queries, second_came = together(queries, second_came)
    second = grow(second, second_came)
    second_low, second_high = second[:, :cut_up], second[:, cut_up:]
    queries, second_low, second_high, cotangent = together(
        queries, second_low, second_high, cotangent
    )
    up_low_came = flip(second_low, *low_stages[0])
    up_high_came = flip(second_high, *high_stages[0])
    grad_in = [regroup(cotangent, turn) for turn in range(2)]
    attended, lse = attention_forward(table, queries, keys, values, rows)
    attended, lse, low_came, high_came, up_low_came, up_high_came, grad_in = together(
        attended, lse, low_came, high_came, up_low_came, up_high_came, grad_in
    )
    first_low, first_high = grow(first_low, low_came), grow(first_high, high_came)
    second_low = grow_all(grow(second_low, up_low_came), low_stages[1:])
    second_high = grow_all(grow(second_high, up_high_came), high_stages[1:])
    low_from, high_from = (source_of(("a",) + axes) for axes in (low_axes, high_axes))

    def exchange(x):
        return [x[0]] + [by_offset(x[d], d) for d in range(1, group)]

    low_at, high_at = place_in(low_from), place_in(high_from)
    out_mine = jnp.concatenate([first_low[:, cut:][low_at], first_high[:, cut:][high_at]], axis=1)
    out_mine = out_mine.reshape(jh, na * nb * part, model)
    out_other = flip(out_mine, "c", 1)
    if group == 2 * jh:
        w_out = jnp.concatenate([out_mine, out_other])
    else:
        w_out = jnp.where(
            ic == 0,
            jnp.stack([out_mine, out_other], axis=1),
            jnp.stack([out_other, out_mine], axis=1),
        ).reshape(group, width, model)
    mixed = exchange(attended.reshape(group, 2 * rows, width))

    def w_out_of(d):
        block = member ^ d
        if group == 2 * jh:
            block = ((block % 2) ^ ic) * jh + block // 2
        return lax.dynamic_index_in_dim(w_out, block, 0, keepdims=False)

    projected = sum(dot(mixed[d], w_out_of(d)) for d in range(group))
    inputs = jnp.concatenate(own).astype(F32)
    hat_ao, rstd_ao = standardize(projected)
    residual = inputs + hat_ao * gain_ao + bias_ao
    hat_mi, rstd_mi = standardize(residual)
    mlp_mine = (hat_mi * gain_mi + bias_mi).astype(BF)
    mlp_normed = jnp.concatenate([mlp_mine, flip(mlp_mine, "c", 1)])
    mlp_normed, second_low, second_high = together(mlp_normed, second_low, second_high)
    if views:
        weights = [second_low, second_high, first_low, first_high]
        weights.append(jnp.stack([low_from, high_from]))
    else:
        up = jnp.concatenate([second_low[low_at], second_high[high_at]], axis=1)
        up = up.reshape(jh, na, nb, jh, 2, part, unit)
        up = up.transpose(0, 4, 1, 2, 5, 3, 6).reshape(model, jh * unit)
        down = [first_low[:, :cut][low_at], first_high[:, :cut][high_at]]
        weights = [up, jnp.concatenate(down, axis=1).reshape(jh * unit, model)]
    pre_act, activated, branch = mlp_forward(mlp_normed, weights, jh)
    count = 2 * rows

    def core_sum(x):
        return x[:count] + flip(x[count:].astype(BF), "c", 1).astype(F32)

    branch = core_sum(branch)
    hat_mo, rstd_mo = standardize(branch)
    block_loose = (residual + hat_mo * gain_mo + bias_mo).astype(BF)

    grad_in = jnp.concatenate(grad_in).astype(F32)
    grad_branch, g_mo_gain, g_mo_bias = norm_backward(hat_mo, rstd_mo, gain_mo, grad_in)
    branch_mine = grad_branch.astype(BF)
    branch_low = jnp.concatenate([branch_mine, flip(branch_mine, "c", 1)])

    down_part = dot(activated, branch_low, TN).astype(BF)
    down_part = down_part.reshape(2, nh, na, nb, n_down, model)
    down_sends = [
        scatter_sends(x, "b", 3, 1) if nb > 1 else None
        for x in (down_part[..., :cut, :], down_part[..., cut:, :])
    ]
    branch_low, down_sends = together(branch_low, down_sends)

    def meet(pair, axis):
        return join(pair[0], flip(pair[1], axis, 1))

    if nb > 1:
        down_came = [flip(down_sends[n][1], "b", 1) for n in range(2)]
    pre_low, grad_mlp = mlp_backward(branch_low, pre_act, weights, jh)
    if nb > 1:
        pre_low, grad_mlp, down_came[0] = together(pre_low, grad_mlp, down_came[0])
    up_part = dot(mlp_normed, pre_low, TN).astype(BF).reshape(2, nh, 2, na, nb, part, jh * unit)
    up_sends = [scatter_sends(up_part[:, :, c], "j", 0, 1) for c in range(2)]
    grad_mlp, up_sends = together(grad_mlp, up_sends)
    up_came = [flip(x[1], "j", 1) for x in up_sends]
    grad_mlp = core_sum(grad_mlp)

    from_mlp, g_mi_gain, g_mi_bias = norm_backward(hat_mi, rstd_mi, gain_mi, grad_mlp)
    grad_residual = grad_in + from_mlp
    grad_projected, g_ao_gain, g_ao_bias = norm_backward(hat_ao, rstd_ao, gain_ao, grad_residual)
    projected_low = grad_projected.astype(BF)
    attended_low = [dot(projected_low, w_out_of(d), NT).astype(BF) for d in range(group)]
    grad_heads = jnp.stack(exchange(attended_low)).reshape(blocks, rows, width)
    grad_out = jnp.stack([dot(mixed[d], projected_low, TN).astype(BF) for d in range(group)])
    grad_out = jnp.stack(
        [lax.dynamic_index_in_dim(grad_out, member ^ m, 0, keepdims=False) for m in range(group)]
    ).reshape(2, nh, 2, na, nb, part, model)
    grad_out = scatter_axis(grad_out, "c", 2)

    if nb > 1:
        down_part = jnp.concatenate(
            [join(mine[0], came) for mine, came in zip(down_sends, down_came)], axis=-2
        )
    down_part = down_part.reshape(2, nh, na, n_down, model)
    up_parts = [
        scatter_axis(join(mine[0], came).reshape(nh, na, nb, part, -1), "h", 0)
        for mine, came in zip(up_sends, up_came)
    ]
    down_sends = scatter_sends(down_part, "j", 0, 1)
    up_sends = [scatter_sends(x, "b", 1, 1) if nb > 1 else None for x in up_parts]
    out_sends = scatter_sends(grad_out, "b", 3, 1) if nb > 1 else None
    grad_heads, down_sends, up_sends, out_sends = together(
        grad_heads, down_sends, up_sends, out_sends
    )

    def backward(pair, grads):
        return attention_backward(
            table, pair, queries, keys, values, attended, grads, lse, cosine, sine
        )

    down_came = flip(down_sends[1], "j", 1)
    if nb > 1:
        up_came = [flip(x[1], "b", 1) for x in up_sends]
        out_came = flip(out_sends[1], "b", 1)
    grad_pairs = [backward(0, grad_heads)]
    if nb > 1:
        grad_pairs, down_came, up_came, out_came = together(
            grad_pairs, down_came, up_came, out_came
        )
        up_parts = [join(mine[0], came) for mine, came in zip(up_sends, up_came)]
        grad_out = join(out_sends[0], out_came)
    else:
        grad_pairs, down_came = together(grad_pairs, down_came)
    down_part = scatter_axis(join(down_sends[0], down_came).reshape(nh, na, n_down, model), "h", 0)
    up_parts = [x.reshape(na, part, -1) for x in up_parts]
    down_sends = scatter_sends(down_part, "a", 0, 1)
    up_sends = [scatter_sends(x, "a", 0, 1) for x in up_parts]
    out_sends = scatter_sends(grad_out.reshape(2, nh, na, part, model), "j", 0, 1)
    weight_pairs = [dot(normed, grad_pairs[0], TN).astype(BF)]
    heads_in = [
        lax.all_to_all(weight_pairs[0].reshape(devices, part, 384), AXES, 0, 0, tiled=True)
    ]
    if pairs > 1:
        grad_heads, down_sends, up_sends, out_sends, weight_pairs = together(
            grad_heads, down_sends, up_sends, out_sends, weight_pairs
        )
    down_came = flip(down_sends[1], "a", 1)
    up_came = [flip(x[1], "a", 1) for x in up_sends]
    out_came = flip(out_sends[1], "j", 1)
    if pairs > 1:
        grad_pairs.append(backward(1, grad_heads))
        grad_pairs, down_came, up_came, out_came = together(
            grad_pairs, down_came, up_came, out_came
        )
        weight_pairs.append(dot(normed, grad_pairs[1], TN).astype(BF))
    grad_pairs, weight_pairs, heads_in = together(grad_pairs, weight_pairs, heads_in)
    for x in weight_pairs[1:]:
        heads_in.append(lax.all_to_all(x.reshape(devices, part, 384), AXES, 0, 0, tiled=True))
    grad_blocks = input_grad(positions_of, grad_pairs, w_heads, rows)
    grad_out = join(out_sends[0], out_came).reshape(nh, na, part, model)
    grad_out = scatter_axis(grad_out, "h", 0)
    grad_out = scatter_axis(grad_out, "a", 0)
    down_part = scatter_axis(join(down_sends[0], down_came), "a", 0, 2)
    up_low, up_high = (
        scatter_axis(join(mine[0], came), "a", 0, 2) for mine, came in zip(up_sends, up_came)
    )
    block_out = ordered(restore(block_loose[:rows], 0), restore(block_loose[rows:], 1))

    sums = {d: [grad_blocks[2 * d + r] for r in range(2)] for d in range(group)}
    for bit in [core_bit] + far_bits:
        kind = BF if far_bits and bit != far_bits[-1] else F32
        for d in [d for d in sums if d & bit]:
            gone = sums.pop(d)
            for r in range(2):
                came = by_offset(gone[r], bit).astype(F32)
                sums[d ^ bit][r] = (sums[d ^ bit][r].astype(F32) + came).astype(kind)
    g_ai_gain, g_ai_bias, grad_tokens = 0.0, 0.0, []
    for r in range(2):
        hat, rstd = standardize(own[r].astype(F32))
        grad_input, gain_term, bias_term = norm_backward(hat, rstd, gain_ai, sums[0][r])
        g_ai_gain, g_ai_bias = g_ai_gain + gain_term, g_ai_bias + bias_term
        total = grad_residual[r * rows : (r + 1) * rows] + grad_input
        if r == 1:
            total, heads_in = together(total, heads_in)
        grad_tokens.append(restore(total.astype(BF), r))
    grad_tokens = ordered(*grad_tokens)

    def spread(m):
        hc, b = divmod(m, nb)
        return [place(j, hc // 2, hc % 2, a, b) for j in range(2) for a in range(na)]

    g_query, g_key, g_value = head_sum(heads_in, group, spread)
    g_down, g_out = down_part.astype(F32), grad_out.astype(F32)
    up_keep = jnp.where(ic == 0, up_low, up_high).reshape(part, jh, unit)
    up_give = jnp.where(ic == 0, up_high, up_low)
    up_come = flip(up_give, "c", 1).reshape(part, jh, unit)
    g_up = jnp.where(
        ic == 0, jnp.stack([up_keep, up_come], axis=2), jnp.stack([up_come, up_keep], axis=2)
    ).reshape(part, ff).astype(F32)

    small = jnp.stack(
        [g_ai_gain, g_ai_bias, g_ao_gain, g_ao_bias, g_mi_gain, g_mi_bias, g_mo_gain, g_mo_bias]
    )
    small = small.reshape(8, devices, part).transpose(1, 0, 2)
    small = jnp.sum(lax.all_to_all(small, AXES, 0, 0, tiled=True), axis=0)
    return (
        block_out, grad_tokens, g_query, g_key, g_value, g_out, g_up, g_down,
        small[0], small[1], small[2], small[3], small[4], small[5], small[6], small[7],
    )


def solution(mesh):
    fsdp, seq = mesh.shape["fsdp"], mesh.shape["seq"]
    inner = Mesh(mesh.devices.reshape(2, fsdp // 4, 2, fsdp, seq // fsdp), AXES)
    lead, line = ("j", "h", "c"), ("a", "b")
    acts = P(lead, line, None)
    weights = P(lead + line, None)
    vector = P(lead + line)
    return jax.shard_map(
        body,
        mesh=inner,
        in_specs=(acts,) * 2 + (weights,) * 6 + (vector,) * 8,
        out_specs=(acts,) * 2 + (weights,) * 6 + (vector,) * 8,
        check_vma=False,
    )
```

time: 2180 us -> 591 us (0.27)
  waiting for transfers between devices: 1220 us -> 166 us
  matrix products: 521 us -> 31.6 us
  blocking collectives: 188 us -> 0 us
  Pallas kernels: 0 us -> 138 us
  starting transfers between devices: 20.6 us -> 106 us
  local copies, waits for them, and re-layouts: 109 us -> 73.6 us
  loops' own time: 28 us -> 0 us
    reduce_scatter x6 -> x0, waiting for transfers between devices: 981 us -> none  [the longest x1 363 us: body(): lax.psum_scatter(grad_up_full, ('fsdp', 'seq'), scatter_dimension=0, tile...]
    dot_general x74 -> x16, matrix products: 521 us -> 31.6 us  [dot(): return lax.dot_general(left, right, dims, preferred_element_type=F32)]
    ppermute x0 -> x63, waiting for transfers between devices: none -> 152 us  [the longest x37 125 us: flip(): return lax.ppermute(x, axis, [(i, i ^ bit) for i in range(size)])]
    pallas_call x0 -> x8, Pallas kernels: none -> 138 us  [the longest x2 49.6 us: attention_backward(): pl.pallas_call(functools.partial(backward_kernel, bq=bq, bk=bk, rows=rows...]
    all_gather x6 -> x0, waiting for transfers between devices: 132 us -> none  [the longest x1 55.4 us: body(): lax.all_gather(w_query, ('fsdp', 'seq'), axis=0, tiled=True)]
    all_to_all x3 -> x0, blocking collectives: 102 us -> none  [the longest x1 37.9 us: body(): lax.all_to_all(jnp.stack(key_grads), 'seq', split_axis=1, concat_axis=2,...]
    all_to_all x5, waiting for transfers between devices: 102 us -> 14.1 us  [the longest x1 14 us: body(): small = jnp.sum(lax.all_to_all(small, AXES, 0, 0, tiled=True), axis=0)]
    unnamed x2 -> x0, blocking collectives: 86 us -> none
  transfers between devices with their start and end apart: 17 -> 68, of which waited for: 12 -> 20; matrix products, arithmetic and copies ran while one was open for 29% -> 20% of each run, Pallas kernels for 0% -> 20%
where the time goes in v1:
time: 591 us; the launch traced here: 583 us
  waiting for transfers between devices  166 us (28%)
  Pallas kernels  138 us (23%)
  starting transfers between devices  106 us (18%)
  local copies, waits for them, and re-layouts  73.6 us (12%)
  other arithmetic  64.2 us (11%)
  matrix products  31.6 us (5%)
    ppermute x37, waiting for transfers between devices, flip(): return lax.ppermute(x, axis, [(i, i ^ bit) for i in range(size)])  125 us
    pallas_call x2, Pallas kernels, attention_backward(): pl.pallas_call(functools.partial(backward_kernel, bq=bq, bk=bk, rows=rows...  49.6 us
    pallas_call x2, Pallas kernels, mlp_call(): pl.pallas_call(kernel, out_shape=[jax.ShapeDtypeStruct((count, halves * u...  44.1 us
    ppermute x37, starting transfers between devices, flip(): return lax.ppermute(x, axis, [(i, i ^ bit) for i in range(size)])  35.1 us
    dot_general x16, matrix products, dot(): return lax.dot_general(left, right, dims, preferred_element_type=F32)  31.6 us
    ppermute x18, waiting for transfers between devices, by_offset(): return lax.ppermute(x, AXES, sends)  27.2 us
    pallas_call x1, Pallas kernels, attention_forward(): pl.pallas_call(functools.partial(forward_kernel, bq=bq, bk=bk, rows=rows)...  22.9 us
    unnamed x175, local copies, waits for them, and re-layouts  15.7 us
  transfers between devices with their start and end apart: 68, of which 20 were waited for; matrix products, arithmetic and copies ran while one was open for 20% of the time, Pallas kernels for 20%

profile of v1, /device:TPU:1, one launch (start us, length us, event | category | flops | bytes accessed | tf_op | source)
XLA Modules:
  0.0 582.5 jit_solution(13975349013583972520)
XLA Ops:
  2.2 7.1 %all-to-all-start.1 = ((bf16[32,2,128]{2,1,0:T(2,128)(2,1)}), bf16[32,2,128]{2,1,0:T(2,128)(2,1)S(1)}, u32[]{:S(2)}, u32[]{:S(2)}) async-start(bf16[32,2,128]{2,1,0:T(2,128)(2,1)} %reshape.516), calls=%async_computation.1 | async-start | bytes 32768 | tf_op jit(solution)/shard_map/all_to_all | solution.py:638
  11.5 4.6 collective-permute-start
  23.6 22.2 %collective-permute-done.2 = bf16[1,160,1024]{2,1,0:T(8,128)(2,1)S(1)} collective-permute-done((bf16[1,160,1024]{2,1,0:T(8,128)(2,1)S(1)}, bf16[1,160,1024]{2,1,0:T(8,128)(2,1)S(1)}, u32[]{:S(2)}, u32[]{:S(2)}) %collective-permute-start.2) | collective-permute-done | bytes 327712 | tf_op jit(solution)/shard_map/ppermute | solution.py:508
  47.1 12.4 %all-to-all-start = ((bf16[32,32,768]{2,1,0:T(8,128)(2,1)}), bf16[32,32,768]{2,1,0:T(8,128)(2,1)S(1)}, u32[]{:S(2)}, u32[]{:S(2)}) async-start(bf16[32,32,768]{2,1,0:T(8,128)(2,1)} %bitcast.264), calls=%async_computation | async-start | bytes 3145728 | tf_op jit(solution)/shard_map/all_to_all | solution.py:684
  66.4 38.5 %collective-permute-done.7 = bf16[1,128,1024]{2,1,0:T(8,128)(2,1)S(1)} collective-permute-done((bf16[1,128,1024]{2,1,0:T(8,128)(2,1)}, bf16[1,128,1024]{2,1,0:T(8,128)(2,1)S(1)}, u32[]{:S(2)}, u32[]{:S(2)}) %collective-permute-start.7) | collective-permute-done | bytes 262176 | tf_op jit(solution)/shard_map/ppermute | solution.py:508
  134.4 12.4 %qkv.1 = (bf16[2048,1024]{1,0:T(8,128)(2,1)}, bf16[2048,256]{1,0:T(8,128)(2,1)S(1)}, bf16[2048,256]{1,0:T(8,128)(2,1)}, bf16[2048,256]{1,0:T(8,128)(2,1)}) custom-call(s32[8]{0:T(128)S(1)} %fusion.78.table, bf16[256,1024]{1,0:T(8,128)(2,1)S(1)} %collective-permute-done.refs_0_, bf16[256,1024]{1,0:T(8,128)(2,1)S(1)} %collective-permute-done.1.refs_1_, ...), custom_call_target="tpu_custom_call" | custom-call | flops 11000000 | bytes 1024 | tf_op jit(solution)/shard_map/qkv/pallas_call | solution.py:68
  154.5 19.3 %collective-permute-done.17 = bf16[4,64,1024]{2,1,0:T(8,128)(2,1)S(1)} collective-permute-done((bf16[4,64,1024]{2,1,0:T(8,128)(2,1)S(1)}, bf16[4,64,1024]{2,1,0:T(8,128)(2,1)S(1)}, u32[]{:S(2)}, u32[]{:S(2)}) %collective-permute-start.17) | collective-permute-done | bytes 524320 | tf_op jit(solution)/shard_map/ppermute | solution.py:508
  178.3 22.9 %attention_forward.1 = (bf16[8,256,256]{2,1,0:T(8,128)(2,1)S(1)}, f32[2048,256]{1,0:T(8,128)}) custom-call(s32[8]{0:T(128)S(1)} %fusion.74.table, bf16[2048,256]{1,0:T(8,128)(2,1)S(1)} %get-tuple-element.163.q_ref, bf16[2048,256]{1,0:T(8,128)(2,1)S(1)} %copy-done.4, bf16[2048,256]{1,0:T(8,128)(2,1)S(1)} %copy-done.5), custom_call_target="tpu_custom_call" | custom-call | flops 23000000 | bytes 1024 | tf_op jit(solution)/shard_map/attention_forward/pallas_call | solution.py:145
  219.1 7.3 %collective-permute-done.22 = bf16[512,256]{1,0:T(8,128)(2,1)S(1)} collective-permute-done((bf16[512,256]{1,0:T(8,128)(2,1)S(1)}, bf16[512,256]{1,0:T(8,128)(2,1)S(1)}, u32[]{:S(2)}, u32[]{:S(2)}) %collective-permute-start.22) | collective-permute-done | bytes 262176 | tf_op jit(solution)/shard_map/ppermute | solution.py:629
  234.6 4.6 collective-permute-done.26
  240.7 8.2 %collective-permute-done.27 = bf16[8,64,1024]{2,1,0:T(8,128)(2,1)S(1)} collective-permute-done((bf16[8,64,1024]{2,1,0:T(8,128)(2,1)S(1)}, bf16[8,64,1024]{2,1,0:T(8,128)(2,1)S(1)}, u32[]{:S(2)}, u32[]{:S(2)}) %collective-permute-start.27) | collective-permute-done | bytes 1048608 | tf_op jit(solution)/shard_map/ppermute | solution.py:508
  252.0 20.4 %mlp_forward.1 = (bf16[1024,2048]{1,0:T(8,128)(2,1)}, bf16[1024,2048]{1,0:T(8,128)(2,1)}, f32[1024,1024]{1,0:T(8,128)}) custom-call(s32[2,16]{1,0:T(2,128)} %pad_add_fusion.refs_0_, bf16[1024,1024]{1,0:T(8,128)(2,1)} %pad_maximum_fusion.refs_1_, bf16[16,64,1024]{2,1,0:T(8,128)(2,1)} %pad_maximum_fusion.1.refs_2_.refs_3_, ...), custom_call_target="tpu_custom_call" | custom-call | flops 18000000 | bytes 1024 | tf_op jit(solution)/shard_map/mlp_forward/pallas_call | solution.py:411
  288.4 7.4 %convolution_convert_fusion.1 = bf16[2048,1024]{1,0:T(8,128)(2,1)S(1)} fusion(bf16[1024,2048]{1,0:T(8,128)(2,1)} %get-tuple-element.184, bf16[512,1024]{1,0:T(8,128)(2,1)} %collective-permute-done.31, bf16[512,1024]{1,0:T(8,128)(2,1)} %get-tuple-element.291), kind=kOutput, calls=%fused_computation.3 | convolution fusion | flops 4301258752 | bytes 10485760 | tf_op jit(solution)/shard_map/dot_general | solution.py:30
  304.2 23.7 %mlp_backward.1 = (bf16[1024,2048]{1,0:T(8,128)(2,1)}, f32[1024,1024]{1,0:T(8,128)}) custom-call(s32[2,16]{1,0:T(2,128)} %pad_add_fusion.refs_0_, bf16[1024,1024]{1,0:T(8,128)(2,1)} %pad_maximum_fusion.3.refs_1_, bf16[1024,2048]{1,0:T(8,128)(2,1)} %get-tuple-element.186.refs_2_, bf16[16,64,1024]{2,1,0:T(8,128)(2,1)} %pad_maximum_fusion.1.refs_2_.refs_3_, ...), custom_call_target="tpu_custom_call" | custom-call | flops 20000000 | bytes 1024 | tf_op jit(solution)/shard_map/mlp_backward/pallas_call | solution.py:411
  327.9 7.2 %convolution_convert_fusion = bf16[1024,2048]{1,0:T(8,128)(2,1)S(1)} fusion(bf16[1024,1024]{1,0:T(8,128)(2,1)S(1)} %copy-done.24, bf16[1024,2048]{1,0:T(8,128)(2,1)} %get-tuple-element.191), kind=kOutput, calls=%fused_computation.2 | convolution fusion | flops 4297064448 | bytes 10485760 | tf_op jit(solution)/shard_map/dot_general | solution.py:30
  372.0 19.0 %collective-permute-done.39 = bf16[1,1,4,2,32,2048]{5,4,3,2,1,0:T(8,128)(2,1)S(1)} collective-permute-done((bf16[1,1,4,2,32,2048]{5,4,3,2,1,0:T(8,128)(2,1)}, bf16[1,1,4,2,32,2048]{5,4,3,2,1,0:T(8,128)(2,1)S(1)}, u32[]{:S(2)}, u32[]{:S(2)}) %collective-permute-start.39) | collective-permute-done | bytes 1048608 | tf_op jit(solution)/shard_map/ppermute | solution.py:508
  402.2 24.7 %attention_backward.2.refs_0_ = bf16[2048,384]{1,0:T(8,128)(2,1)} custom-call(s32[8]{0:T(128)} %copy-done.14, bf16[2048,256]{1,0:T(8,128)(2,1)} %copy-done.3, bf16[2048,256]{1,0:T(8,128)(2,1)} %get-tuple-element.164.k_ref, bf16[2048,256]{1,0:T(8,128)(2,1)} %get-tuple-element.165.v_ref, bf16[8,256,256]{2,1,0:T(8,128)(2,1)} %copy-done.6, ...), custom_call_target="tpu_custom_call" | custom-call | flops 44000000 | bytes 1024 | tf_op jit(solution)/shard_map/attention_backward/pallas_call | solution.py:273
  449.6 5.6 all-to-all-start.2
  455.1 24.9 %attention_backward.3.refs_1_ = bf16[2048,384]{1,0:T(8,128)(2,1)} custom-call(s32[8]{0:T(128)} %copy-done.14, bf16[2048,256]{1,0:T(8,128)(2,1)} %copy-done.3, bf16[2048,256]{1,0:T(8,128)(2,1)} %get-tuple-element.164.k_ref, bf16[2048,256]{1,0:T(8,128)(2,1)} %get-tuple-element.165.v_ref, bf16[8,256,256]{2,1,0:T(8,128)(2,1)} %copy-done.6, ...), custom_call_target="tpu_custom_call" | custom-call | flops 44000000 | bytes 1024 | tf_op jit(solution)/shard_map/attention_backward/pallas_call | solution.py:273
  495.4 6.5 %input_grad.1 = bf16[8,256,1024]{2,1,0:T(8,128)(2,1)S(1)} custom-call(s32[8]{0:T(128)S(1)} %fusion.78.table, bf16[2048,384]{1,0:T(8,128)(2,1)S(1)} %copy-done.9, bf16[2048,384]{1,0:T(8,128)(2,1)S(1)} %copy-done.11, bf16[1024,768]{1,0:T(8,128)(2,1)S(1)} %bitcast.250), custom_call_target="tpu_custom_call" | custom-call | flops 6000000 | bytes 1024 | tf_op jit(solution)/shard_map/input_grad/pallas_call | solution.py:451
  517.9 5.0 all-to-all-start.3
  525.5 16.4 %collective-permute-done.55 = bf16[256,1024]{1,0:T(8,128)(2,1)S(1)} collective-permute-done((bf16[256,1024]{1,0:T(8,128)(2,1)}, bf16[256,1024]{1,0:T(8,128)(2,1)S(1)}, u32[]{:S(2)}, u32[]{:S(2)}) %collective-permute-start.55) | collective-permute-done | bytes 524320 | tf_op jit(solution)/shard_map/ppermute | solution.py:629
  556.2 4.8 all-to-all-start.4
  562.7 14.0 %all-to-all-done.4 = f32[32,1,256]{2,1,0:T(1,128)S(1)} async-done(((f32[32,1,256]{2,1,0:T(1,128)}), f32[32,1,256]{2,1,0:T(1,128)S(1)}, u32[]{:S(2)}, u32[]{:S(2)}) %all-to-all-start.4) | async-done | bytes 32800 | tf_op jit(solution)/shard_map/all_to_all | solution.py:937
  (490 shorter events, 240.6 us)
Async XLA Ops:
  2.2 44.9 %all-to-all-start.1 = ((bf16[32,2,128]{2,1,0:T(2,128)(2,1)}), bf16[32,2,128]{2,1,0:T(2,128)(2,1)S(1)}, u32[]{:S(2)}, u32[]{:S(2)}) async-start(bf16[32,2,128]{2,1,0:T(2,128)(2,1)} %reshape.516), calls=%async_computation.1 | async-start | bytes 32768 | tf_op jit(solution)/shard_map/all_to_all | solution.py:638
  11.5 34.3 %collective-permute-start = (bf16[256,1024]{1,0:T(8,128)(2,1)}, bf16[256,1024]{1,0:T(8,128)(2,1)S(1)}, u32[]{:S(2)}, u32[]{:S(2)}) collective-permute-start(bf16[256,1024]{1,0:T(8,128)(2,1)} %get-tuple-element.332), channel_id=1, source_target_pairs={{0,0},{1,1},{2,8},{3,9},{4,2},{5,3},{6,10},{7,11},{8,4},{9,5},{10,... | collective-permute-start | bytes 1572872 | tf_op jit(solution)/shard_map/ppermute | solution.py:615
  47.1 80.4 %all-to-all-start = ((bf16[32,32,768]{2,1,0:T(8,128)(2,1)}), bf16[32,32,768]{2,1,0:T(8,128)(2,1)S(1)}, u32[]{:S(2)}, u32[]{:S(2)}) async-start(bf16[32,32,768]{2,1,0:T(8,128)(2,1)} %bitcast.264), calls=%async_computation | async-start | bytes 3145728 | tf_op jit(solution)/shard_map/all_to_all | solution.py:684
  59.6 47.1 %collective-permute-start.6 = (bf16[2,160,1024]{2,1,0:T(8,128)(2,1)S(1)}, bf16[2,160,1024]{2,1,0:T(8,128)(2,1)S(1)}, u32[]{:S(2)}, u32[]{:S(2)}) collective-permute-start(bf16[2,160,1024]{2,1,0:T(8,128)(2,1)S(1)} %pad_maximum_fusion.16), channel_id=1, source_target_pairs={{0,2},{2,0},{4,6},{6,4},{1,3},{3,1},{5,7},{7,5},{8,10},{10,8},{12,... | collective-permute-start | bytes 1966088 | tf_op jit(solution)/shard_map/ppermute | solution.py:508
  61.1 43.8 %collective-permute-start.4 = (bf16[256,1024]{1,0:T(8,128)(2,1)S(1)}, bf16[256,1024]{1,0:T(8,128)(2,1)S(1)}, u32[]{:S(2)}, u32[]{:S(2)}) collective-permute-start(bf16[256,1024]{1,0:T(8,128)(2,1)S(1)} %collective-permute-done.refs_0_), channel_id=1, source_target_pairs={{0,1},{1,0},{2,3},{3,2},{4,5},{5,4},{6,7},{7,6},{8,9},{9,8},{10,11... | collective-permute-start | bytes 1572872 | tf_op jit(solution)/shard_map/ppermute | solution.py:629
  62.3 42.7 %collective-permute-start.5 = (bf16[256,1024]{1,0:T(8,128)(2,1)S(1)}, bf16[256,1024]{1,0:T(8,128)(2,1)S(1)}, u32[]{:S(2)}, u32[]{:S(2)}) collective-permute-start(bf16[256,1024]{1,0:T(8,128)(2,1)S(1)} %collective-permute-done.1.refs_1_), channel_id=1, source_target_pairs={{0,1},{1,0},{2,3},{3,2},{4,5},{5,4},{6,7},{7,6},{8,9},{9,8},{10,11... | collective-permute-start | bytes 1572872 | tf_op jit(solution)/shard_map/ppermute | solution.py:629
  62.6 42.4 %collective-permute-start.7 = (bf16[1,128,1024]{2,1,0:T(8,128)(2,1)}, bf16[1,128,1024]{2,1,0:T(8,128)(2,1)S(1)}, u32[]{:S(2)}, u32[]{:S(2)}) collective-permute-start(bf16[1,128,1024]{2,1,0:T(8,128)(2,1)} %bitcast.276), channel_id=1, source_target_pairs={{0,4},{2,6},{4,0},{6,2},{1,5},{3,7},{5,1},{7,3},{8,12},{10,14},{12... | collective-permute-start | bytes 786440 | tf_op jit(solution)/shard_map/ppermute | solution.py:508
  132.7 68.6 %collective-permute-start.15 = (bf16[8,80,1024]{2,1,0:T(8,128)(2,1)S(1)}, bf16[8,80,1024]{2,1,0:T(8,128)(2,1)}, u32[]{:S(2)}, u32[]{:S(2)}) collective-permute-start(bf16[8,80,1024]{2,1,0:T(8,128)(2,1)S(1)} %get-tuple-element.168), channel_id=1, source_target_pairs={{0,16},{16,0},{1,17},{17,1},{2,18},{18,2},{3,19},{19,3},{4,20},{20... | collective-permute-start | bytes 3932168 | tf_op jit(solution)/shard_map/ppermute | solution.py:508
  134.0 67.4 %collective-permute-start.16 = (bf16[8,80,1024]{2,1,0:T(8,128)(2,1)S(1)}, bf16[8,80,1024]{2,1,0:T(8,128)(2,1)}, u32[]{:S(2)}, u32[]{:S(2)}) collective-permute-start(bf16[8,80,1024]{2,1,0:T(8,128)(2,1)S(1)} %get-tuple-element.169), channel_id=1, source_target_pairs={{0,1},{1,0},{2,3},{3,2},{4,5},{5,4},{6,7},{7,6},{8,9},{9,8},{10,11... | collective-permute-start | bytes 3932168 | tf_op jit(solution)/shard_map/ppermute | solution.py:508
  149.6 51.7 %collective-permute-start.18 = (bf16[4,64,1024]{2,1,0:T(8,128)(2,1)S(1)}, bf16[4,64,1024]{2,1,0:T(8,128)(2,1)S(1)}, u32[]{:S(2)}, u32[]{:S(2)}) collective-permute-start(bf16[4,64,1024]{2,1,0:T(8,128)(2,1)S(1)} %get-tuple-element.171), channel_id=1, source_target_pairs={{0,16},{16,0},{1,17},{17,1},{2,18},{18,2},{3,19},{19,3},{4,20},{20... | collective-permute-start | bytes 1572872 | tf_op jit(solution)/shard_map/ppermute | solution.py:508
  150.9 50.4 %collective-permute-start.19 = (bf16[256,1024]{1,0:T(8,128)(2,1)}, bf16[256,1024]{1,0:T(8,128)(2,1)S(1)}, u32[]{:S(2)}, u32[]{:S(2)}) collective-permute-start(bf16[256,1024]{1,0:T(8,128)(2,1)} %get-tuple-element.328), channel_id=1, source_target_pairs={{0,0},{1,1},{2,8},{3,9},{4,2},{5,3},{6,10},{7,11},{8,4},{9,5},{10,... | collective-permute-start | bytes 1572872 | tf_op jit(solution)/shard_map/ppermute | solution.py:615
  303.0 46.8 %collective-permute-start.37 = (bf16[2,1,4,1,64,1024]{5,4,3,2,0,1:T(8,128)(2,1)}, bf16[2,1,4,1,64,1024]{5,4,3,2,0,1:T(8,128)(2,1)}, u32[]{:S(2)}, u32[]{:S(2)}) collective-permute-start(bf16[2,1,4,1,64,1024]{5,4,3,2,0,1:T(8,128)(2,1)} %get-tuple-element.196), channel_id=1, source_target_pairs={{0,1},{1,0},{2,3},{3,2},{4,5},{5,4},{6,7},{7,6},{8,9},{9,8},{10,11... | collective-permute-start | bytes 3145736 | tf_op jit(solution)/shard_map/ppermute | solution.py:508
  343.8 47.2 %collective-permute-start.39 = (bf16[1,1,4,2,32,2048]{5,4,3,2,1,0:T(8,128)(2,1)}, bf16[1,1,4,2,32,2048]{5,4,3,2,1,0:T(8,128)(2,1)S(1)}, u32[]{:S(2)}, u32[]{:S(2)}) collective-permute-start(bf16[1,1,4,2,32,2048]{5,4,3,2,1,0:T(8,128)(2,1)} %get-tuple-element.200), channel_id=1, source_target_pairs={{0,16},{16,0},{1,17},{17,1},{2,18},{18,2},{3,19},{19,3},{4,20},{20... | collective-permute-start | bytes 3145736 | tf_op jit(solution)/shard_map/ppermute | solution.py:508
  395.5 36.6 %collective-permute-start.41 = (bf16[1,1,4,128,1024]{4,3,2,1,0:T(8,128)(2,1)}, bf16[1,1,4,128,1024]{4,3,2,1,0:T(8,128)(2,1)S(1)}, u32[]{:S(2)}, u32[]{:S(2)}) collective-permute-start(bf16[1,1,4,128,1024]{4,3,2,1,0:T(8,128)(2,1)} %get-tuple-element.203), channel_id=1, source_target_pairs={{0,16},{16,0},{1,17},{17,1},{2,18},{18,2},{3,19},{19,3},{4,20},{20... | collective-permute-start | bytes 3145736 | tf_op jit(solution)/shard_map/ppermute | solution.py:508
  397.6 34.5 %collective-permute-start.44 = (bf16[2,1,4,1,32,1024]{5,4,2,3,1,0:T(8,128)(2,1)}, bf16[2,1,4,1,32,1024]{5,4,2,3,1,0:T(8,128)(2,1)S(1)}, u32[]{:S(2)}, u32[]{:S(2)}) collective-permute-start(bf16[2,1,4,1,32,1024]{5,4,2,3,1,0:T(8,128)(2,1)} %get-tuple-element.206), channel_id=1, source_target_pairs={{0,1},{1,0},{2,3},{3,2},{4,5},{5,4},{6,7},{7,6},{8,9},{9,8},{10,11... | collective-permute-start | bytes 1572872 | tf_op jit(solution)/shard_map/ppermute | solution.py:508
  399.6 44.9 %collective-permute-start.29 = (bf16[256,1024]{1,0:T(8,128)(2,1)}, bf16[256,1024]{1,0:T(8,128)(2,1)S(1)}, u32[]{:S(2)}, u32[]{:S(2)}) collective-permute-start(bf16[256,1024]{1,0:T(8,128)(2,1)} %get-tuple-element.321), channel_id=1, source_target_pairs={{2,0},{3,1},{10,2},{11,3},{0,4},{1,5},{8,6},{9,7},{6,8},{7,9},{14,... | collective-permute-start | bytes 1572872 | tf_op jit(solution)/shard_map/ppermute | solution.py:618
  440.8 39.3 %collective-permute-start.45 = (bf16[2,128,1024]{2,1,0:T(8,128)(2,1)}, bf16[2,128,1024]{2,1,0:T(8,128)(2,1)}, u32[]{:S(2)}, u32[]{:S(2)}) collective-permute-start(bf16[2,128,1024]{2,1,0:T(8,128)(2,1)} %get-tuple-element.218), channel_id=1, source_target_pairs={{0,2},{2,0},{4,6},{6,4},{1,3},{3,1},{5,7},{7,5},{8,10},{10,8},{12,... | collective-permute-start | bytes 1572872 | tf_op jit(solution)/shard_map/ppermute | solution.py:508
  443.0 37.0 %collective-permute-start.46 = (bf16[2,32,2048]{2,1,0:T(8,128)(2,1)}, bf16[2,32,2048]{2,1,0:T(8,128)(2,1)}, u32[]{:S(2)}, u32[]{:S(2)}) collective-permute-start(bf16[2,32,2048]{2,1,0:T(8,128)(2,1)} %get-tuple-element.219), channel_id=1, source_target_pairs={{0,2},{2,0},{4,6},{6,4},{1,3},{3,1},{5,7},{7,5},{8,10},{10,8},{12,... | collective-permute-start | bytes 786440 | tf_op jit(solution)/shard_map/ppermute | solution.py:508
  444.1 35.9 %collective-permute-start.47 = (bf16[2,32,2048]{2,1,0:T(8,128)(2,1)}, bf16[2,32,2048]{2,1,0:T(8,128)(2,1)}, u32[]{:S(2)}, u32[]{:S(2)}) collective-permute-start(bf16[2,32,2048]{2,1,0:T(8,128)(2,1)} %get-tuple-element.220), channel_id=1, source_target_pairs={{0,2},{2,0},{4,6},{6,4},{1,3},{3,1},{5,7},{7,5},{8,10},{10,8},{12,... | collective-permute-start | bytes 786440 | tf_op jit(solution)/shard_map/ppermute | solution.py:508
  444.5 35.6 %collective-permute-start.48 = (bf16[1,1,4,32,1024]{4,3,2,1,0:T(8,128)(2,1)}, bf16[1,1,4,32,1024]{4,3,2,1,0:T(8,128)(2,1)}, u32[]{:S(2)}, u32[]{:S(2)}) collective-permute-start(bf16[1,1,4,32,1024]{4,3,2,1,0:T(8,128)(2,1)} %get-tuple-element.221), channel_id=1, source_target_pairs={{0,16},{16,0},{1,17},{17,1},{2,18},{18,2},{3,19},{19,3},{4,20},{20... | collective-permute-start | bytes 786440 | tf_op jit(solution)/shard_map/ppermute | solution.py:508
  449.6 43.0 %all-to-all-start.2 = ((bf16[32,32,384]{2,1,0:T(8,128)(2,1)}), bf16[32,32,384]{2,1,0:T(8,128)(2,1)S(1)}, u32[]{:S(2)}, u32[]{:S(2)}) async-start(bf16[32,32,384]{2,1,0:T(8,128)(2,1)} %bitcast.280), calls=%async_computation.2 | async-start | bytes 1572864 | tf_op jit(solution)/shard_map/all_to_all | solution.py:873
  516.9 36.2 %collective-permute-start.62 = (bf16[1,128,1024]{2,1,0:T(8,128)(2,1)}, bf16[1,128,1024]{2,1,0:T(8,128)(2,1)}, u32[]{:S(2)}, u32[]{:S(2)}) collective-permute-start(bf16[1,128,1024]{2,1,0:T(8,128)(2,1)} %constant_dynamic-slice_fusion.13), channel_id=1, source_target_pairs={{0,4},{2,6},{4,0},{6,2},{1,5},{3,7},{5,1},{7,3},{8,12},{10,14},{12... | collective-permute-start | bytes 786440 | tf_op jit(solution)/shard_map/ppermute | solution.py:508
  517.9 34.7 %all-to-all-start.3 = ((bf16[32,32,384]{2,1,0:T(8,128)(2,1)}), bf16[32,32,384]{2,1,0:T(8,128)(2,1)S(1)}, u32[]{:S(2)}, u32[]{:S(2)}) async-start(bf16[32,32,384]{2,1,0:T(8,128)(2,1)} %bitcast.279), calls=%async_computation.3 | async-start | bytes 1572864 | tf_op jit(solution)/shard_map/all_to_all | solution.py:890
  546.8 34.1 %collective-permute-start.56 = (bf16[256,1024]{1,0:T(8,128)(2,1)}, bf16[256,1024]{1,0:T(8,128)(2,1)S(1)}, u32[]{:S(2)}, u32[]{:S(2)}) collective-permute-start(bf16[256,1024]{1,0:T(8,128)(2,1)} %fusion.28), channel_id=1, source_target_pairs={{0,0},{1,1},{8,2},{9,3},{2,4},{3,5},{10,6},{11,7},{4,8},{5,9},{12,... | collective-permute-start | bytes 1572872 | tf_op jit(solution)/shard_map/ppermute | solution.py:618
  (128 other events, 1309.6 us)

commit v2 on v1

v2 whole, which is shorter than its diff:
```python
import functools
import math

import jax
import jax.numpy as jnp
from jax import lax
from jax.experimental import pallas as pl
from jax.experimental.pallas import tpu as pltpu
from jax.sharding import Mesh
from jax.sharding import PartitionSpec as P

HEADS = 16
HEAD_DIM = 64
EPSILON = 1e-05
NEGATIVE = -1e30
LOG2E = math.log2(math.e)
AXES = ("j", "h", "c", "a", "b")
BF = jnp.bfloat16
F32 = jnp.float32
NT = (((1,), (1,)), ((), ()))
NN = (((1,), (0,)), ((), ()))
TN = (((0,), (0,)), ((), ()))


def cost(us):
    return pl.CostEstimate(flops=int(us * 1e6), bytes_accessed=1 << 10, transcendentals=0)


def dot(left, right, dims=NN):
    return lax.dot_general(left, right, dims, preferred_element_type=F32)


def qkv_kernel(table, order, *refs, group, shape):
    x_refs = refs[:group]
    w_in_ref, vec_ref, cos_ref, sin_ref, n_ref, q_ref, k_ref, v_ref, w_ref, held = refs[group:]
    step = pl.program_id(0)

    @pl.when(step == 0)
    def _():
        if shape is None:
            w_ref[...] = w_in_ref[...]
            return
        na, nb, part = shape
        for n in range(w_in_ref.shape[0]):
            j, a = order[n] // na, order[n] % na
            for m in range(group):
                row = ((j * (group // nb) + m // nb) * na + a) * nb + m % nb
                start = pl.multiple_of(row * part, part)
                w_ref[pl.ds(start, part), :] = w_in_ref[n, m * part : (m + 1) * part, :]

    for n in range(group):

        @pl.when(step // 2 == n)
        def _(n=n):
            held[...] = x_refs[n][step % 2]

    x = held[...].astype(F32)
    center = x - jnp.mean(x, axis=1, keepdims=True)
    rstd = lax.rsqrt(jnp.mean(center * center, axis=1, keepdims=True) + EPSILON)
    normed = (center * rstd * vec_ref[0:1] + vec_ref[1:2]).astype(BF)
    n_ref[...] = normed
    full = dot(normed, w_ref[...])
    lane = lax.broadcasted_iota(jnp.int32, (1, 128), 1)
    first = (lane % HEAD_DIM) < HEAD_DIM // 2
    cosine, sine = cos_ref[...], sin_ref[...]
    for pair in range(q_ref.shape[1] // 128):
        at = slice(pair * 128, (pair + 1) * 128)
        for which, out, scale in ((0, q_ref, LOG2E * HEAD_DIM**-0.5), (1, k_ref, 1.0)):
            t = full[:, (3 * pair + which) * 128 : (3 * pair + which + 1) * 128]
            other = jnp.where(first, pltpu.roll(t, 96, 1), pltpu.roll(t, 32, 1))
            out[:, at] = ((t * cosine + other * sine) * scale).astype(BF)
        v_ref[:, at] = full[:, (3 * pair + 2) * 128 : (3 * pair + 3) * 128].astype(BF)


def qkv_call(table, order, pieces, w, vec, cosine, sine, shape):
    group = len(pieces)
    _, rows, model = pieces[0].shape
    width = model // group
    length = 2 * group * rows
    at = lambda i, *t: (t[0][i], 0)
    fixed = lambda shape: pl.BlockSpec(
        shape, lambda i, *t: (0,) * len(shape), pipeline_mode=pl.Buffered(1)
    )
    return pl.pallas_call(
        functools.partial(qkv_kernel, group=group, shape=shape),
        out_shape=[jax.ShapeDtypeStruct((length, model), BF)]
        + [jax.ShapeDtypeStruct((length, width), BF)] * 3
        + [jax.ShapeDtypeStruct((model, 3 * width), BF)],
        grid_spec=pltpu.PrefetchScalarGridSpec(
            num_scalar_prefetch=2,
            grid=(2 * group,),
            in_specs=[fixed((2, rows, model))] * group
            + [fixed(w.shape), fixed(vec.shape)]
            + [pl.BlockSpec((rows, 128), at)] * 2,
            out_specs=[pl.BlockSpec((rows, model), at)]
            + [pl.BlockSpec((rows, width), at)] * 3
            + [fixed((model, 3 * width))],
            scratch_shapes=[pltpu.VMEM((rows, model), BF)],
        ),
        compiler_params=pltpu.CompilerParams(
            dimension_semantics=("arbitrary",), vmem_limit_bytes=60 << 20
        ),
        cost_estimate=cost(11),
        name="qkv",
    )(table, order, *pieces, w, vec, cosine, sine)


def forward_kernel(table, q_ref, k_ref, v_ref, o_ref, lse_ref, vaug, *, bq, bk, rows):
    i = pl.program_id(1)
    lane = lax.broadcasted_iota(jnp.int32, (1, 128), 1)
    low = lane < HEAD_DIM

    @pl.when(i == 0)
    def _():
        v = v_ref[...]
        one = jnp.ones_like(v)
        vaug[0] = jnp.where(low, v, one)
        vaug[1] = jnp.where(low, one, v)

    parts = bq // bk
    heads = []
    for n in range(parts):
        q = q_ref[n * bk : (n + 1) * bk, :]
        zero = jnp.zeros_like(q)
        heads.append((jnp.where(low, q, zero), jnp.where(low, zero, q)))

    def step(kb, carry, first, masked):
        start = pl.multiple_of(kb * bk, bk)
        k_blk = k_ref[pl.ds(start, bk), :]
        out = list(carry)
        for n in range(first, parts):
            for h in range(2):
                top, acc = carry[2 * n + h]
                s = dot(heads[n][h], k_blk, NT)
                if masked and n == first:
                    row = lax.broadcasted_iota(jnp.int32, s.shape, 0)
                    col = lax.broadcasted_iota(jnp.int32, s.shape, 1)
                    s = jnp.where(col <= row, s, NEGATIVE)
                new = jnp.maximum(top, jnp.max(s, axis=1, keepdims=True))
                p = jnp.exp2(s - new)
                acc = acc * jnp.exp2(top - new) + dot(p.astype(BF), vaug[h, pl.ds(start, bk), :])
                out[2 * n + h] = (new, acc)
        return tuple(out)

    carry = tuple(
        (jnp.full((bk, 1), NEGATIVE, F32), jnp.zeros((bk, 128), F32)) for _ in range(2 * parts)
    )
    full = i * parts
    carry = lax.fori_loop(0, full, lambda kb, c: step(kb, c, 0, False), carry)
    for d in range(parts):
        carry = step(full + d, carry, d, True)
    for n in range(parts):
        (top0, acc0), (top1, acc1) = carry[2 * n : 2 * n + 2]
        total = pltpu.roll(jnp.where(low, acc1, acc0), HEAD_DIM, 1)
        o = (jnp.where(low, acc0, acc1) / total).astype(BF)
        for d in range(bk // rows):
            o_ref[table[(full + n) * (bk // rows) + d]] = o[d * rows : (d + 1) * rows]
        lse_ref[n * bk : (n + 1) * bk, :] = jnp.where(low, top0, top1) + jnp.log2(total)


def attention_forward(table, q, k, v, rows):
    length, width = q.shape
    bq, bk = min(2048, length), min(512, length)
    blocks = length // rows
    return pl.pallas_call(
        functools.partial(forward_kernel, bq=bq, bk=bk, rows=rows),
        out_shape=[
            jax.ShapeDtypeStruct((blocks, rows, width), BF),
            jax.ShapeDtypeStruct((length, width), F32),
        ],
        grid_spec=pltpu.PrefetchScalarGridSpec(
            num_scalar_prefetch=1,
            grid=(width // 128, length // bq),
            in_specs=[
                pl.BlockSpec((bq, 128), lambda p, i, t: (i, p)),
                pl.BlockSpec((length, 128), lambda p, i, t: (0, p)),
                pl.BlockSpec((length, 128), lambda p, i, t: (0, p)),
            ],
            out_specs=[
                pl.BlockSpec((blocks, rows, 128), lambda p, i, t: (0, 0, p)),
                pl.BlockSpec((bq, 128), lambda p, i, t: (i, p)),
            ],
            scratch_shapes=[pltpu.VMEM((2, length, 128), BF)],
        ),
        compiler_params=pltpu.CompilerParams(
            dimension_semantics=("arbitrary", "arbitrary"), vmem_limit_bytes=60 << 20
        ),
        cost_estimate=cost(23),
        name="attention_forward",
    )(table, q, k, v)


def split3(x):
    high = x.astype(BF)
    rest = x - high.astype(F32)
    mid = rest.astype(BF)
    return high, mid, (rest - mid.astype(F32)).astype(BF)


def backward_kernel(
    table, q_ref, k_ref, v_ref, o_ref, do_ref, lse_ref, cos_ref, sin_ref, ck_ref, sk_ref,
    d_ref, qa, da, dqt, *, bk, rows
):
    j = pl.program_id(0)
    length = q_ref.shape[0]
    lane = lax.broadcasted_iota(jnp.int32, (1, 128), 1)
    low = lane < HEAD_DIM
    first = (lane % HEAD_DIM) < HEAD_DIM // 2

    def unturn(t, cosine, sine):
        other = jnp.where(first, pltpu.roll(t, 96, 1), pltpu.roll(t, 32, 1))
        return t * cosine - other * sine

    @pl.when(j == 0)
    def _():
        dqt[...] = jnp.zeros_like(dqt)

        def prep(b, _):
            r = pl.ds(pl.multiple_of(b * rows, rows), rows)
            q, do = q_ref[r, :], do_ref[table[b]]
            product = o_ref[table[b]].astype(F32) * do.astype(F32)
            for h in range(2):
                mine = low if h == 0 else jnp.logical_not(low)
                base = HEAD_DIM if h == 0 else 0
                delta = -jnp.sum(jnp.where(mine, product, 0.0), axis=1, keepdims=True)
                lse = -lse_ref[r, HEAD_DIM * h : HEAD_DIM * h + 1]
                for source, value, target in ((q, lse, qa), (do, delta, da)):
                    x = jnp.where(mine, source, jnp.zeros_like(source))
                    for n, part in enumerate(split3(value)):
                        x = jnp.where(lane == base + n, part, x)
                    target[h, r, :] = x
            return 0

        lax.fori_loop(0, length // rows, prep, 0)

    k, v = k_ref[...], v_ref[...]
    one, zero = jnp.ones_like(k), jnp.zeros_like(k)
    ka, va, kt = [], [], []
    for h in range(2):
        mine = low if h == 0 else jnp.logical_not(low)
        base = HEAD_DIM if h == 0 else 0
        extra = jnp.where(jnp.logical_and(lane >= base, lane < base + 3), one, zero)
        ka.append(jnp.where(mine, k, extra))
        va.append(jnp.where(mine, v, extra))
        kt.append(jnp.where(mine, k, zero).T)

    def products(h, keys, r, masked):
        qh, dh = qa[h, r, :], da[h, r, :]
        st = dot(ka[h][keys], qh, NT)
        if masked:
            key = lax.broadcasted_iota(jnp.int32, st.shape, 0)
            query = lax.broadcasted_iota(jnp.int32, st.shape, 1)
            st = jnp.where(key <= query, st, NEGATIVE)
        p = jnp.exp2(st)
        ds = (p * dot(va[h][keys], dh, NT)).astype(BF)
        return dot(ds, qh), dot(p.astype(BF), dh), ds

    def step(qb, carry):
        r = pl.ds(pl.multiple_of(qb * bk, bk), bk)
        out, low_scores = [], []
        for h in range(2):
            dk, dv, ds = products(h, slice(None), r, False)
            out.append((carry[h][0] + dk, carry[h][1] + dv))
            low_scores.append(ds)
        dqt[:, r] += dot(kt[0], low_scores[0]) + dot(kt[1], low_scores[1])
        return tuple(out)

    half = bk // 2
    carry = []
    upper = pl.ds(pl.multiple_of(j * bk, bk), bk)
    lower = pl.ds(pl.multiple_of(j * bk + half, half), half)
    firsts = [products(h, slice(0, half), upper, True) for h in range(2)]
    seconds = [products(h, slice(half, bk), lower, True) for h in range(2)]
    for h in range(2):
        carry.append(
            tuple(jnp.concatenate([firsts[h][n], seconds[h][n]], axis=0) for n in range(2))
        )
    dqt[:, upper] += dot(kt[0][:, :half], firsts[0][2]) + dot(kt[1][:, :half], firsts[1][2])
    dqt[:, lower] += dot(kt[0][:, half:], seconds[0][2]) + dot(kt[1][:, half:], seconds[1][2])
    carry = lax.fori_loop(j + 1, length // bk, step, tuple(carry))
    (dk0, dv0), (dk1, dv1) = carry
    dk = unturn(jnp.where(low, dk0, dk1) * (1.0 / LOG2E), ck_ref[...], sk_ref[...])
    mine = pl.ds(pl.multiple_of(j * bk, bk), bk)
    d_ref[mine, 128:256] = dk.astype(BF)
    d_ref[mine, 256:384] = jnp.where(low, dv0, dv1).astype(BF)

    @pl.when(j == pl.num_programs(0) - 1)
    def _():
        dq = dqt[...].T * HEAD_DIM**-0.5
        d_ref[:, 0:128] = unturn(dq, cos_ref[...], sin_ref[...]).astype(BF)


def attention_backward(table, pair, q, k, v, o, do, lse, cosine, sine):
    length = q.shape[0]
    blocks, rows, _ = o.shape
    bk = min(512, length)
    full = pl.BlockSpec((length, 128), lambda j, t: (0, pair))
    block = pl.BlockSpec((bk, 128), lambda j, t: (j, pair))
    loose = pl.BlockSpec((blocks, rows, 128), lambda j, t: (0, 0, pair))
    return pl.pallas_call(
        functools.partial(backward_kernel, bk=bk, rows=rows),
        out_shape=jax.ShapeDtypeStruct((length, 384), BF),
        grid_spec=pltpu.PrefetchScalarGridSpec(
            num_scalar_prefetch=1,
            grid=(length // bk,),
            in_specs=[
                full, block, block, loose, loose, full,
                pl.BlockSpec((length, 128), lambda j, t: (0, 0)),
                pl.BlockSpec((length, 128), lambda j, t: (0, 0)),
                pl.BlockSpec((bk, 128), lambda j, t: (j, 0)),
                pl.BlockSpec((bk, 128), lambda j, t: (j, 0)),
            ],
            out_specs=pl.BlockSpec((length, 384), lambda j, t: (0, 0)),
            scratch_shapes=[
                pltpu.VMEM((2, length, 128), BF),
                pltpu.VMEM((2, length, 128), BF),
                pltpu.VMEM((128, length), F32),
            ],
        ),
        compiler_params=pltpu.CompilerParams(
            dimension_semantics=("arbitrary",), vmem_limit_bytes=56 << 20
        ),
        cost_estimate=cost(44),
        name="attention_backward",
    )(table, q, k, v, o, do, lse, cosine, sine, cosine, sine)


def gelu(v):
    return 0.5 * v * (1.0 + jnp.tanh(0.7978845608 * (v + 0.044715 * v * v * v)))


def gelu_slope(v):
    square = v * v
    t = jnp.tanh(0.7978845608 * v * (1.0 + 0.044715 * square))
    inner = 0.7978845608 * (1.0 + 3.0 * 0.044715 * square)
    return 0.5 * (1.0 + t) + 0.5 * v * (1.0 - t * t) * inner


def load_weights(order, weight_refs, up, down):
    if order is None:
        up[...], down[...] = weight_refs[0][...], weight_refs[1][...]
        return
    half = pl.program_id(0)
    ups, downs = weight_refs[:2], weight_refs[2:]
    sources, rows, _ = ups[0].shape
    part, cut = rows // 2, downs[0].shape[1]
    per = down.shape[0] // (2 * cut)
    for which in range(2):

        @pl.when(half == which)
        def _(which=which):
            for n in range(sources):
                source = order[which, n]
                base = (source // per) * 2 * per + source % per
                for c in range(2):
                    start = pl.multiple_of((base + c * per) * part, part)
                    up[pl.ds(start, part), :] = ups[which][n, c * part : (c + 1) * part, :]

        for n in range(sources):
            source = order[which, n]

            @pl.when(source // per == half)
            def _(n=n, source=source, which=which):
                start = pl.multiple_of(((source % per) * 2 + which) * cut, cut)
                down[pl.ds(start, cut), :] = downs[which][n]


def take(step, refs, held):
    for n, ref in enumerate(refs):

        @pl.when(step == n)
        def _(ref=ref):
            held[...] = ref[...].reshape(held.shape)

    return held[...]


def add_halves(term, own_ref, other_ref, total):
    half, tile = pl.program_id(0), pl.program_id(1)

    @pl.when(half == 0)
    def _():
        total[tile] = term

    @pl.when(half != 0)
    def _():
        total[tile] += term

    @pl.when(jnp.logical_and(half == pl.num_programs(0) - 1, tile == 0))
    def _():
        own_ref[...] = total[0]

    @pl.when(jnp.logical_and(half == pl.num_programs(0) - 1, tile == 1))
    def _():
        other_ref[...] = total[1].astype(BF)


def mlp_forward_kernel(*refs, tables):
    order = refs[0] if tables else None
    pre_ref, act_ref, own_ref, other_ref, up, down, held, total = refs[-8:]
    x_refs, weight_refs = refs[tables : tables + 2], refs[tables + 2 : -8]

    @pl.when(pl.program_id(1) == 0)
    def _():
        load_weights(order, weight_refs, up, down)

    pre = dot(take(pl.program_id(1), x_refs, held), up[...])
    act = gelu(pre).astype(BF)
    pre_ref[...] = pre.astype(BF)
    act_ref[...] = act
    add_halves(dot(act, down[...]), own_ref, other_ref, total)


def mlp_backward_kernel(*refs, tables):
    order = refs[0] if tables else None
    low_ref, own_ref, other_ref, up, down, held, total = refs[-7:]
    g_refs, pre_ref, weight_refs = refs[tables : tables + 2], refs[tables + 2], refs[tables + 3 : -7]

    @pl.when(pl.program_id(1) == 0)
    def _():
        load_weights(order, weight_refs, up, down)

    grad = dot(take(pl.program_id(1), g_refs, held), down[...], NT)
    low = (grad * gelu_slope(pre_ref[...].astype(F32))).astype(BF)
    low_ref[...] = low
    add_halves(dot(low, up[...], NT), own_ref, other_ref, total)


def mlp_call(kernel, name, us, narrow, wide, weights, halves, wide_outs):
    count, model = narrow[0].shape
    tables = weights[4:]
    fixed = lambda shape: pl.BlockSpec(
        shape, lambda f, m, *t: (0,) * len(shape), pipeline_mode=pl.Buffered(1)
    )
    if tables:
        sources, rows, _ = weights[0].shape
        unit = model
        specs = [fixed((sources, rows, model))] * 4
    else:
        unit = weights[1].shape[0] // halves
        specs = [
            pl.BlockSpec((model, unit), lambda f, m, *t: (0, f)),
            pl.BlockSpec((unit, model), lambda f, m, *t: (f, 0)),
        ]
    wide_spec = pl.BlockSpec((count, unit), lambda f, m, *t: (m, f))
    return pl.pallas_call(
        functools.partial(kernel, tables=len(tables)),
        out_shape=[jax.ShapeDtypeStruct((2 * count, halves * unit), BF)] * wide_outs
        + [jax.ShapeDtypeStruct((count, model), F32), jax.ShapeDtypeStruct((count, model), BF)],
        grid_spec=pltpu.PrefetchScalarGridSpec(
            num_scalar_prefetch=len(tables),
            grid=(halves, 2),
            in_specs=[fixed((count, model))] * 2 + [wide_spec] * len(wide) + specs,
            out_specs=[wide_spec] * wide_outs + [fixed((count, model))] * 2,
            scratch_shapes=[
                pltpu.VMEM((model, unit), BF),
                pltpu.VMEM((unit, model), BF),
                pltpu.VMEM((count, model), BF),
                pltpu.VMEM((2, count, model), F32),
            ],
        ),
        compiler_params=pltpu.CompilerParams(
            dimension_semantics=("arbitrary", "arbitrary"), vmem_limit_bytes=56 << 20
        ),
        cost_estimate=cost(us),
        name=name,
    )(*tables, *narrow, *wide, *weights[: 4 if tables else 2])


def mlp_forward(narrow, weights, halves):
    return mlp_call(mlp_forward_kernel, "mlp_forward", 18, narrow, [], weights, halves, 2)


def mlp_backward(narrow, pre, weights, halves):
    return mlp_call(mlp_backward_kernel, "mlp_backward", 20, narrow, [pre], weights, halves, 1)


def spread_of(values):
    center = values - jnp.mean(values, axis=1, keepdims=True)
    rstd = lax.rsqrt(jnp.mean(center * center, axis=1, keepdims=True) + EPSILON)
    return center * rstd, rstd


def norm_slope(hat, rstd, gain, grad, sums_ref, at):
    scaled = grad * gain
    inner = scaled - jnp.mean(scaled, axis=1, keepdims=True)
    sums_ref[at : at + 1] += jnp.sum(grad * hat, axis=0, keepdims=True)
    sums_ref[at + 1 : at + 2] += jnp.sum(grad, axis=0, keepdims=True)
    return rstd * (inner - hat * jnp.mean(scaled * hat, axis=1, keepdims=True))


def clear_at_start(ref):
    @pl.when(pl.program_id(0) == 0)
    def _():
        ref[...] = jnp.zeros_like(ref)


def out_kernel(order, places, *refs, group, views):
    projected_ref, residual_ref, normed_ref, w_ref, held = refs[-5:]
    mixed, tokens, vec_ref, weights = refs[:group], refs[group : group + 2], refs[group + 2], refs[group + 3 : -5]
    step = pl.program_id(0)

    @pl.when(step == 0)
    def _():
        if not views:
            w_ref[...] = weights[0][...]
            return
        sources, cut = weights[0].shape[0], weights[0].shape[1] // 2
        halves = places.shape[0] // 2
        per = sources // halves
        for which in range(2):
            for n in range(sources):
                source = order[which, n]
                start = pl.multiple_of((source % per) * 2 * cut + which * cut, cut)
                for core in range(2):
                    block = places[core * halves + source // per]
                    w_ref[block, pl.ds(start, cut), :] = weights[core][n, which * cut : (which + 1) * cut]

    projected = dot(mixed[0][...], w_ref[0])
    for d in range(1, group):
        projected = projected + dot(mixed[d][...], w_ref[d])
    projected_ref[...] = projected
    hat, _ = spread_of(projected)
    x = take(step, tokens, held).astype(F32)
    residual = x + hat * vec_ref[2:3] + vec_ref[3:4]
    residual_ref[...] = residual
    hat, _ = spread_of(residual)
    normed_ref[...] = (hat * vec_ref[4:5] + vec_ref[5:6]).astype(BF)


def out_projection(order, places, mixed, tokens, vec, weights, views):
    group = len(mixed)
    count, width = mixed[0].shape
    rows, model = tokens[0].shape
    fixed = lambda shape: pl.BlockSpec(shape, lambda i, *t: (0,) * len(shape))
    tall = pl.BlockSpec((rows, model), lambda i, *t: (i, 0))
    specs = [fixed(x.shape) for x in weights]
    return pl.pallas_call(
        functools.partial(out_kernel, group=group, views=views),
        out_shape=[
            jax.ShapeDtypeStruct((count, model), F32),
            jax.ShapeDtypeStruct((count, model), F32),
            jax.ShapeDtypeStruct((count, model), BF),
            jax.ShapeDtypeStruct((group, width, model), BF),
        ],
        grid_spec=pltpu.PrefetchScalarGridSpec(
            num_scalar_prefetch=2,
            grid=(count // rows,),
            in_specs=[pl.BlockSpec((rows, width), lambda i, *t: (i, 0))] * group
            + [fixed((rows, model))] * 2
            + [fixed(vec.shape)]
            + specs,
            out_specs=[tall, tall, tall, fixed((group, width, model))],
            scratch_shapes=[pltpu.VMEM((rows, model), BF)],
        ),
        compiler_params=pltpu.CompilerParams(
            dimension_semantics=("arbitrary",), vmem_limit_bytes=40 << 20
        ),
        cost_estimate=cost(5),
        name="out_projection",
    )(order, places, *mixed, *tokens, vec, *weights)


def middle_kernel(own_ref, came_ref, residual_ref, g0_ref, g1_ref, vec_ref, out_ref, low_ref, sums_ref, held):
    clear_at_start(sums_ref)
    hat, rstd = spread_of(own_ref[...] + came_ref[...].astype(F32))
    out_ref[...] = (residual_ref[...] + hat * vec_ref[6:7] + vec_ref[7:8]).astype(BF)
    grad = take(pl.program_id(0), (g0_ref, g1_ref), held).astype(F32)
    low_ref[...] = norm_slope(hat, rstd, vec_ref[6:7], grad, sums_ref, 6).astype(BF)


def turn_kernel(own_ref, came_ref, residual_ref, projected_ref, g0_ref, g1_ref, vec_ref, w_ref, *refs, group):
    grad_ref, low_ref, *heads, sums_ref, held = refs
    clear_at_start(sums_ref)
    hat, rstd = spread_of(residual_ref[...])
    grad = own_ref[...] + came_ref[...].astype(F32)
    passed = take(pl.program_id(0), (g0_ref, g1_ref), held).astype(F32)
    grad = passed + norm_slope(hat, rstd, vec_ref[4:5], grad, sums_ref, 4)
    grad_ref[...] = grad
    hat, rstd = spread_of(projected_ref[...])
    low = norm_slope(hat, rstd, vec_ref[2:3], grad, sums_ref, 2).astype(BF)
    low_ref[...] = low
    for d in range(group):
        heads[d][...] = dot(low, w_ref[d], NT).astype(BF)


def last_kernel(x_ref, grad_ref, *refs):
    *parts, vec_ref, out_ref, sums_ref = refs
    clear_at_start(sums_ref)
    hat, rstd = spread_of(x_ref[...].astype(F32))
    grad = parts[0][...].astype(F32)
    for part in parts[1:]:
        grad = grad + part[...].astype(F32)
    grad = norm_slope(hat, rstd, vec_ref[0:1], grad, sums_ref, 0)
    out_ref[...] = (grad_ref[...] + grad).astype(BF)


def row_call(kernel, name, us, rows, tall, halves, fixed, outs):
    model = tall[0].shape[1]
    count = tall[0].shape[0]
    whole = lambda x: pl.BlockSpec(x.shape, lambda i, n=x.ndim: (0,) * n)
    block = lambda width: pl.BlockSpec((rows, width), lambda i: (i, 0))
    return pl.pallas_call(
        kernel,
        out_shape=[jax.ShapeDtypeStruct((count, width), kind) for width, kind in outs]
        + [jax.ShapeDtypeStruct((8, model), F32)],
        grid=(count // rows,),
        in_specs=[block(model)] * len(tall) + [whole(x) for x in (*halves, *fixed)],
        out_specs=[block(width) for width, _ in outs] + [pl.BlockSpec((8, model), lambda i: (0, 0))],
        scratch_shapes=[pltpu.VMEM((rows, model), BF)] if halves else [],
        compiler_params=pltpu.CompilerParams(
            dimension_semantics=("arbitrary",), vmem_limit_bytes=40 << 20
        ),
        cost_estimate=cost(us),
        name=name,
    )(*tall, *halves, *fixed)


def input_grad_kernel(table, *refs):
    w_ref, give_ref, keep_ref = refs[-3:]
    total = None
    for n, ref in enumerate(refs[:-3]):
        term = dot(ref[...], w_ref[:, n * 384 : (n + 1) * 384], NT)
        total = term if total is None else total + term
    giving = pl.program_id(0) < pl.num_programs(0) // 2

    @pl.when(giving)
    def _():
        give_ref[0] = total.astype(BF)

    @pl.when(jnp.logical_not(giving))
    def _():
        keep_ref[0] = total.astype(BF)


def input_grad(table, grads, w, rows):
    model = w.shape[0]
    blocks = grads[0].shape[0] // rows
    half = blocks // 2
    return pl.pallas_call(
        input_grad_kernel,
        out_shape=[jax.ShapeDtypeStruct((half, rows, model), BF)] * 2,
        grid_spec=pltpu.PrefetchScalarGridSpec(
            num_scalar_prefetch=1,
            grid=(blocks,),
            in_specs=[pl.BlockSpec((rows, 384), lambda i, t: (t[i], 0))] * len(grads)
            + [pl.BlockSpec(w.shape, lambda i, t: (0, 0))],
            out_specs=[
                pl.BlockSpec((1, rows, model), lambda i, t: (jnp.minimum(i, half - 1), 0, 0)),
                pl.BlockSpec((1, rows, model), lambda i, t: (jnp.maximum(i - half, 0), 0, 0)),
            ],
        ),
        compiler_params=pltpu.CompilerParams(
            dimension_semantics=("arbitrary",), vmem_limit_bytes=40 << 20
        ),
        cost_estimate=cost(6),
        name="input_grad",
    )(table, *grads, w)


def head_sum_kernel(*refs, group, spread):
    x_refs, outs = refs[:-3], refs[-3:]
    width = outs[0].shape[1] // group
    for m in range(group):
        for pair, ref in enumerate(x_refs):
            total = None
            for n in spread(m):
                term = ref[n].astype(F32)
                total = term if total is None else total + term
            at = slice(m * width + pair * 128, m * width + (pair + 1) * 128)
            for which, out in enumerate(outs):
                out[:, at] = total[:, which * 128 : (which + 1) * 128]


def head_sum(parts, group, spread):
    _, rows, wide = parts[0].shape
    return pl.pallas_call(
        functools.partial(head_sum_kernel, group=group, spread=spread),
        out_shape=[jax.ShapeDtypeStruct((rows, group * len(parts) * wide // 3), F32)] * 3,
        cost_estimate=cost(2),
        name="head_sum",
    )(*parts)


def flip(x, axis, bit):
    size = lax.axis_size(axis)
    return lax.ppermute(x, axis, [(i, i ^ bit) for i in range(size)])


def scatter_sends(x, axis, dim, bit):
    here = (lax.axis_index(axis) // bit) % 2
    shape = x.shape
    x = x.reshape(shape[:dim] + (shape[dim] // 2, 2) + shape[dim + 1 :])
    mine = lax.dynamic_index_in_dim(x, here, dim + 1, keepdims=False)
    return mine, lax.dynamic_index_in_dim(x, 1 - here, dim + 1, keepdims=False)


def join(mine, came, kind=BF):
    return (mine.astype(F32) + came.astype(F32)).astype(kind)


def scatter_axis(x, axis, dim, bit=1, kind=BF):
    size = lax.axis_size(axis)
    while bit < size:
        mine, theirs = scatter_sends(x, axis, dim, bit)
        x = join(mine, flip(theirs, axis, bit), kind)
        bit *= 2
    return x.reshape(x.shape[:dim] + x.shape[dim + 1 :])


def together(*groups):
    flat, tree = jax.tree.flatten(groups)
    return jax.tree.unflatten(tree, lax.optimization_barrier(tuple(flat)))


def place_in(order):
    index = jnp.arange(order.shape[0], dtype=jnp.int32)
    return jnp.sum(jnp.where(order[:, None] == index[None, :], index[:, None], 0), axis=0)


def gather_order(axes):
    masks = {axis: [0] for axis in AXES}
    for axis in axes:
        bit = lax.axis_size(axis) // 2
        while bit:
            for name in AXES:
                step = bit if name == axis else 0
                masks[name] = masks[name] + [m ^ step for m in masks[name]]
            bit //= 2
    return {axis: jnp.array(masks[axis], jnp.int32) for axis in AXES}


def source_of(axes, along=("j", "h", "a", "b")):
    masks, total = gather_order(axes), 0
    for axis in along:
        total = total * lax.axis_size(axis) + (lax.axis_index(axis) ^ masks[axis])
    return total


def stages_of(axes):
    stages = []
    for axis in axes:
        bit = lax.axis_size(axis) // 2
        while bit:
            stages.append((axis, bit))
            bit //= 2
    return stages


def after(x, *others):
    return lax.optimization_barrier((x,) + others)[0]


def body(
    tokens, cotangent, w_query, w_key, w_value, w_output, w_up, w_down,
    attn_in_gain, attn_in_bias, attn_out_gain, attn_out_bias,
    mlp_in_gain, mlp_in_bias, mlp_out_gain, mlp_out_bias,
):
    _, rows, model = tokens.shape
    nh, na, nb = lax.axis_size("h"), lax.axis_size("a"), lax.axis_size("b")
    jh = 2 * nh
    devices = 4 * nh * na * nb
    group = 2 * nh * nb
    half = na // 2
    length = rows * na * nb
    width = model // group
    pairs = width // 128
    part = w_query.shape[0]
    ij, ih, ic, ia, ib = (lax.axis_index(axis) for axis in AXES)
    slot, parity = ia // half, ia % 2
    member = (ih * 2 + ic) * nb + ib

    def place(j, h, c, a, b):
        return (((j * nh + h) * 2 + c) * na + a) * nb + b

    everyone = [
        (j, h, c, a, b)
        for j in range(2)
        for h in range(nh)
        for c in range(2)
        for a in range(na)
        for b in range(nb)
    ]
    moves = ([], [])
    for turn in range(2):
        for j, h, c, a, b in everyone:
            to_h, to_c = divmod(a % half, 2)
            plane = (h * 2 + c) * 2 + (turn + a // half) % 2
            target = place(j, to_h, to_c, plane, b)
            moves[turn].append((place(j, h, c, a, b), target))

    def regroup(x, turn):
        x = lax.dynamic_index_in_dim(x, (turn + slot) % 2, 0, keepdims=False)
        return lax.ppermute(x, AXES, moves[turn])

    def restore(x, turn):
        return lax.ppermute(x, AXES, [(there, here) for here, there in moves[turn]])

    def ordered(first, second):
        swap = slot == 1
        return jnp.stack([jnp.where(swap, second, first), jnp.where(swap, first, second)])

    def by_offset(x, offset):
        sends = []
        for j, h, c, a, b in everyone:
            to_hc, to_b = divmod(((h * 2 + c) * nb + b) ^ offset, nb)
            sends.append((place(j, h, c, a, b), place(j, to_hc // 2, to_hc % 2, a, to_b)))
        return lax.ppermute(x, AXES, sends)

    core_bit = nb
    far_bits = [1 << n for n in range(group.bit_length() - 1) if (1 << n) != core_bit]

    ff = w_up.shape[1]
    unit = ff // (2 * jh)
    up_split = w_up.reshape(part, jh, 2, unit)
    up_mine = lax.dynamic_index_in_dim(up_split, ic, 2, keepdims=False)
    up_other = flip(lax.dynamic_index_in_dim(up_split, 1 - ic, 2, keepdims=False), "c", 1)
    up_rows = jnp.stack(
        [jnp.where(ic == 0, up_mine, up_other), jnp.where(ic == 0, up_other, up_mine)]
    )
    n_up, n_down = 2 * part * jh * unit // model, w_down.shape[0]
    views = unit == model and part % 32 == 0 and n_up == n_down
    up_rows = up_rows.transpose(2, 0, 1, 3).reshape(n_up, model)
    cut, cut_up, cut_out = n_down // 2, n_up // 2, part // 2

    line_stages = stages_of(("a",))
    low_axes, high_axes = ("b", "h", "j"), ("h", "j", "b")

    def grow(x, came):
        return jnp.concatenate([x, came])

    def grow_all(x, stages):
        for axis, bit in stages:
            x = grow(x, flip(x, axis, bit))
        return x

    first = jnp.concatenate([w_down[:cut], w_output[:cut_out], w_down[cut:], w_output[cut_out:]])
    first, second = first[None], up_rows[None]

    columns = jnp.stack(
        [w.reshape(part, group, pairs, 128) for w in (w_query, w_key, w_value)], axis=3
    ).reshape(part, group, 3 * width)
    columns = columns.transpose(1, 0, 2)
    columns = lax.all_to_all(columns, ("h", "c", "b"), 0, 0, tiled=True)
    columns = columns.reshape(1, group * part, 3 * width)

    blocks = 2 * group
    index = jnp.arange(blocks, dtype=jnp.int32)
    table = (member ^ (index % group)) * 2 + (parity ^ (index // group))
    positions_of = (parity ^ (index % 2)) * group + (member ^ (index // 2))
    lane = jnp.arange(128, dtype=jnp.int32)
    frequency = jnp.exp(
        (lane % (HEAD_DIM // 2)).astype(F32) * (-2.0 * math.log(10000.0) / HEAD_DIM)
    )
    angles = jnp.arange(length, dtype=jnp.int32).astype(F32)[:, None] * frequency[None, :]
    cosine = jnp.cos(angles)
    sine = jnp.sin(angles) * jnp.where((lane // (HEAD_DIM // 2)) % 2 == 0, -1.0, 1.0)[None, :]

    vectors = grow_all(
        jnp.stack(
            [attn_in_gain, attn_in_bias, attn_out_gain, attn_out_bias,
             mlp_in_gain, mlp_in_bias, mlp_out_gain, mlp_out_bias]
        )[None],
        stages_of(("c", "b", "h", "j", "a")),
    )
    vectors = vectors[place_in(source_of(("c", "b", "h", "j", "a"), AXES))]
    vectors = vectors.transpose(1, 0, 2).reshape(8, model).astype(F32)

    def columns_in_order(x):
        x = x[place_in(w_from)].reshape(2, na, nh, 2, nb, part, 3 * width)
        return x.transpose(0, 2, 3, 1, 4, 5, 6).reshape(model, 3 * width)

    own = [regroup(tokens, turn) for turn in range(2)]
    first_came = flip(first, *line_stages[0])
    w_came = flip(columns, *line_stages[0])
    first = grow_all(grow(first, first_came), line_stages[1:])
    wide = cut + cut_out
    low_stages, high_stages = stages_of(low_axes), stages_of(high_axes)
    first_low, first_high = first[:, :wide], first[:, wide:]
    own, first_low, first_high, w_came, second, cosine, sine, vectors = together(
        own, first_low, first_high, w_came, second, cosine, sine, vectors
    )
    columns = grow_all(grow(columns, w_came), line_stages[1:-1])
    second_came, w_came = flip(second, *line_stages[0]), flip(columns, *line_stages[-1])
    high_came = flip(first_high, *high_stages[0])
    pieces = {0: jnp.stack(own)}
    for bit in far_bits:
        for offset in list(pieces):
            pieces[offset ^ bit] = by_offset(pieces[offset], bit)
    pieces[core_bit] = by_offset(pieces[0], core_bit)
    pieces, high_came, second_came, w_came = together(pieces, high_came, second_came, w_came)
    second = grow_all(grow(second, second_came), line_stages[1:-1])
    columns = grow(columns, w_came)

    w_came = flip(columns, "j", 1)
    w_from = source_of(("a", "j"), ("j", "a"))
    low_came, second_came = flip(first_low, *low_stages[0]), flip(second, *line_stages[-1])
    for offset in range(1, group):
        if not offset & core_bit:
            pieces[offset ^ core_bit] = by_offset(pieces[offset], core_bit)
    pieces, w_came, low_came, second_came = together(pieces, w_came, low_came, second_came)
    columns = grow(columns, w_came)
    if views:
        w_heads, w_shape = columns, (na, nb, part)
    else:
        w_heads, w_shape = columns_in_order(columns), None
    first_low = grow_all(grow(first_low, low_came), low_stages[1:-1])
    first_high = grow_all(grow(first_high, high_came), high_stages[1:-1])
    second = grow(second, second_came)
    second_low, second_high = second[:, :cut_up], second[:, cut_up:]
    pieces, first_low, first_high, second_low, second_high = together(
        pieces, first_low, first_high, second_low, second_high
    )
    low_came, high_came = flip(first_low, *low_stages[-1]), flip(first_high, *high_stages[-1])
    up_low_came = flip(second_low, *low_stages[0])
    up_high_came = flip(second_high, *high_stages[0])
    normed, queries, keys, values, w_heads = qkv_call(
        positions_of, w_from, [pieces[d] for d in range(group)], w_heads, vectors,
        cosine, sine, w_shape,
    )
    attended, lse = attention_forward(table, queries, keys, values, rows)
    attended, lse, low_came, high_came, up_low_came, up_high_came, cotangent = together(
        attended, lse, low_came, high_came, up_low_came, up_high_came, cotangent
    )
    first_low, first_high = grow(first_low, low_came), grow(first_high, high_came)
    second_low = grow_all(grow(second_low, up_low_came), low_stages[1:])
    second_high = grow_all(grow(second_high, up_high_came), high_stages[1:])
    low_from, high_from = (source_of(("a",) + axes) for axes in (low_axes, high_axes))

    def exchange(x):
        return [x[0]] + [by_offset(x[d], d) for d in range(1, group)]

    order = jnp.stack([low_from, high_from])
    low_at, high_at = place_in(low_from), place_in(high_from)
    core_block = jnp.arange(2 * jh, dtype=jnp.int32)
    if views:
        mine = jnp.concatenate([first_low[:, cut:], first_high[:, cut:]], axis=1)
        out_weights = [mine, flip(mine, "c", 1)]
    else:
        mine = jnp.concatenate(
            [first_low[:, cut:][low_at], first_high[:, cut:][high_at]], axis=1
        ).reshape(jh, na * nb * part, model)
        other = flip(mine, "c", 1)
        w_out = jnp.where(
            ic == 0, jnp.stack([mine, other], axis=1), jnp.stack([other, mine], axis=1)
        ).reshape(group, width, model)
        out_weights = [w_out[member ^ jnp.arange(group)]]
    places = member ^ ((core_block % jh) * 2 + (ic ^ (core_block // jh)))
    mixed = exchange(attended.reshape(group, 2 * rows, width))
    projected, residual, mlp_mine, w_out = out_projection(
        order, places, mixed, own, vectors, out_weights, views
    )
    mlp_rows = [mlp_mine, flip(mlp_mine, "c", 1)]
    mlp_rows, second_low, second_high, cotangent = together(
        mlp_rows, second_low, second_high, cotangent
    )
    if views:
        weights = [second_low, second_high, first_low, first_high, order]
    else:
        up = jnp.concatenate([second_low[low_at], second_high[high_at]], axis=1)
        up = up.reshape(jh, na, nb, jh, 2, part, unit)
        up = up.transpose(0, 4, 1, 2, 5, 3, 6).reshape(model, jh * unit)
        down = [first_low[:, :cut][low_at], first_high[:, :cut][high_at]]
        weights = [up, jnp.concatenate(down, axis=1).reshape(jh * unit, model)]
    grad_in = [regroup(cotangent, turn) for turn in range(2)]
    pre_act, activated, branch, branch_other = mlp_forward(mlp_rows, weights, jh)
    branch, branch_other, grad_in = together(branch, branch_other, grad_in)
    block_loose, branch_mine, mo_sums = row_call(
        middle_kernel, "middle", 3, rows,
        [branch, flip(branch_other, "c", 1), residual], grad_in, [vectors],
        [(model, BF), (model, BF)],
    )
    branch_rows = [branch_mine, flip(branch_mine, "c", 1)]

    def sends(x, axis, dim):
        return scatter_sends(x, axis, dim, 1) if lax.axis_size(axis) > 1 else (x, None)

    def send(pair, axis):
        return None if pair[1] is None else flip(pair[1], axis, 1)

    def added(pair, came, shape):
        return (pair[0] if came is None else join(pair[0], came)).reshape(shape)

    down_part = dot(activated, jnp.concatenate(branch_rows), TN).astype(BF)
    down_part = down_part.reshape(2, nh, na, nb, n_down, model)
    low_sends = sends(down_part[..., :cut, :], "b", 3)
    high_sends = sends(down_part[..., cut:, :], "j", 0)
    branch_rows, low_sends, high_sends, block_loose = together(
        branch_rows, low_sends, high_sends, block_loose
    )
    low_came, high_came = send(low_sends, "b"), send(high_sends, "j")
    block_came = [restore(block_loose[:rows], 0), restore(block_loose[rows:], 1)]
    pre_low, grad_mlp, grad_other = mlp_backward(branch_rows, pre_act, weights, jh)
    pre_low, grad_mlp, grad_other, low_came, high_came = together(
        pre_low, grad_mlp, grad_other, low_came, high_came
    )
    grad_other = flip(grad_other, "c", 1)
    low_sends = sends(added(low_sends, low_came, (2, nh, na, cut, model)), "j", 0)
    high_sends = sends(added(high_sends, high_came, (nh, na, nb, cut, model)), "b", 2)
    grad_mlp, grad_other, low_sends, high_sends = together(
        grad_mlp, grad_other, low_sends, high_sends
    )
    low_came, high_came = send(low_sends, "j"), send(high_sends, "b")
    grad_residual, projected_low, *attended_low, turn_sums = row_call(
        functools.partial(turn_kernel, group=group), "turn", 6, rows,
        [grad_mlp, grad_other, residual, projected], grad_in, [vectors, w_out],
        [(model, F32), (model, BF)] + [(width, BF)] * group,
    )
    attended_low, pre_low, low_came, high_came, block_came = together(
        attended_low, pre_low, low_came, high_came, block_came
    )
    grad_heads = jnp.stack(exchange(attended_low)).reshape(blocks, rows, width)
    down_part = jnp.concatenate(
        [
            added(low_sends, low_came, (nh, na, cut, model)),
            added(high_sends, high_came, (nh, na, cut, model)),
        ],
        axis=2,
    )
    down_sends = sends(scatter_axis(down_part, "h", 0), "a", 0)
    up_part = dot(jnp.concatenate(mlp_rows), pre_low, TN).astype(BF)
    up_part = up_part.reshape(2, nh, 2, na, nb, part, jh * unit)
    low_sends = sends(up_part[:, :, 0], "j", 0)
    high_sends = sends(up_part[:, :, 1], "b", 3)
    grad_out = jnp.stack([dot(mixed[d], projected_low, TN).astype(BF) for d in range(group)])
    grad_out = jnp.stack(
        [lax.dynamic_index_in_dim(grad_out, member ^ m, 0, keepdims=False) for m in range(group)]
    ).reshape(2, nh, 2, na, nb, part, model)
    out_sends = sends(scatter_axis(grad_out, "c", 2), "j", 0)
    grad_heads, down_sends, low_sends, high_sends, out_sends = together(
        grad_heads, down_sends, low_sends, high_sends, out_sends
    )

    def backward(pair, grads):
        return attention_backward(
            table, pair, queries, keys, values, attended, grads, lse, cosine, sine
        )

    low_came, high_came = send(low_sends, "j"), send(high_sends, "b")
    down_came, out_came = send(down_sends, "a"), send(out_sends, "j")
    grad_pairs = [backward(0, grad_heads)]
    grad_pairs, down_came, low_came, high_came, out_came = together(
        grad_pairs, down_came, low_came, high_came, out_came
    )
    down_part = added(down_sends, down_came, (na // 2, n_down, model))
    down_sends = scatter_sends(down_part, "a", 0, 2)
    low_part = scatter_axis(added(low_sends, low_came, (nh, na, nb, part, jh * unit)), "h", 0)
    low_sends = sends(low_part, "b", 1)
    high_sends = sends(added(high_sends, high_came, (2, nh, na, part, jh * unit)), "j", 0)
    out_part = scatter_axis(added(out_sends, out_came, (nh, na, nb, part, model)), "h", 0)
    out_sends = sends(out_part, "b", 1)
    weight_pairs = [dot(normed, grad_pairs[0], TN).astype(BF)]
    heads_in = [
        lax.all_to_all(weight_pairs[0].reshape(devices, part, 384), AXES, 0, 0, tiled=True)
    ]
    if pairs > 1:
        grad_heads, down_sends, low_sends, high_sends, out_sends, weight_pairs = together(
            grad_heads, down_sends, low_sends, high_sends, out_sends, weight_pairs
        )
    down_came, low_came = flip(down_sends[1], "a", 2), send(low_sends, "b")
    high_came, out_came = send(high_sends, "j"), send(out_sends, "b")
    if pairs > 1:
        grad_pairs.append(backward(1, grad_heads))
    grads_give = [d for d in range(group) if d & core_bit]
    block_order = [2 * d + r for d in grads_give for r in range(2)]
    block_order += [2 * (d ^ core_bit) + r for d in grads_give for r in range(2)]
    grad_pairs, down_came, low_came, high_came, out_came, heads_in = together(
        grad_pairs, down_came, low_came, high_came, out_came, heads_in
    )
    grad_give, grad_keep = input_grad(
        positions_of[jnp.array(block_order, jnp.int32)], grad_pairs, w_heads, rows
    )
    grad_give, grad_keep, down_came, low_came, high_came, out_came, grad_pairs = together(
        grad_give, grad_keep, down_came, low_came, high_came, out_came, grad_pairs
    )
    give_came = by_offset(grad_give, core_bit)
    rest_part = jnp.concatenate(
        [
            added(low_sends, low_came, (na, part, jh * unit)),
            scatter_axis(added(high_sends, high_came, (nh, na, part, jh * unit)), "h", 0),
            added(out_sends, out_came, (na, part, model)),
        ],
        axis=2,
    )
    rest_sends = sends(rest_part, "a", 0)
    give_came, rest_sends, grad_keep = together(give_came, rest_sends, grad_keep)
    rest_came = send(rest_sends, "a")

    grad_keep = join(grad_keep, give_came)
    sums = {
        d ^ core_bit: [grad_keep[2 * n + r] for r in range(2)] for n, d in enumerate(grads_give)
    }
    for bit in far_bits[:-1]:
        for d in [d for d in sums if d & bit]:
            gone = sums.pop(d)
            for r in range(2):
                sums[d ^ bit][r] = join(sums[d ^ bit][r], by_offset(gone[r], bit))
    sums, grad_pairs = together(sums, grad_pairs)
    if far_bits:
        final = [by_offset(x, far_bits[-1]) for x in sums[far_bits[-1]]]
    weight_pairs = [dot(normed, x, TN).astype(BF) for x in grad_pairs[1:]]
    if far_bits:
        final[0], rest_came, down_came, block_came = together(
            final[0], rest_came, down_came, block_came
        )
    for x in weight_pairs:
        heads_in.append(lax.all_to_all(x.reshape(devices, part, 384), AXES, 0, 0, tiled=True))
    rest_part = added(rest_sends, rest_came, (na // 2, part, -1))
    rest_part = scatter_axis(rest_part, "a", 0, 2)
    down_part = join(down_sends[0], down_came).reshape(na // 4, n_down, model)
    down_part = scatter_axis(down_part, "a", 0, 4)
    block_out = ordered(*block_came)

    small, grad_tokens = mo_sums + turn_sums, []
    for r in range(2):
        parts = [sums[0][r]] + ([final[r]] if far_bits else [])
        total, sums_in = row_call(
            last_kernel, "last", 2, rows,
            [own[r], grad_residual[r * rows : (r + 1) * rows]] + parts, [], [vectors],
            [(model, BF)],
        )
        small = small + sums_in
        if r == 0 and far_bits:
            total, final[1] = together(total, final[1])
        grad_tokens.append(restore(total, r))
    grad_tokens = ordered(*grad_tokens)

    def spread(m):
        hc, b = divmod(m, nb)
        return [place(j, hc // 2, hc % 2, a, b) for j in range(2) for a in range(na)]

    g_query, g_key, g_value = head_sum(heads_in, group, spread)
    g_down, g_out = down_part.astype(F32), rest_part[:, 2 * jh * unit :].astype(F32)
    up_part = jnp.stack([rest_part[:, n * jh * unit : (n + 1) * jh * unit] for n in range(2)])
    up_keep = lax.dynamic_index_in_dim(up_part, ic, 0, keepdims=False).reshape(part, jh, unit)
    up_give = lax.dynamic_index_in_dim(up_part, 1 - ic, 0, keepdims=False)
    up_come = flip(up_give, "c", 1).reshape(part, jh, unit)
    g_up = jnp.where(
        ic == 0, jnp.stack([up_keep, up_come], axis=2), jnp.stack([up_come, up_keep], axis=2)
    ).reshape(part, ff).astype(F32)

    small = small.reshape(8, 2, nh, 2, na, nb, part).transpose(3, 5, 1, 2, 4, 0, 6)
    for axis in ("c", "b", "j", "h", "a"):
        small = scatter_axis(small, axis, 0, kind=F32)
    return (
        block_out, grad_tokens, g_query, g_key, g_value, g_out, g_up, g_down,
        small[0], small[1], small[2], small[3], small[4], small[5], small[6], small[7],
    )


def solution(mesh):
    fsdp, seq = mesh.shape["fsdp"], mesh.shape["seq"]
    inner = Mesh(mesh.devices.reshape(2, fsdp // 4, 2, fsdp, seq // fsdp), AXES)
    lead, line = ("j", "h", "c"), ("a", "b")
    acts = P(lead, line, None)
    weights = P(lead + line, None)
    vector = P(lead + line)
    return jax.shard_map(
        body,
        mesh=inner,
        in_specs=(acts,) * 2 + (weights,) * 6 + (vector,) * 8,
        out_specs=(acts,) * 2 + (weights,) * 6 + (vector,) * 8,
        check_vma=False,
    )
```

time: 591 us -> 538 us (0.910)
  local copies, waits for them, and re-layouts: 73.6 us -> 48.9 us
  other arithmetic: 64.2 us -> 43.9 us
  waiting for transfers between devices: 166 us -> 148 us
  Pallas kernels: 138 us -> 150 us
  matrix products: 31.6 us -> 20.7 us
  starting transfers between devices: 106 us -> 115 us
    ppermute x37 -> x47, waiting for transfers between devices: 125 us -> 92.2 us  [flip(): return lax.ppermute(x, axis, [(i, i ^ bit) for i in range(size)])]
    ppermute x18 -> x12, waiting for transfers between devices: 27.2 us -> 52.7 us  [by_offset(): return lax.ppermute(x, AXES, sends)]
    ppermute x37 -> x47, starting transfers between devices: 35.1 us -> 59.9 us  [flip(): return lax.ppermute(x, axis, [(i, i ^ bit) for i in range(size)])]
    all_to_all x3 -> x1, starting transfers between devices: 24.3 us -> 3.64 us  [body(): columns = lax.all_to_all(columns, ('h', 'c', 'b'), 0, 0, tiled=True)]
    pallas_call x6 -> x11, Pallas kernels: 113 us -> 128 us  [the longest x2 48.9 us: attention_backward(): pl.pallas_call(functools.partial(backward_kernel, bk=bk, rows=rows), out_...]
    reduce_sum x13 -> x0, other arithmetic: 15.1 us -> none  [the longest x4 10.6 us: norm_backward(): return (rstd * inner, jnp.sum(grad * xhat, axis=0), jnp.sum(grad, axis=0))]
    all_to_all x3 -> x1, waiting for transfers between devices: 14.1 us -> 0.01 us  [body(): columns = lax.all_to_all(columns, ('h', 'c', 'b'), 0, 0, tiled=True)]
    another operation x11 -> x2, local copies, waits for them, and re-layouts: 12.6 us -> 0.04 us  [the longest x1 0.02 us: body(): jnp.stack([rest_part[:, n * jh * unit:(n + 1) * jh * unit] for n in range...]
  transfers between devices with their start and end apart: 68 -> 70, of which waited for: 20 -> 26; matrix products, arithmetic and copies ran while one was open for 20% -> 15% of each run, Pallas kernels for 20% -> 26%
where the time goes in v2:
time: 538 us; the launch traced here: 530 us
  Pallas kernels  150 us (28%)
  waiting for transfers between devices  148 us (28%)
  starting transfers between devices  115 us (21%)
  local copies, waits for them, and re-layouts  48.9 us (9%)
  other arithmetic  43.9 us (8%)
  matrix products  20.7 us (4%)
    ppermute x47, waiting for transfers between devices, flip(): return lax.ppermute(x, axis, [(i, i ^ bit) for i in range(size)])  92.2 us
    ppermute x47, starting transfers between devices, flip(): return lax.ppermute(x, axis, [(i, i ^ bit) for i in range(size)])  59.9 us
    ppermute x12, waiting for transfers between devices, by_offset(): return lax.ppermute(x, AXES, sends)  52.7 us
    pallas_call x2, Pallas kernels, attention_backward(): pl.pallas_call(functools.partial(backward_kernel, bk=bk, rows=rows), out_...  48.9 us
    pallas_call x2, Pallas kernels, mlp_call(): pl.pallas_call(functools.partial(kernel, tables=len(tables)), out_shape=[...  41.4 us
    ppermute x12, starting transfers between devices, by_offset(): return lax.ppermute(x, AXES, sends)  21.4 us
    dot_general x8, matrix products, dot(): return lax.dot_general(left, right, dims, preferred_element_type=F32)  20.7 us
    pallas_call x1, Pallas kernels, attention_forward(): pl.pallas_call(functools.partial(forward_kernel, bq=bq, bk=bk, rows=rows)...  19.8 us
  transfers between devices with their start and end apart: 70, of which 26 were waited for; matrix products, arithmetic and copies ran while one was open for 15% of the time, Pallas kernels for 26%

profile of v2, /device:TPU:1, one launch (start us, length us, event | category | flops | bytes accessed | tf_op | source)
XLA Modules:
  0.0 529.7 jit_solution(14760011597108021874)
XLA Ops:
  3.2 5.7 %collective-permute-start = (bf16[256,1024]{1,0:T(8,128)(2,1)}, bf16[256,1024]{1,0:T(8,128)(2,1)S(1)}, u32[]{:S(2)}, u32[]{:S(2)}) collective-permute-start(bf16[256,1024]{1,0:T(8,128)(2,1)} %get-tuple-element.393), channel_id=1, source_target_pairs={{0,0},{1,1},{2,8},{3,9},{4,2},{5,3},{6,10},{7,11},{8,4},{9,5},{10,... | collective-permute-start | bytes 1572872 | tf_op jit(solution)/shard_map/ppermute | solution.py:794
  18.8 5.6 %fusion.11 = (f32[2048,128]{1,0:T(8,128)}, f32[2048,128]{1,0:T(8,128)}) fusion(f32[128]{0:T(128)S(1)} %get-tuple-element.436, f32[128]{0:T(128)S(1)} %get-tuple-element.437, f32[2048]{0:T(1024)S(1)} %iota_convert_fusion), kind=kLoop, calls=%fused_computation.43 | loop fusion | flops 524288 | bytes 2106368 | tf_op jit(solution)/shard_map/mul | solution.py:857
  32.6 6.7 %collective-permute-done.9 = bf16[8,8,32]{2,1,0:T(8,128)(2,1)S(1)} collective-permute-done((bf16[8,8,32]{2,1,0:T(8,128)(2,1)S(1)}, bf16[8,8,32]{2,1,0:T(8,128)(2,1)S(1)}, u32[]{:S(2)}, u32[]{:S(2)}) %collective-permute-start.9) | collective-permute-done | bytes 4128 | tf_op jit(solution)/shard_map/ppermute | solution.py:687
  39.8 7.3 %collective-permute-start.10 = (bf16[16,8,32]{2,1,0:T(8,128)(2,1)S(1)}, bf16[16,8,32]{2,1,0:T(8,128)(2,1)S(1)}, u32[]{:S(2)}, u32[]{:S(2)}) collective-permute-start(bf16[16,8,32]{2,1,0:T(8,128)(2,1)S(1)} %get-tuple-element.412), channel_id=1, source_target_pairs={{0,2},{2,0},{4,6},{6,4},{1,3},{3,1},{5,7},{7,5},{8,10},{10,8},{12,... | collective-permute-start | bytes 24584 | tf_op jit(solution)/shard_map/ppermute | solution.py:687
  56.7 9.0 %collective-permute-done.3 = bf16[2,160,1024]{2,1,0:T(8,128)(2,1)S(1)} collective-permute-done((bf16[2,160,1024]{2,1,0:T(8,128)(2,1)S(1)}, bf16[2,160,1024]{2,1,0:T(8,128)(2,1)S(1)}, u32[]{:S(2)}, u32[]{:S(2)}) %collective-permute-start.3) | collective-permute-done | bytes 655392 | tf_op jit(solution)/shard_map/ppermute | solution.py:687
  75.0 11.6 %collective-permute-done.14 = bf16[1,128,1024]{2,1,0:T(8,128)(2,1)S(1)} collective-permute-done((bf16[1,128,1024]{2,1,0:T(8,128)(2,1)S(1)}, bf16[1,128,1024]{2,1,0:T(8,128)(2,1)S(1)}, u32[]{:S(2)}, u32[]{:S(2)}) %collective-permute-start.14) | collective-permute-done | bytes 262176 | tf_op jit(solution)/shard_map/ppermute | solution.py:687
  98.8 10.4 %collective-permute-done.18 = bf16[4,80,1024]{2,1,0:T(8,128)(2,1)S(1)} collective-permute-done((bf16[4,80,1024]{2,1,0:T(8,128)(2,1)S(1)}, bf16[4,80,1024]{2,1,0:T(8,128)(2,1)S(1)}, u32[]{:S(2)}, u32[]{:S(2)}) %collective-permute-start.18) | collective-permute-done | bytes 655392 | tf_op jit(solution)/shard_map/ppermute | solution.py:687
  119.5 13.9 %qkv.1 = (bf16[2048,1024]{1,0:T(8,128)(2,1)}, bf16[2048,256]{1,0:T(8,128)(2,1)}, bf16[2048,256]{1,0:T(8,128)(2,1)}, bf16[2048,256]{1,0:T(8,128)(2,1)}, bf16[1024,768]{1,0:T(8,128)(2,1)}) custom-call(s32[8]{0:T(128)} %get-tuple-element.434.table, s32[8]{0:T(128)} %xor_add_fusion.3.order, bf16[2,256,1024]{2,1,0:T(8,128)(2,1)} %copy-done.42, ...), custom_call_target="tpu_custom_call" | custom-call | flops 11000000 | bytes 1024 | tf_op jit(solution)/shard_map/qkv/pallas_call | solution.py:84
  133.4 19.8 %attention_forward.1 = (bf16[8,256,256]{2,1,0:T(8,128)(2,1)}, f32[2048,256]{1,0:T(8,128)}) custom-call(s32[8]{0:T(128)} %get-tuple-element.435.table, bf16[2048,256]{1,0:T(8,128)(2,1)} %get-tuple-element.205.q_ref, bf16[2048,256]{1,0:T(8,128)(2,1)} %get-tuple-element.206.k_ref, bf16[2048,256]{1,0:T(8,128)(2,1)} %get-tuple-element.207.v_ref), custom_call_target="tpu_custom_call" | custom-call | flops 23000000 | bytes 1024 | tf_op jit(solution)/shard_map/attention_forward/pallas_call | solution.py:165
  169.8 27.4 %collective-permute-done.26.refs_3_ = bf16[512,256]{1,0:T(8,128)(2,1)S(1)} collective-permute-done((bf16[512,256]{1,0:T(8,128)(2,1)S(1)}, bf16[512,256]{1,0:T(8,128)(2,1)S(1)}, u32[]{:S(2)}, u32[]{:S(2)}) %collective-permute-start.26) | collective-permute-done | bytes 262176 | tf_op jit(solution)/shard_map/ppermute | solution.py:808
  216.7 20.1 %mlp_forward.1 = (bf16[1024,2048]{1,0:T(8,128)(2,1)}, bf16[1024,2048]{1,0:T(8,128)(2,1)}, f32[512,1024]{1,0:T(8,128)}, bf16[512,1024]{1,0:T(8,128)(2,1)}) custom-call(s32[2,16]{1,0:T(2,128)} %copy-done.28, bf16[512,1024]{1,0:T(8,128)(2,1)} %copy-done.18, bf16[512,1024]{1,0:T(8,128)(2,1)} %copy-done.50, ...), custom_call_target="tpu_custom_call" | custom-call | flops 18000000 | bytes 1024 | tf_op jit(solution)/shard_map/mlp_forward/pallas_call | solution.py:446
  251.1 7.4 %convolution_convert_fusion.1 = bf16[2048,1024]{1,0:T(8,128)(2,1)S(1)} fusion(bf16[1024,2048]{1,0:T(8,128)(2,1)} %get-tuple-element.234, bf16[512,1024]{1,0:T(8,128)(2,1)} %collective-permute-done.34.refs_2_, bf16[512,1024]{1,0:T(8,128)(2,1)} %get-tuple-element.236.refs_1_), kind=kOutput, calls=%fused_computation.4 | convolution fusion | flops 4301258752 | bytes 10485760 | tf_op jit(solution)/shard_map/dot_general | solution.py:30
  264.3 21.3 %mlp_backward.1 = (bf16[1024,2048]{1,0:T(8,128)(2,1)}, f32[512,1024]{1,0:T(8,128)}, bf16[512,1024]{1,0:T(8,128)(2,1)}) custom-call(s32[2,16]{1,0:T(2,128)} %copy-done.28, bf16[512,1024]{1,0:T(8,128)(2,1)} %get-tuple-element.236.refs_1_, bf16[512,1024]{1,0:T(8,128)(2,1)} %collective-permute-done.34.refs_2_, bf16[1024,2048]{1,0:T(8,128)(2,1)} %get-tuple-element.238.refs_3_, ...), custom_call_target="tpu_custom_call" | custom-call | flops 20000000 | bytes 1024 | tf_op jit(solution)/shard_map/mlp_backward/pallas_call | solution.py:446
  296.3 6.6 %turn.1 = (f32[512,1024]{1,0:T(8,128)S(1)}, bf16[512,1024]{1,0:T(8,128)(2,1)S(1)}, bf16[512,256]{1,0:T(8,128)(2,1)S(1)}, bf16[512,256]{1,0:T(8,128)(2,1)S(1)}, b...) custom-call(f32[512,1024]{1,0:T(8,128)S(1)} %copy-done.7, ...), custom_call_target="tpu_custom_call" | custom-call | flops 6000000 | bytes 1024 | tf_op jit(solution)/shard_map/turn/pallas_call | solution.py:603
  315.6 4.9 convolution_convert_fusion
  330.8 5.1 collective-permute-done.44
  340.8 24.8 %attention_backward.2.refs_0_ = bf16[2048,384]{1,0:T(8,128)(2,1)} custom-call(s32[8]{0:T(128)} %get-tuple-element.435.table, bf16[2048,256]{1,0:T(8,128)(2,1)} %get-tuple-element.205.q_ref, bf16[2048,256]{1,0:T(8,128)(2,1)} %get-tuple-element.206.k_ref, bf16[2048,256]{1,0:T(8,128)(2,1)} %get-tuple-element.207.v_ref, ...), custom_call_target="tpu_custom_call" | custom-call | flops 44000000 | bytes 1024 | tf_op jit(solution)/shard_map/attention_backward/pallas_call | solution.py:300
  365.7 8.8 %collective-permute-done.49 = bf16[1,1,4,2,32,1024]{5,4,3,2,1,0:T(8,128)(2,1)} collective-permute-done((bf16[1,1,4,2,32,1024]{5,4,3,2,1,0:T(8,128)(2,1)}, bf16[1,1,4,2,32,1024]{5,4,3,2,1,0:T(8,128)(2,1)}, u32[]{:S(2)}, u32[]{:S(2)}) %collective-permute-start.49) | collective-permute-done | bytes 524320 | tf_op jit(solution)/shard_map/ppermute | solution.py:687
  399.4 24.1 %attention_backward.3.refs_1_ = bf16[2048,384]{1,0:T(8,128)(2,1)} custom-call(s32[8]{0:T(128)} %get-tuple-element.435.table, bf16[2048,256]{1,0:T(8,128)(2,1)} %get-tuple-element.205.q_ref, bf16[2048,256]{1,0:T(8,128)(2,1)} %get-tuple-element.206.k_ref, bf16[2048,256]{1,0:T(8,128)(2,1)} %get-tuple-element.207.v_ref, ...), custom_call_target="tpu_custom_call" | custom-call | flops 44000000 | bytes 1024 | tf_op jit(solution)/shard_map/attention_backward/pallas_call | solution.py:300
  426.3 6.9 %input_grad.1 = (bf16[4,256,1024]{2,1,0:T(8,128)(2,1)S(1)}, bf16[4,256,1024]{2,1,0:T(8,128)(2,1)S(1)}) custom-call(s32[8]{0:T(128)S(1)} %gather_fusion, bf16[2048,384]{1,0:T(8,128)(2,1)S(1)} %copy-done, bf16[2048,384]{1,0:T(8,128)(2,1)S(1)} %copy-done.1, bf16[1024,768]{1,0:T(8,128)(2,1)S(1)} %copy-done.17), custom_call_target="tpu_custom_call" | custom-call | flops 6000000 | bytes 1024 | tf_op jit(solution)/shard_map/input_grad/pallas_call | solution.py:640
  452.0 5.9 %collective-permute-done.55.refs_1_ = bf16[256,1024]{1,0:T(8,128)(2,1)} collective-permute-done((bf16[256,1024]{1,0:T(8,128)(2,1)}, bf16[256,1024]{1,0:T(8,128)(2,1)}, u32[]{:S(2)}, u32[]{:S(2)}) %collective-permute-start.55) | collective-permute-done | bytes 524320 | tf_op jit(solution)/shard_map/ppermute | solution.py:808
  460.9 14.3 %collective-permute-done.57.refs_1_ = bf16[256,1024]{1,0:T(8,128)(2,1)} collective-permute-done((bf16[256,1024]{1,0:T(8,128)(2,1)}, bf16[256,1024]{1,0:T(8,128)(2,1)}, u32[]{:S(2)}, u32[]{:S(2)}) %collective-permute-start.57) | collective-permute-done | bytes 524320 | tf_op jit(solution)/shard_map/ppermute | solution.py:808
  492.6 14.0 %collective-permute-done.65 = f32[2,8,32]{2,1,0:T(8,128)S(1)} collective-permute-done((f32[2,8,32]{2,1,0:T(8,128)S(1)}, f32[2,8,32]{2,1,0:T(8,128)S(1)}, u32[]{:S(2)}, u32[]{:S(2)}) %collective-permute-start.65) | collective-permute-done | bytes 2080 | tf_op jit(solution)/shard_map/ppermute | solution.py:687
  507.6 14.0 %collective-permute-done.66 = f32[1,8,32]{2,1,0:T(8,128)S(1)} collective-permute-done((f32[1,8,32]{2,1,0:T(8,128)S(1)}, f32[1,8,32]{2,1,0:T(8,128)S(1)}, u32[]{:S(2)}, u32[]{:S(2)}) %collective-permute-start.66) | collective-permute-done | bytes 1056 | tf_op jit(solution)/shard_map/ppermute | solution.py:687
  (463 shorter events, 231.4 us)
Async XLA Ops:
  3.2 62.8 %collective-permute-start = (bf16[256,1024]{1,0:T(8,128)(2,1)}, bf16[256,1024]{1,0:T(8,128)(2,1)S(1)}, u32[]{:S(2)}, u32[]{:S(2)}) collective-permute-start(bf16[256,1024]{1,0:T(8,128)(2,1)} %get-tuple-element.393), channel_id=1, source_target_pairs={{0,0},{1,1},{2,8},{3,9},{4,2},{5,3},{6,10},{7,11},{8,4},{9,5},{10,... | collective-permute-start | bytes 1572872 | tf_op jit(solution)/shard_map/ppermute | solution.py:794
  8.9 57.1 %collective-permute-start.1 = (bf16[256,1024]{1,0:T(8,128)(2,1)}, bf16[256,1024]{1,0:T(8,128)(2,1)S(1)}, u32[]{:S(2)}, u32[]{:S(2)}) collective-permute-start(bf16[256,1024]{1,0:T(8,128)(2,1)} %get-tuple-element.392), channel_id=1, source_target_pairs={{0,2},{1,3},{2,10},{3,11},{4,0},{5,1},{6,8},{7,9},{8,6},{9,7},{10,... | collective-permute-start | bytes 1572872 | tf_op jit(solution)/shard_map/ppermute | solution.py:794
  11.7 41.1 %collective-permute-start.5 = (bf16[32,2,1024]{2,0,1:T(8,128)(2,1)}, bf16[32,2,1024]{2,0,1:T(8,128)(2,1)}, u32[]{:S(2)}, u32[]{:S(2)}) collective-permute-start(bf16[32,2,1024]{2,0,1:T(8,128)(2,1)} %bitcast.211), channel_id=1, source_target_pairs={{0,8},{8,0},{1,9},{9,1},{2,10},{10,2},{3,11},{11,3},{4,12},{12,4},... | collective-permute-start | bytes 393224 | tf_op jit(solution)/shard_map/ppermute | solution.py:687
  12.2 34.9 %collective-permute-start.2 = (bf16[1,160,1024]{2,1,0:T(8,128)(2,1)S(1)}, bf16[1,160,1024]{2,1,0:T(8,128)(2,1)S(1)}, u32[]{:S(2)}, u32[]{:S(2)}) collective-permute-start(bf16[1,160,1024]{2,1,0:T(8,128)(2,1)S(1)} %maximum_bitcast_fusion), channel_id=1, source_target_pairs={{0,4},{2,6},{4,0},{6,2},{1,5},{3,7},{5,1},{7,3},{8,12},{10,14},{12... | collective-permute-start | bytes 983048 | tf_op jit(solution)/shard_map/ppermute | solution.py:687
  14.4 39.4 %all-to-all-start = ((bf16[4,32,768]{2,1,0:T(8,128)(2,1)}), bf16[4,32,768]{2,1,0:T(8,128)(2,1)S(1)}, u32[]{:S(2)}, u32[]{:S(2)}) async-start(bf16[4,32,768]{2,1,0:T(8,128)(2,1)} %bitcast.3), calls=%async_computation | async-start | bytes 393216 | tf_op jit(solution)/shard_map/all_to_all | solution.py:844
  112.8 42.0 %collective-permute-start.20 = (bf16[8,80,1024]{2,1,0:T(8,128)(2,1)}, bf16[8,80,1024]{2,1,0:T(8,128)(2,1)}, u32[]{:S(2)}, u32[]{:S(2)}) collective-permute-start(bf16[8,80,1024]{2,1,0:T(8,128)(2,1)} %pad_maximum_fusion.6), channel_id=1, source_target_pairs={{0,16},{16,0},{1,17},{17,1},{2,18},{18,2},{3,19},{19,3},{4,20},{20... | collective-permute-start | bytes 3932168 | tf_op jit(solution)/shard_map/ppermute | solution.py:687
  114.0 40.8 %collective-permute-start.21 = (bf16[8,80,1024]{2,1,0:T(8,128)(2,1)S(1)}, bf16[8,80,1024]{2,1,0:T(8,128)(2,1)}, u32[]{:S(2)}, u32[]{:S(2)}) collective-permute-start(bf16[8,80,1024]{2,1,0:T(8,128)(2,1)S(1)} %pad_maximum_fusion.7), channel_id=1, source_target_pairs={{0,1},{1,0},{2,3},{3,2},{4,5},{5,4},{6,7},{7,6},{8,9},{9,8},{10,11... | collective-permute-start | bytes 3932168 | tf_op jit(solution)/shard_map/ppermute | solution.py:687
  115.8 39.0 %collective-permute-start.22 = (bf16[4,64,1024]{2,1,0:T(8,128)(2,1)S(1)}, bf16[4,64,1024]{2,1,0:T(8,128)(2,1)}, u32[]{:S(2)}, u32[]{:S(2)}) collective-permute-start(bf16[4,64,1024]{2,1,0:T(8,128)(2,1)S(1)} %get-tuple-element.212), channel_id=1, source_target_pairs={{0,1},{1,0},{2,3},{3,2},{4,5},{5,4},{6,7},{7,6},{8,9},{9,8},{10,11... | collective-permute-start | bytes 1572872 | tf_op jit(solution)/shard_map/ppermute | solution.py:687
  116.0 38.8 %collective-permute-start.23 = (bf16[4,64,1024]{2,1,0:T(8,128)(2,1)S(1)}, bf16[4,64,1024]{2,1,0:T(8,128)(2,1)}, u32[]{:S(2)}, u32[]{:S(2)}) collective-permute-start(bf16[4,64,1024]{2,1,0:T(8,128)(2,1)S(1)} %get-tuple-element.213), channel_id=1, source_target_pairs={{0,16},{16,0},{1,17},{17,1},{2,18},{18,2},{3,19},{19,3},{4,20},{20... | collective-permute-start | bytes 1572872 | tf_op jit(solution)/shard_map/ppermute | solution.py:687
  158.9 38.3 %collective-permute-start.27 = (bf16[16,32,1024]{2,1,0:T(8,128)(2,1)S(1)}, bf16[16,32,1024]{2,1,0:T(8,128)(2,1)S(1)}, u32[]{:S(2)}, u32[]{:S(2)}) collective-permute-start(bf16[16,32,1024]{2,1,0:T(8,128)(2,1)S(1)} %pad_maximum_fusion.10.refs_7_), channel_id=1, source_target_pairs={{0,8},{8,0},{1,9},{9,1},{2,10},{10,2},{3,11},{11,3},{4,12},{12,4},... | collective-permute-start | bytes 3145736 | tf_op jit(solution)/shard_map/ppermute | solution.py:687
  163.5 37.7 %collective-permute-start.30 = (bf16[8,64,1024]{2,1,0:T(8,128)(2,1)S(1)}, bf16[8,64,1024]{2,1,0:T(8,128)(2,1)S(1)}, u32[]{:S(2)}, u32[]{:S(2)}) collective-permute-start(bf16[8,64,1024]{2,1,0:T(8,128)(2,1)S(1)} %pad_maximum_fusion.12), channel_id=1, source_target_pairs={{0,1},{1,0},{2,3},{3,2},{4,5},{5,4},{6,7},{7,6},{8,9},{9,8},{10,11... | collective-permute-start | bytes 3145736 | tf_op jit(solution)/shard_map/ppermute | solution.py:687
  166.2 31.0 %collective-permute-start.26 = (bf16[512,256]{1,0:T(8,128)(2,1)S(1)}, bf16[512,256]{1,0:T(8,128)(2,1)S(1)}, u32[]{:S(2)}, u32[]{:S(2)}) collective-permute-start(bf16[512,256]{1,0:T(8,128)(2,1)S(1)} %bitcast.240), channel_id=1, source_target_pairs={{0,9},{1,8},{2,11},{3,10},{4,13},{5,12},{6,15},{7,14},{8,1},{9,0},... | collective-permute-start | bytes 786440 | tf_op jit(solution)/shard_map/ppermute | solution.py:808
  168.5 36.2 %collective-permute-start.29 = (bf16[8,64,1024]{2,1,0:T(8,128)(2,1)S(1)}, bf16[8,64,1024]{2,1,0:T(8,128)(2,1)S(1)}, u32[]{:S(2)}, u32[]{:S(2)}) collective-permute-start(bf16[8,64,1024]{2,1,0:T(8,128)(2,1)S(1)} %pad_maximum_fusion.11), channel_id=1, source_target_pairs={{0,16},{16,0},{1,17},{17,1},{2,18},{18,2},{3,19},{19,3},{4,20},{20... | collective-permute-start | bytes 3145736 | tf_op jit(solution)/shard_map/ppermute | solution.py:687
  338.5 36.0 %collective-permute-start.47 = (bf16[1,1,4,2,32,2048]{5,4,3,2,1,0:T(8,128)(2,1)}, bf16[1,1,4,2,32,2048]{5,4,3,2,1,0:T(8,128)(2,1)}, u32[]{:S(2)}, u32[]{:S(2)}) collective-permute-start(bf16[1,1,4,2,32,2048]{5,4,3,2,1,0:T(8,128)(2,1)} %get-tuple-element.275), channel_id=1, source_target_pairs={{0,16},{16,0},{1,17},{17,1},{2,18},{18,2},{3,19},{19,3},{4,20},{20... | collective-permute-start | bytes 3145736 | tf_op jit(solution)/shard_map/ppermute | solution.py:687
  338.7 35.8 %collective-permute-start.48 = (bf16[2,1,4,1,32,2048]{5,4,2,3,1,0:T(8,128)(2,1)}, bf16[2,1,4,1,32,2048]{5,4,2,3,1,0:T(8,128)(2,1)}, u32[]{:S(2)}, u32[]{:S(2)}) collective-permute-start(bf16[2,1,4,1,32,2048]{5,4,2,3,1,0:T(8,128)(2,1)} %get-tuple-element.276), channel_id=1, source_target_pairs={{0,1},{1,0},{2,3},{3,2},{4,5},{5,4},{6,7},{7,6},{8,9},{9,8},{10,11... | collective-permute-start | bytes 3145736 | tf_op jit(solution)/shard_map/ppermute | solution.py:687
  339.7 34.8 %collective-permute-start.49 = (bf16[1,1,4,2,32,1024]{5,4,3,2,1,0:T(8,128)(2,1)}, bf16[1,1,4,2,32,1024]{5,4,3,2,1,0:T(8,128)(2,1)}, u32[]{:S(2)}, u32[]{:S(2)}) collective-permute-start(bf16[1,1,4,2,32,1024]{5,4,3,2,1,0:T(8,128)(2,1)} %get-tuple-element.277), channel_id=1, source_target_pairs={{0,16},{16,0},{1,17},{17,1},{2,18},{18,2},{3,19},{19,3},{4,20},{20... | collective-permute-start | bytes 1572872 | tf_op jit(solution)/shard_map/ppermute | solution.py:687
  379.9 43.6 %all-to-all-start.1 = ((bf16[32,32,384]{2,1,0:T(8,128)(2,1)}), bf16[32,32,384]{2,1,0:T(8,128)(2,1)}, u32[]{:S(2)}, u32[]{:S(2)}) async-start(bf16[32,32,384]{2,1,0:T(8,128)(2,1)} %bitcast.69), calls=%async_computation.1 | async-start | bytes 1572864 | tf_op jit(solution)/shard_map/all_to_all | solution.py:1054
  390.4 33.1 %collective-permute-start.51 = (bf16[4,1,32,2048]{3,2,0,1:T(8,128)(2,1)}, bf16[4,1,32,2048]{3,2,0,1:T(8,128)(2,1)}, u32[]{:S(2)}, u32[]{:S(2)}) collective-permute-start(bf16[4,1,32,2048]{3,2,0,1:T(8,128)(2,1)} %get-tuple-element.290), channel_id=1, source_target_pairs={{0,1},{1,0},{2,3},{3,2},{4,5},{5,4},{6,7},{7,6},{8,9},{9,8},{10,11... | collective-permute-start | bytes 1572872 | tf_op jit(solution)/shard_map/ppermute | solution.py:687
  391.8 31.7 %collective-permute-start.52 = (bf16[1,1,4,32,2048]{4,3,2,1,0:T(8,128)(2,1)}, bf16[1,1,4,32,2048]{4,3,2,1,0:T(8,128)(2,1)}, u32[]{:S(2)}, u32[]{:S(2)}) collective-permute-start(bf16[1,1,4,32,2048]{4,3,2,1,0:T(8,128)(2,1)} %get-tuple-element.291), channel_id=1, source_target_pairs={{0,16},{16,0},{1,17},{17,1},{2,18},{18,2},{3,19},{19,3},{4,20},{20... | collective-permute-start | bytes 1572872 | tf_op jit(solution)/shard_map/ppermute | solution.py:687
  444.3 30.9 %collective-permute-start.57 = (bf16[256,1024]{1,0:T(8,128)(2,1)}, bf16[256,1024]{1,0:T(8,128)(2,1)}, u32[]{:S(2)}, u32[]{:S(2)}) collective-permute-start(bf16[256,1024]{1,0:T(8,128)(2,1)} %get-tuple-element.325), channel_id=1, source_target_pairs={{0,1},{1,0},{2,3},{3,2},{4,5},{5,4},{6,7},{7,6},{8,9},{9,8},{10,11... | collective-permute-start | bytes 1572872 | tf_op jit(solution)/shard_map/ppermute | solution.py:808
  447.9 79.3 %all-to-all-start.2 = ((bf16[32,32,384]{2,1,0:T(8,128)(2,1)}), bf16[32,32,384]{2,1,0:T(8,128)(2,1)}, u32[]{:S(2)}, u32[]{:S(2)}) async-start(bf16[32,32,384]{2,1,0:T(8,128)(2,1)} %bitcast.237), calls=%async_computation.2 | async-start | bytes 1572864 | tf_op jit(solution)/shard_map/all_to_all | solution.py:1107
  481.8 40.5 %collective-permute-start.60 = (bf16[1,32,5120]{2,1,0:T(8,128)(2,1)S(1)}, bf16[1,32,5120]{2,1,0:T(8,128)(2,1)S(1)}, u32[]{:S(2)}, u32[]{:S(2)}) collective-permute-start(bf16[1,32,5120]{2,1,0:T(8,128)(2,1)S(1)} %constant_dynamic-slice_fusion.4), channel_id=1, source_target_pairs={{0,4},{2,6},{4,0},{6,2},{1,5},{3,7},{5,1},{7,3},{8,12},{10,14},{12... | collective-permute-start | bytes 983048 | tf_op jit(solution)/shard_map/ppermute | solution.py:687
  482.0 44.2 %collective-permute-start.58 = (bf16[256,1024]{1,0:T(8,128)(2,1)S(1)}, bf16[256,1024]{1,0:T(8,128)(2,1)S(1)}, u32[]{:S(2)}, u32[]{:S(2)}) collective-permute-start(bf16[256,1024]{1,0:T(8,128)(2,1)S(1)} %get-tuple-element.327), channel_id=1, source_target_pairs={{2,0},{3,1},{10,2},{11,3},{0,4},{1,5},{8,6},{9,7},{6,8},{7,9},{14,... | collective-permute-start | bytes 1572872 | tf_op jit(solution)/shard_map/ppermute | solution.py:797
  484.7 41.4 %collective-permute-start.59 = (bf16[256,1024]{1,0:T(8,128)(2,1)S(1)}, bf16[256,1024]{1,0:T(8,128)(2,1)S(1)}, u32[]{:S(2)}, u32[]{:S(2)}) collective-permute-start(bf16[256,1024]{1,0:T(8,128)(2,1)S(1)} %copy-done.30), channel_id=1, source_target_pairs={{0,0},{1,1},{8,2},{9,3},{2,4},{3,5},{10,6},{11,7},{4,8},{5,9},{12,... | collective-permute-start | bytes 1572872 | tf_op jit(solution)/shard_map/ppermute | solution.py:797
  (138 other events, 1674.3 us)

commit v3 on v2

--- a/solution.py
+++ b/solution.py
@@ -31,22 +31,24 @@
 
 
 def qkv_kernel(table, order, *refs, group, shape):
-    x_refs = refs[:group]
-    w_in_ref, vec_ref, cos_ref, sin_ref, n_ref, q_ref, k_ref, v_ref, w_ref, held = refs[group:]
+    x_refs, w_refs = refs[:group], refs[group:-9]
+    vec_ref, cos_ref, sin_ref, n_ref, q_ref, k_ref, v_ref, w_ref, held = refs[-9:]
     step = pl.program_id(0)
 
     @pl.when(step == 0)
     def _():
         if shape is None:
-            w_ref[...] = w_in_ref[...]
+            w_ref[...] = w_refs[0][...]
             return
         na, nb, part = shape
-        for n in range(w_in_ref.shape[0]):
+        sources = w_refs[0].shape[0]
+        for n in range(len(w_refs) * sources):
             j, a = order[n] // na, order[n] % na
             for m in range(group):
                 row = ((j * (group // nb) + m // nb) * na + a) * nb + m % nb
                 start = pl.multiple_of(row * part, part)
-                w_ref[pl.ds(start, part), :] = w_in_ref[n, m * part : (m + 1) * part, :]
+                block = w_refs[n // sources][n % sources, m * part : (m + 1) * part, :]
+                w_ref[pl.ds(start, part), :] = block
 
     for n in range(group):
 
@@ -90,7 +92,7 @@
             num_scalar_prefetch=2,
             grid=(2 * group,),
             in_specs=[fixed((2, rows, model))] * group
-            + [fixed(w.shape), fixed(vec.shape)]
+            + [fixed(x.shape) for x in (*w, vec)]
             + [pl.BlockSpec((rows, 128), at)] * 2,
             out_specs=[pl.BlockSpec((rows, model), at)]
             + [pl.BlockSpec((rows, width), at)] * 3
@@ -102,7 +104,7 @@
         ),
         cost_estimate=cost(11),
         name="qkv",
-    )(table, order, *pieces, w, vec, cosine, sine)
+    )(table, order, *pieces, *w, vec, cosine, sine)
 
 
 def forward_kernel(table, q_ref, k_ref, v_ref, o_ref, lse_ref, vaug, *, bq, bk, rows):
@@ -336,35 +338,6 @@
     return 0.5 * (1.0 + t) + 0.5 * v * (1.0 - t * t) * inner
 
 
-def load_weights(order, weight_refs, up, down):
-    if order is None:
-        up[...], down[...] = weight_refs[0][...], weight_refs[1][...]
-        return
-    half = pl.program_id(0)
-    ups, downs = weight_refs[:2], weight_refs[2:]
-    sources, rows, _ = ups[0].shape
-    part, cut = rows // 2, downs[0].shape[1]
-    per = down.shape[0] // (2 * cut)
-    for which in range(2):
-
-        @pl.when(half == which)
-        def _(which=which):
-            for n in range(sources):
-                source = order[which, n]
-                base = (source // per) * 2 * per + source % per
-                for c in range(2):
-                    start = pl.multiple_of((base + c * per) * part, part)
-                    up[pl.ds(start, part), :] = ups[which][n, c * part : (c + 1) * part, :]
-
-        for n in range(sources):
-            source = order[which, n]
-
-            @pl.when(source // per == half)
-            def _(n=n, source=source, which=which):
-                start = pl.multiple_of(((source % per) * 2 + which) * cut, cut)
-                down[pl.ds(start, cut), :] = downs[which][n]
-
-
 def take(step, refs, held):
     for n, ref in enumerate(refs):
 
@@ -375,104 +348,205 @@
     return held[...]
 
 
-def add_halves(term, own_ref, other_ref, total):
-    half, tile = pl.program_id(0), pl.program_id(1)
-
-    @pl.when(half == 0)
+def load_up(order, refs, up):
+    pieces, (sources, rows, unit) = len(refs) // 2, refs[0].shape
+    part, total = rows // 2, pieces * sources
+    per = total // (up.shape[1] // unit)
+    for which in range(2):
+        for n in range(total):
+            source = order[which, n]
+            ref = refs[which * pieces + n // sources]
+            base = (source // per) * 2 * per + source % per
+            for c in range(2):
+                start = pl.multiple_of((base + c * per) * part, part)
+                up[pl.ds(start, part), which * unit : (which + 1) * unit] = ref[
+                    n % sources, c * part : (c + 1) * part, :
+                ]
+
+
+def load_down(order, refs, down):
+    at = 0
+    for ref in refs:
+        deep = ref.shape[1]
+        for n in range(ref.shape[0]):
+            down[pl.ds(pl.multiple_of(order[2, at] * deep, deep), deep), :] = ref[n]
+            at += 1
+
+
+def mlp_up_kernel(*refs, tables):
+    pre_ref, act_ref, held = refs[tables + 2 :][-(3 + tables) :][:3]
+    x_refs, weights = refs[tables : tables + 2], refs[tables + 2 : -(3 + tables)]
+    up = weights[0]
+    if tables:
+        up = refs[-1]
+
+        @pl.when(pl.program_id(0) == 0)
+        def _():
+            load_up(refs[0], weights, up)
+
+    x = take(pl.program_id(0), x_refs, held)
+    for n in range(up.shape[1] // x.shape[1]):
+        at = slice(n * x.shape[1], (n + 1) * x.shape[1])
+        pre = dot(x, up[:, at])
+        pre_ref[:, at] = pre.astype(BF)
+        act_ref[:, at] = gelu(pre).astype(BF)
+
+
+def leave(total, own_ref, other_ref):
+    @pl.when(pl.program_id(0) == 0)
     def _():
-        total[tile] = term
-
-    @pl.when(half != 0)
+        own_ref[...] = total
+
+    @pl.when(pl.program_id(0) == 1)
     def _():
-        total[tile] += term
-
-    @pl.when(jnp.logical_and(half == pl.num_programs(0) - 1, tile == 0))
-    def _():
-        own_ref[...] = total[0]
-
-    @pl.when(jnp.logical_and(half == pl.num_programs(0) - 1, tile == 1))
-    def _():
-        other_ref[...] = total[1].astype(BF)
-
-
-def mlp_forward_kernel(*refs, tables):
-    order = refs[0] if tables else None
-    pre_ref, act_ref, own_ref, other_ref, up, down, held, total = refs[-8:]
-    x_refs, weight_refs = refs[tables : tables + 2], refs[tables + 2 : -8]
-
-    @pl.when(pl.program_id(1) == 0)
-    def _():
-        load_weights(order, weight_refs, up, down)
-
-    pre = dot(take(pl.program_id(1), x_refs, held), up[...])
-    act = gelu(pre).astype(BF)
-    pre_ref[...] = pre.astype(BF)
-    act_ref[...] = act
-    add_halves(dot(act, down[...]), own_ref, other_ref, total)
+        other_ref[...] = total.astype(BF)
+
+
+def mlp_down_kernel(*refs, tables):
+    act_ref, weights = refs[tables], refs[tables + 1 : -(2 + tables)]
+    own_ref, other_ref = refs[tables + 1 :][-(2 + tables) :][:2]
+    down = weights[0]
+    if tables:
+        down = refs[-1]
+
+        @pl.when(pl.program_id(0) == 0)
+        def _():
+            load_down(refs[0], weights, down)
+
+    leave(dot(act_ref[...], down[...]), own_ref, other_ref)
 
 
 def mlp_backward_kernel(*refs, tables):
-    order = refs[0] if tables else None
-    low_ref, own_ref, other_ref, up, down, held, total = refs[-7:]
-    g_refs, pre_ref, weight_refs = refs[tables : tables + 2], refs[tables + 2], refs[tables + 3 : -7]
-
-    @pl.when(pl.program_id(1) == 0)
-    def _():
-        load_weights(order, weight_refs, up, down)
-
-    grad = dot(take(pl.program_id(1), g_refs, held), down[...], NT)
-    low = (grad * gelu_slope(pre_ref[...].astype(F32))).astype(BF)
-    low_ref[...] = low
-    add_halves(dot(low, up[...], NT), own_ref, other_ref, total)
-
-
-def mlp_call(kernel, name, us, narrow, wide, weights, halves, wide_outs):
-    count, model = narrow[0].shape
-    tables = weights[4:]
+    g_refs, pre_ref, weights = refs[tables : tables + 2], refs[tables + 2], refs[tables + 3 : -(4 + 2 * tables)]
+    low_ref, own_ref, other_ref, held = refs[tables + 3 :][-(4 + 2 * tables) :][:4]
+    up, down = weights[0], weights[-1]
+    if tables:
+        up, down = refs[-2:]
+
+        @pl.when(pl.program_id(0) == 0)
+        def _():
+            load_up(refs[0], weights[:4], up)
+            load_down(refs[0], weights[4:], down)
+
+    g = take(pl.program_id(0), g_refs, held)
+    total = None
+    for n in range(up.shape[1] // g.shape[1]):
+        at = slice(n * g.shape[1], (n + 1) * g.shape[1])
+        grad = dot(g, down[at, :], NT)
+        low = (grad * gelu_slope(pre_ref[:, at].astype(F32))).astype(BF)
+        low_ref[:, at] = low
+        term = dot(low, up[:, at], NT)
+        total = term if total is None else total + term
+    leave(total, own_ref, other_ref)
+
+
+def mlp_call(kernel, name, us, narrow, wide, weights, tables, scratch, wide_outs, split):
+    count = (narrow or wide)[0].shape[0] if narrow else wide[0].shape[0] // 2
+    model = weights[0][0].shape[-1] if tables else min(weights[0][0].shape)
+    units = 2 * model if tables else max(weights[0][0].shape)
     fixed = lambda shape: pl.BlockSpec(
-        shape, lambda f, m, *t: (0,) * len(shape), pipeline_mode=pl.Buffered(1)
-    )
-    if tables:
-        sources, rows, _ = weights[0].shape
-        unit = model
-        specs = [fixed((sources, rows, model))] * 4
-    else:
-        unit = weights[1].shape[0] // halves
-        specs = [
-            pl.BlockSpec((model, unit), lambda f, m, *t: (0, f)),
-            pl.BlockSpec((unit, model), lambda f, m, *t: (f, 0)),
-        ]
-    wide_spec = pl.BlockSpec((count, unit), lambda f, m, *t: (m, f))
+        shape, lambda m, *t: (0,) * len(shape), pipeline_mode=pl.Buffered(1)
+    )
+    wide_spec = pl.BlockSpec((count, units), lambda m, *t: (m, 0))
     return pl.pallas_call(
         functools.partial(kernel, tables=len(tables)),
-        out_shape=[jax.ShapeDtypeStruct((2 * count, halves * unit), BF)] * wide_outs
-        + [jax.ShapeDtypeStruct((count, model), F32), jax.ShapeDtypeStruct((count, model), BF)],
+        out_shape=[jax.ShapeDtypeStruct((2 * count, units), BF)] * wide_outs
+        + [jax.ShapeDtypeStruct((count, model), kind) for kind in (F32, BF) if split],
         grid_spec=pltpu.PrefetchScalarGridSpec(
             num_scalar_prefetch=len(tables),
-            grid=(halves, 2),
-            in_specs=[fixed((count, model))] * 2 + [wide_spec] * len(wide) + specs,
-            out_specs=[wide_spec] * wide_outs + [fixed((count, model))] * 2,
-            scratch_shapes=[
-                pltpu.VMEM((model, unit), BF),
-                pltpu.VMEM((unit, model), BF),
-                pltpu.VMEM((count, model), BF),
-                pltpu.VMEM((2, count, model), F32),
-            ],
+            grid=(2,),
+            in_specs=[fixed((count, model))] * len(narrow)
+            + [wide_spec] * len(wide)
+            + [fixed(x.shape[:-2] + (rows, x.shape[-1])) for x, rows in weights],
+            out_specs=[wide_spec] * wide_outs + [fixed((count, model))] * (2 * split),
+            scratch_shapes=[pltpu.VMEM((count, model), BF)] * bool(narrow)
+            + [pltpu.VMEM(shape, BF) for shape in scratch if tables],
         ),
         compiler_params=pltpu.CompilerParams(
-            dimension_semantics=("arbitrary", "arbitrary"), vmem_limit_bytes=56 << 20
+            dimension_semantics=("arbitrary",), vmem_limit_bytes=56 << 20
         ),
         cost_estimate=cost(us),
         name=name,
-    )(*tables, *narrow, *wide, *weights[: 4 if tables else 2])
-
-
-def mlp_forward(narrow, weights, halves):
-    return mlp_call(mlp_forward_kernel, "mlp_forward", 18, narrow, [], weights, halves, 2)
-
-
-def mlp_backward(narrow, pre, weights, halves):
-    return mlp_call(mlp_backward_kernel, "mlp_backward", 20, narrow, [pre], weights, halves, 1)
+    )(*tables, *narrow, *wide, *[x for x, _ in weights])
+
+
+def relay_kernel(here, *refs, layout, arrivals):
+    count = sum(len(pieces) for _, pieces in layout)
+    kept, came = refs[:count], refs[count : count + arrivals]
+    outs, given = refs[count + arrivals : 2 * count + arrivals], refs[2 * count + arrivals :]
+    at = 0
+    for g, (n, pieces) in enumerate(layout):
+        mine = here[g]
+        for start, source, offset in pieces:
+            width = kept[at].shape[3]
+            for i in range(n):
+                for keep in (True, False):
+                    half = mine if keep else 1 - mine
+                    x = kept[at][i, half].astype(F32)
+                    x = x + came[source][i, half, :, offset : offset + width].astype(F32)
+                    if keep:
+                        outs[at][i] = x.astype(BF)
+                    else:
+                        given[g][i, :, start : start + width] = x.astype(BF)
+            at += 1
+
+
+def relay(groups, fused):
+    if not fused:
+        results = []
+        for here, (n, halves, m), pieces in groups:
+            kept, given = [], []
+            for x, came, offset in pieces:
+                width = x.shape[-1]
+                x = x.reshape(-1, width)
+                if came is not None:
+                    x = join(x, came.reshape(-1, came.shape[-1])[:, offset : offset + width])
+                if x.shape[0] != n * halves * m:
+                    x = scatter_axis(x.reshape(lax.axis_size("h"), -1, width), "h", 0)
+                x = x.reshape(n, halves, m, width)
+                mine = 0 if here is None else here
+                kept.append(lax.dynamic_index_in_dim(x, mine, 1, keepdims=False))
+                if here is not None:
+                    given.append(lax.dynamic_index_in_dim(x, 1 - here, 1, keepdims=False))
+            results.append((kept, jnp.concatenate(given, axis=-1) if given else None))
+        return results
+    kept, came, layout, widths = [], [], [], []
+    for _, (n, halves, m), pieces in groups:
+        start, entries = 0, []
+        for x, arrived, offset in pieces:
+            kept.append(x.reshape(n, halves, m, x.shape[-1]))
+            if not any(arrived is y for y, _ in came):
+                came.append((arrived, (n, halves, m, arrived.shape[-1])))
+            source = [arrived is y for y, _ in came].index(True)
+            entries.append((start, source, offset))
+            start += x.shape[-1]
+        layout.append((n, tuple(entries)))
+        widths.append((n, m, start))
+    came = [y.reshape(shape) for y, shape in came]
+    shapes = [(x.shape[0],) + x.shape[2:] for x in kept] + widths
+    fixed = lambda shape: pl.BlockSpec(
+        tuple(shape), lambda i, t: (0,) * len(shape), pipeline_mode=pl.Buffered(1)
+    )
+    outs = pl.pallas_call(
+        functools.partial(relay_kernel, layout=tuple(layout), arrivals=len(came)),
+        out_shape=[jax.ShapeDtypeStruct(shape, BF) for shape in shapes],
+        grid_spec=pltpu.PrefetchScalarGridSpec(
+            num_scalar_prefetch=1,
+            grid=(1,),
+            in_specs=[fixed(x.shape) for x in kept + came],
+            out_specs=[fixed(shape) for shape in shapes],
+        ),
+        compiler_params=pltpu.CompilerParams(
+            dimension_semantics=("arbitrary",), vmem_limit_bytes=60 << 20
+        ),
+        cost_estimate=cost(4),
+        name="relay",
+    )(jnp.stack([here for here, *_ in groups]), *kept, *came)
+    results, at = [], 0
+    for g, (_, entries) in enumerate(layout):
+        results.append((list(outs[at : at + len(entries)]), outs[len(kept) + g]))
+        at += len(entries)
+    return results
 
 
 def spread_of(values):
@@ -493,6 +567,29 @@
     @pl.when(pl.program_id(0) == 0)
     def _():
         ref[...] = jnp.zeros_like(ref)
+
+
+def pick_kernel(*refs):
+    out = refs[-1]
+    sources, cut, _ = refs[0].shape
+    for n, ref in enumerate(refs[:-1]):
+        which, piece = divmod(n, (len(refs) - 1) // 2)
+        out[piece * sources : (piece + 1) * sources, which * cut : (which + 1) * cut] = ref[...]
+
+
+def pick(arrays, cut):
+    sources, wide, model = arrays[0].shape
+    spec = pl.BlockSpec((sources, cut, model), lambda i: (0, wide // cut - 1, 0))
+    shape = (sources * len(arrays) // 2, 2 * cut, model)
+    return pl.pallas_call(
+        pick_kernel,
+        out_shape=jax.ShapeDtypeStruct(shape, BF),
+        grid=(1,),
+        in_specs=[spec] * len(arrays),
+        out_specs=pl.BlockSpec(shape, lambda i: (0, 0, 0)),
+        cost_estimate=cost(2),
+        name="pick",
+    )(*arrays)
 
 
 def out_kernel(order, places, *refs, group, views):
@@ -595,9 +692,11 @@
     out_ref[...] = (grad_ref[...] + grad).astype(BF)
 
 
-def row_call(kernel, name, us, rows, tall, halves, fixed, outs):
+def row_call(kernel, name, us, rows, tall, halves, fixed, outs, limit=40):
     model = tall[0].shape[1]
     count = tall[0].shape[0]
+    starts = [at[1] if isinstance(at, tuple) else 0 for at in tall]
+    tall = [at[0] if isinstance(at, tuple) else at for at in tall]
     whole = lambda x: pl.BlockSpec(x.shape, lambda i, n=x.ndim: (0,) * n)
     block = lambda width: pl.BlockSpec((rows, width), lambda i: (i, 0))
     return pl.pallas_call(
@@ -605,11 +704,14 @@
         out_shape=[jax.ShapeDtypeStruct((count, width), kind) for width, kind in outs]
         + [jax.ShapeDtypeStruct((8, model), F32)],
         grid=(count // rows,),
-        in_specs=[block(model)] * len(tall) + [whole(x) for x in (*halves, *fixed)],
+        in_specs=[
+            pl.BlockSpec((rows, model), lambda i, start=start: (i + start, 0)) for start in starts
+        ]
+        + [whole(x) for x in (*halves, *fixed)],
         out_specs=[block(width) for width, _ in outs] + [pl.BlockSpec((8, model), lambda i: (0, 0))],
         scratch_shapes=[pltpu.VMEM((rows, model), BF)] if halves else [],
         compiler_params=pltpu.CompilerParams(
-            dimension_semantics=("arbitrary",), vmem_limit_bytes=40 << 20
+            dimension_semantics=("arbitrary",), vmem_limit_bytes=limit << 20
         ),
         cost_estimate=cost(us),
         name=name,
@@ -834,8 +936,8 @@
             x = grow(x, flip(x, axis, bit))
         return x
 
-    first = jnp.concatenate([w_down[:cut], w_output[:cut_out], w_down[cut:], w_output[cut_out:]])
-    first, second = first[None], up_rows[None]
+    first = [up_rows[:cut_up], w_output[:cut_out], up_rows[cut_up:], w_output[cut_out:]]
+    first, second = jnp.concatenate(first)[None], w_down[None]
 
     columns = jnp.stack(
         [w.reshape(part, group, pairs, 128) for w in (w_query, w_key, w_value)], axis=3
@@ -848,7 +950,7 @@
     index = jnp.arange(blocks, dtype=jnp.int32)
     table = (member ^ (index % group)) * 2 + (parity ^ (index // group))
     positions_of = (parity ^ (index % 2)) * group + (member ^ (index // 2))
-    lane = jnp.arange(128, dtype=jnp.int32)
+    lane, first = together(jnp.arange(128, dtype=jnp.int32), first)
     frequency = jnp.exp(
         (lane % (HEAD_DIM // 2)).astype(F32) * (-2.0 * math.log(10000.0) / HEAD_DIM)
     )
@@ -856,14 +958,15 @@
     cosine = jnp.cos(angles)
     sine = jnp.sin(angles) * jnp.where((lane // (HEAD_DIM // 2)) % 2 == 0, -1.0, 1.0)[None, :]
 
-    vectors = grow_all(
+    vectors, columns = together(
         jnp.stack(
             [attn_in_gain, attn_in_bias, attn_out_gain, attn_out_bias,
              mlp_in_gain, mlp_in_bias, mlp_out_gain, mlp_out_bias]
-        )[None],
-        stages_of(("c", "b", "h", "j", "a")),
-    )
-    vectors = vectors[place_in(source_of(("c", "b", "h", "j", "a"), AXES))]
+        ),
+        columns,
+    )
+    vectors = jnp.broadcast_to(vectors[None], (devices,) + vectors.shape)
+    vectors = lax.all_to_all(vectors, AXES, 0, 0, tiled=True)
     vectors = vectors.transpose(1, 0, 2).reshape(8, model).astype(F32)
 
     def columns_in_order(x):
@@ -873,13 +976,13 @@
     own = [regroup(tokens, turn) for turn in range(2)]
     first_came = flip(first, *line_stages[0])
     w_came = flip(columns, *line_stages[0])
+    own, first_came, w_came, second, cosine, sine, vectors = together(
+        own, first_came, w_came, second, cosine, sine, vectors
+    )
     first = grow_all(grow(first, first_came), line_stages[1:])
-    wide = cut + cut_out
+    wide = cut_up + cut_out
     low_stages, high_stages = stages_of(low_axes), stages_of(high_axes)
     first_low, first_high = first[:, :wide], first[:, wide:]
-    own, first_low, first_high, w_came, second, cosine, sine, vectors = together(
-        own, first_low, first_high, w_came, second, cosine, sine, vectors
-    )
     columns = grow_all(grow(columns, w_came), line_stages[1:-1])
     second_came, w_came = flip(second, *line_stages[0]), flip(columns, *line_stages[-1])
     high_came = flip(first_high, *high_stages[0])
@@ -899,47 +1002,54 @@
         if not offset & core_bit:
             pieces[offset ^ core_bit] = by_offset(pieces[offset], core_bit)
     pieces, w_came, low_came, second_came = together(pieces, w_came, low_came, second_came)
-    columns = grow(columns, w_came)
     if views:
-        w_heads, w_shape = columns, (na, nb, part)
+        w_heads, w_shape = [columns, w_came], (na, nb, part)
     else:
-        w_heads, w_shape = columns_in_order(columns), None
+        w_heads, w_shape = [columns_in_order(grow(columns, w_came))], None
     first_low = grow_all(grow(first_low, low_came), low_stages[1:-1])
     first_high = grow_all(grow(first_high, high_came), high_stages[1:-1])
     second = grow(second, second_came)
-    second_low, second_high = second[:, :cut_up], second[:, cut_up:]
-    pieces, first_low, first_high, second_low, second_high = together(
-        pieces, first_low, first_high, second_low, second_high
-    )
+    pieces, first_low, first_high, second = together(pieces, first_low, first_high, second)
     low_came, high_came = flip(first_low, *low_stages[-1]), flip(first_high, *high_stages[-1])
-    up_low_came = flip(second_low, *low_stages[0])
-    up_high_came = flip(second_high, *high_stages[0])
+    seconds = [second]
+    if views:
+        seconds += [flip(second, "b", 1), flip(second, "j", 1)]
     normed, queries, keys, values, w_heads = qkv_call(
         positions_of, w_from, [pieces[d] for d in range(group)], w_heads, vectors,
         cosine, sine, w_shape,
     )
+    grad_in = [regroup(cotangent, 0)]
     attended, lse = attention_forward(table, queries, keys, values, rows)
-    attended, lse, low_came, high_came, up_low_came, up_high_came, cotangent = together(
-        attended, lse, low_came, high_came, up_low_came, up_high_came, cotangent
-    )
-    first_low, first_high = grow(first_low, low_came), grow(first_high, high_came)
-    second_low = grow_all(grow(second_low, up_low_came), low_stages[1:])
-    second_high = grow_all(grow(second_high, up_high_came), high_stages[1:])
+    attended, lse, low_came, high_came, grad_in, cotangent = together(
+        attended, lse, low_came, high_came, grad_in, cotangent
+    )
+    first_low, first_high = [first_low, low_came], [first_high, high_came]
+    if views:
+        near = source_of(("a",))
+        over_b, over_j = (near // nb) * nb + (near % nb ^ 1), near ^ (na * nb)
+        over_both = over_b ^ (na * nb)
+        down_from = jnp.concatenate([near, over_b, over_j, over_both])
+    else:
+        seconds = [grow_all(second, stages_of(("h", "j", "b")))]
+        down_from = source_of(("a", "h", "j", "b"))
     low_from, high_from = (source_of(("a",) + axes) for axes in (low_axes, high_axes))
 
     def exchange(x):
         return [x[0]] + [by_offset(x[d], d) for d in range(1, group)]
 
-    order = jnp.stack([low_from, high_from])
+    order = jnp.stack([low_from, high_from, down_from])
     low_at, high_at = place_in(low_from), place_in(high_from)
     core_block = jnp.arange(2 * jh, dtype=jnp.int32)
     if views:
-        mine = jnp.concatenate([first_low[:, cut:], first_high[:, cut:]], axis=1)
+        mine = pick(first_low + first_high, cut_out)
         out_weights = [mine, flip(mine, "c", 1)]
     else:
         mine = jnp.concatenate(
-            [first_low[:, cut:][low_at], first_high[:, cut:][high_at]], axis=1
-        ).reshape(jh, na * nb * part, model)
+            [jnp.concatenate([x[:, cut_up:] for x in pair]) for pair in (first_low, first_high)],
+            axis=1,
+        )
+        mine = jnp.concatenate([mine[:, :cut_out][low_at], mine[:, cut_out:][high_at]], axis=1)
+        mine = mine.reshape(jh, na * nb * part, model)
         other = flip(mine, "c", 1)
         w_out = jnp.where(
             ic == 0, jnp.stack([mine, other], axis=1), jnp.stack([other, mine], axis=1)
@@ -951,20 +1061,33 @@
         order, places, mixed, own, vectors, out_weights, views
     )
     mlp_rows = [mlp_mine, flip(mlp_mine, "c", 1)]
-    mlp_rows, second_low, second_high, cotangent = together(
-        mlp_rows, second_low, second_high, cotangent
-    )
     if views:
-        weights = [second_low, second_high, first_low, first_high, order]
+        mlp_rows, seconds = together(mlp_rows, seconds)
+        seconds += [flip(seconds[1][: na // 2], "j", 1), flip(seconds[2][na // 2 :], "b", 1)]
+    if views:
+        tables = [order]
+        up_weights = [(x, 2 * part) for x in first_low + first_high]
     else:
-        up = jnp.concatenate([second_low[low_at], second_high[high_at]], axis=1)
+        tables = []
+        up = [jnp.concatenate([x[:, :cut_up] for x in pair]) for pair in (first_low, first_high)]
+        up = jnp.concatenate([up[0][low_at], up[1][high_at]], axis=1)
         up = up.reshape(jh, na, nb, jh, 2, part, unit)
-        up = up.transpose(0, 4, 1, 2, 5, 3, 6).reshape(model, jh * unit)
-        down = [first_low[:, :cut][low_at], first_high[:, :cut][high_at]]
-        weights = [up, jnp.concatenate(down, axis=1).reshape(jh * unit, model)]
-    grad_in = [regroup(cotangent, turn) for turn in range(2)]
-    pre_act, activated, branch, branch_other = mlp_forward(mlp_rows, weights, jh)
-    branch, branch_other, grad_in = together(branch, branch_other, grad_in)
+        up_weights = [(up.transpose(0, 4, 1, 2, 5, 3, 6).reshape(model, jh * unit), model)]
+    grad_in.append(regroup(cotangent, 1))
+    pre_act, activated = mlp_call(
+        mlp_up_kernel, "mlp_up", 11, mlp_rows, [], up_weights, tables,
+        [(model, jh * unit)], 2, False,
+    )
+    activated, grad_in, seconds = together(activated, grad_in, seconds)
+    if views:
+        down_weights = [(x, n_down) for x in seconds]
+    else:
+        down = seconds[0][place_in(down_from)]
+        down_weights = [(down.reshape(jh * unit, model), jh * unit)]
+    branch, branch_other = mlp_call(
+        mlp_down_kernel, "mlp_down", 9, [], [activated], down_weights, tables,
+        [(jh * unit, model)], 0, True,
+    )
     block_loose, branch_mine, mo_sums = row_call(
         middle_kernel, "middle", 3, rows,
         [branch, flip(branch_other, "c", 1), residual], grad_in, [vectors],
@@ -980,6 +1103,20 @@
 
     def added(pair, came, shape):
         return (pair[0] if came is None else join(pair[0], came)).reshape(shape)
+
+    def sends_of(arrays, axis, dim):
+        kept, given = zip(*[sends(x, axis, dim) for x in arrays])
+        return list(kept), None if given[0] is None else jnp.concatenate(given, axis=-1)
+
+    def added_of(kept, came, shape):
+        out, start = [], 0
+        for x in kept:
+            width = x.shape[-1]
+            if came is not None:
+                x = join(x, came[..., start : start + width])
+            out.append(x.reshape(shape + (width,)))
+            start += width
+        return out
 
     down_part = dot(activated, jnp.concatenate(branch_rows), TN).astype(BF)
     down_part = down_part.reshape(2, nh, na, nb, n_down, model)
@@ -988,15 +1125,25 @@
     branch_rows, low_sends, high_sends, block_loose = together(
         branch_rows, low_sends, high_sends, block_loose
     )
+    half_b, halves_b = (ib if nb > 1 else None), min(nb, 2)
+    low_bit, next_bit = ia % 2, (ia // 2) % 2
     low_came, high_came = send(low_sends, "b"), send(high_sends, "j")
     block_came = [restore(block_loose[:rows], 0), restore(block_loose[rows:], 1)]
-    pre_low, grad_mlp, grad_other = mlp_backward(branch_rows, pre_act, weights, jh)
-    pre_low, grad_mlp, grad_other, low_came, high_came = together(
-        pre_low, grad_mlp, grad_other, low_came, high_came
+    pre_low, grad_mlp, grad_other = mlp_call(
+        mlp_backward_kernel, "mlp_backward", 20, branch_rows, [pre_act],
+        up_weights + down_weights, tables, [(model, jh * unit), (jh * unit, model)], 1, True,
+    )
+    pre_low, grad_mlp, grad_other, low_came, high_came, block_came = together(
+        pre_low, grad_mlp, grad_other, low_came, high_came, block_came
     )
     grad_other = flip(grad_other, "c", 1)
-    low_sends = sends(added(low_sends, low_came, (2, nh, na, cut, model)), "j", 0)
-    high_sends = sends(added(high_sends, high_came, (nh, na, nb, cut, model)), "b", 2)
+    low_sends, high_sends = relay(
+        [
+            (ij, (1, 2, nh * na * cut), [(low_sends[0], low_came, 0)]),
+            (half_b, (nh * na, halves_b, cut), [(high_sends[0], high_came, 0)]),
+        ],
+        views,
+    )
     grad_mlp, grad_other, low_sends, high_sends = together(
         grad_mlp, grad_other, low_sends, high_sends
     )
@@ -1004,31 +1151,27 @@
     grad_residual, projected_low, *attended_low, turn_sums = row_call(
         functools.partial(turn_kernel, group=group), "turn", 6, rows,
         [grad_mlp, grad_other, residual, projected], grad_in, [vectors, w_out],
-        [(model, F32), (model, BF)] + [(width, BF)] * group,
-    )
-    attended_low, pre_low, low_came, high_came, block_came = together(
-        attended_low, pre_low, low_came, high_came, block_came
-    )
-    grad_heads = jnp.stack(exchange(attended_low)).reshape(blocks, rows, width)
-    down_part = jnp.concatenate(
-        [
-            added(low_sends, low_came, (nh, na, cut, model)),
-            added(high_sends, high_came, (nh, na, cut, model)),
-        ],
-        axis=2,
-    )
-    down_sends = sends(scatter_axis(down_part, "h", 0), "a", 0)
+        [(model, F32), (model, BF)] + [(width, BF)] * group, limit=60,
+    )
+    attended_low, projected_low, pre_low, low_came, high_came, block_came = together(
+        attended_low, projected_low, pre_low, low_came, high_came, block_came
+    )
+    grad_heads = exchange(attended_low)
+    grad_heads[1], pre_low = together(grad_heads[1], pre_low)
+    grad_heads = jnp.stack(grad_heads).reshape(blocks, rows, width)
+    down_pieces = [(low_sends[0][0], low_came, 0), (high_sends[0][0], high_came, 0)]
+    (down_sends,) = relay([(low_bit, (na // 2, 2, cut), down_pieces)], views)
     up_part = dot(jnp.concatenate(mlp_rows), pre_low, TN).astype(BF)
     up_part = up_part.reshape(2, nh, 2, na, nb, part, jh * unit)
-    low_sends = sends(up_part[:, :, 0], "j", 0)
-    high_sends = sends(up_part[:, :, 1], "b", 3)
     grad_out = jnp.stack([dot(mixed[d], projected_low, TN).astype(BF) for d in range(group)])
     grad_out = jnp.stack(
         [lax.dynamic_index_in_dim(grad_out, member ^ m, 0, keepdims=False) for m in range(group)]
     ).reshape(2, nh, 2, na, nb, part, model)
-    out_sends = sends(scatter_axis(grad_out, "c", 2), "j", 0)
-    grad_heads, down_sends, low_sends, high_sends, out_sends = together(
-        grad_heads, down_sends, low_sends, high_sends, out_sends
+    grad_out = scatter_axis(grad_out, "c", 2)
+    low_sends = sends_of([up_part[:, :, 0], grad_out[..., : model // 2]], "j", 0)
+    high_sends = sends_of([up_part[:, :, 1], grad_out[..., model // 2 :]], "b", 3)
+    grad_heads, down_sends, low_sends, high_sends = together(
+        grad_heads, down_sends, low_sends, high_sends
     )
 
     def backward(pair, grads):
@@ -1036,53 +1179,55 @@
             table, pair, queries, keys, values, attended, grads, lse, cosine, sine
         )
 
+    units = jh * unit
     low_came, high_came = send(low_sends, "j"), send(high_sends, "b")
-    down_came, out_came = send(down_sends, "a"), send(out_sends, "j")
+    down_came = send(down_sends, "a")
     grad_pairs = [backward(0, grad_heads)]
-    grad_pairs, down_came, low_came, high_came, out_came = together(
-        grad_pairs, down_came, low_came, high_came, out_came
-    )
-    down_part = added(down_sends, down_came, (na // 2, n_down, model))
-    down_sends = scatter_sends(down_part, "a", 0, 2)
-    low_part = scatter_axis(added(low_sends, low_came, (nh, na, nb, part, jh * unit)), "h", 0)
-    low_sends = sends(low_part, "b", 1)
-    high_sends = sends(added(high_sends, high_came, (2, nh, na, part, jh * unit)), "j", 0)
-    out_part = scatter_axis(added(out_sends, out_came, (nh, na, nb, part, model)), "h", 0)
-    out_sends = sends(out_part, "b", 1)
+    grad_pairs, down_came, low_came, high_came = together(
+        grad_pairs, down_came, low_came, high_came
+    )
     weight_pairs = [dot(normed, grad_pairs[0], TN).astype(BF)]
+    low_pieces = [(low_sends[0][0], low_came, 0), (low_sends[0][1], low_came, units)]
+    high_pieces = [(high_sends[0][0], high_came, 0), (high_sends[0][1], high_came, units)]
+    down_pieces = [(down_sends[0][0], down_came, 0), (down_sends[0][1], down_came, model)]
+    low_sends, high_sends, down_sends = relay(
+        [
+            (half_b, (na, halves_b, part), low_pieces),
+            (ij, (1, 2, nh * na * part), high_pieces),
+            (next_bit, (na // 4, 2, cut), down_pieces),
+        ],
+        views,
+    )
     heads_in = [
         lax.all_to_all(weight_pairs[0].reshape(devices, part, 384), AXES, 0, 0, tiled=True)
     ]
     if pairs > 1:
-        grad_heads, down_sends, low_sends, high_sends, out_sends, weight_pairs = together(
-            grad_heads, down_sends, low_sends, high_sends, out_sends, weight_pairs
+        grad_heads, down_sends, low_sends, high_sends, weight_pairs = together(
+            grad_heads, down_sends, low_sends, high_sends, weight_pairs
         )
     down_came, low_came = flip(down_sends[1], "a", 2), send(low_sends, "b")
-    high_came, out_came = send(high_sends, "j"), send(out_sends, "b")
+    high_came = send(high_sends, "j")
     if pairs > 1:
         grad_pairs.append(backward(1, grad_heads))
     grads_give = [d for d in range(group) if d & core_bit]
     block_order = [2 * d + r for d in grads_give for r in range(2)]
     block_order += [2 * (d ^ core_bit) + r for d in grads_give for r in range(2)]
-    grad_pairs, down_came, low_came, high_came, out_came, heads_in = together(
-        grad_pairs, down_came, low_came, high_came, out_came, heads_in
+    grad_pairs, down_came, low_came, high_came, heads_in = together(
+        grad_pairs, down_came, low_came, high_came, heads_in
     )
     grad_give, grad_keep = input_grad(
         positions_of[jnp.array(block_order, jnp.int32)], grad_pairs, w_heads, rows
     )
-    grad_give, grad_keep, down_came, low_came, high_came, out_came, grad_pairs = together(
-        grad_give, grad_keep, down_came, low_came, high_came, out_came, grad_pairs
+    grad_give, grad_keep, down_came, low_came, high_came, grad_pairs = together(
+        grad_give, grad_keep, down_came, low_came, high_came, grad_pairs
     )
     give_came = by_offset(grad_give, core_bit)
-    rest_part = jnp.concatenate(
-        [
-            added(low_sends, low_came, (na, part, jh * unit)),
-            scatter_axis(added(high_sends, high_came, (nh, na, part, jh * unit)), "h", 0),
-            added(out_sends, out_came, (na, part, model)),
-        ],
-        axis=2,
-    )
-    rest_sends = sends(rest_part, "a", 0)
+    rest_pieces = [
+        (x, came, at)
+        for (kept, _), came in ((low_sends, low_came), (high_sends, high_came))
+        for x, at in zip(kept, (0, units))
+    ]
+    (rest_sends,) = relay([(low_bit, (na // 2, 2, part), rest_pieces)], views)
     give_came, rest_sends, grad_keep = together(give_came, rest_sends, grad_keep)
     rest_came = send(rest_sends, "a")
 
@@ -1105,24 +1250,37 @@
         )
     for x in weight_pairs:
         heads_in.append(lax.all_to_all(x.reshape(devices, part, 384), AXES, 0, 0, tiled=True))
-    rest_part = added(rest_sends, rest_came, (na // 2, part, -1))
-    rest_part = scatter_axis(rest_part, "a", 0, 2)
-    down_part = join(down_sends[0], down_came).reshape(na // 4, n_down, model)
-    down_part = scatter_axis(down_part, "a", 0, 4)
+    starts = (0, units, units + model // 2, 2 * units + model // 2)
+    rest_pieces = [(x, rest_came, at) for x, at in zip(rest_sends[0], starts)]
+    (rest_sends,) = relay([(next_bit, (na // 4, 2, part), rest_pieces)], views)
+    rest_came = flip(rest_sends[1], "a", 2)
+    if far_bits:
+        final[1], rest_came = together(final[1], rest_came)
+    down_parts = added_of(down_sends[0], down_came, (na // 4, cut))
+    down_part = jnp.concatenate([scatter_axis(x, "a", 0, 4) for x in down_parts])
     block_out = ordered(*block_came)
 
-    small, grad_tokens = mo_sums + turn_sums, []
+    small, totals = mo_sums + turn_sums, []
     for r in range(2):
         parts = [sums[0][r]] + ([final[r]] if far_bits else [])
         total, sums_in = row_call(
             last_kernel, "last", 2, rows,
-            [own[r], grad_residual[r * rows : (r + 1) * rows]] + parts, [], [vectors],
+            [own[r], (grad_residual, r)] + parts, [], [vectors],
             [(model, BF)],
         )
         small = small + sums_in
         if r == 0 and far_bits:
             total, final[1] = together(total, final[1])
-        grad_tokens.append(restore(total, r))
+        totals.append(total)
+    small = small.reshape(8, 2, nh, 2, na, nb, part).transpose(4, 3, 5, 1, 2, 0, 6)
+    small = scatter_axis(small, "a", 0, kind=F32)
+    small, totals = together(small, totals)
+    grad_tokens = [restore(totals[0], 0)]
+    grad_tokens.append(restore(totals[1], 1))
+    rest_parts = added_of(rest_sends[0], rest_came, (na // 4, part))
+    low_up, low_out, high_up, high_out = (scatter_axis(x, "a", 0, 4) for x in rest_parts)
+    for axis in ("c", "b", "j", "h"):
+        small = scatter_axis(small, axis, 0, kind=F32)
     grad_tokens = ordered(*grad_tokens)
 
     def spread(m):
@@ -1130,8 +1288,8 @@
         return [place(j, hc // 2, hc % 2, a, b) for j in range(2) for a in range(na)]
 
     g_query, g_key, g_value = head_sum(heads_in, group, spread)
-    g_down, g_out = down_part.astype(F32), rest_part[:, 2 * jh * unit :].astype(F32)
-    up_part = jnp.stack([rest_part[:, n * jh * unit : (n + 1) * jh * unit] for n in range(2)])
+    g_down, g_out = down_part.astype(F32), jnp.concatenate([low_out, high_out], axis=1).astype(F32)
+    up_part = jnp.stack([low_up, high_up])
     up_keep = lax.dynamic_index_in_dim(up_part, ic, 0, keepdims=False).reshape(part, jh, unit)
     up_give = lax.dynamic_index_in_dim(up_part, 1 - ic, 0, keepdims=False)
     up_come = flip(up_give, "c", 1).reshape(part, jh, unit)
@@ -1139,9 +1297,6 @@
         ic == 0, jnp.stack([up_keep, up_come], axis=2), jnp.stack([up_come, up_keep], axis=2)
     ).reshape(part, ff).astype(F32)
 
-    small = small.reshape(8, 2, nh, 2, na, nb, part).transpose(3, 5, 1, 2, 4, 0, 6)
-    for axis in ("c", "b", "j", "h", "a"):
-        small = scatter_axis(small, axis, 0, kind=F32)
     return (
         block_out, grad_tokens, g_query, g_key, g_value, g_out, g_up, g_down,
         small[0], small[1], small[2], small[3], small[4], small[5], small[6], small[7],

time: 538 us -> 517 us (0.961)
  starting transfers between devices: 115 us -> 87.8 us
  Pallas kernels: 150 us -> 175 us
  other arithmetic: 43.9 us -> 25.4 us
  local copies, waits for them, and re-layouts: 48.9 us -> 39.2 us
  matrix products: 20.7 us -> 27.4 us
    ppermute x47 -> x40, starting transfers between devices: 59.9 us -> 34.8 us  [flip(): return lax.ppermute(x, axis, [(i, i ^ bit) for i in range(size)])]
    ppermute x12, waiting for transfers between devices: 52.7 us -> 27.7 us  [by_offset(): return lax.ppermute(x, AXES, sends)]
    pallas_call x0 -> x6, Pallas kernels: none -> 20.6 us  [the longest x5 18.2 us: relay(): pl.pallas_call(functools.partial(relay_kernel, layout=tuple(layout), arri...]
    all_to_all x0 -> x1, waiting for transfers between devices: none -> 20.3 us  [body(): vectors = lax.all_to_all(vectors, AXES, 0, 0, tiled=True)]
    ppermute x4, waiting for transfers between devices: 3.12 us -> 17.7 us  [restore(): return lax.ppermute(x, AXES, [(there, here) for here, there in moves[turn]])]
    convert_element_type x14 -> x2, other arithmetic: 14.9 us -> 3.87 us  [join(): return (mine.astype(F32) + came.astype(F32)).astype(kind)]
    ppermute x12, starting transfers between devices: 21.4 us -> 10.6 us  [by_offset(): return lax.ppermute(x, AXES, sends)]
    concatenate x15 -> x6, other arithmetic: 12.7 us -> 2.72 us  [grow(): return jnp.concatenate([x, came])]
  transfers between devices with their start and end apart: 70 -> 64, of which waited for: 26 -> 27; matrix products, arithmetic and copies ran while one was open for 15% -> 10% of each run, Pallas kernels for 26% -> 30%
where the time goes in v3:
time: 517 us; the launch traced here: 510 us
  Pallas kernels  175 us (34%)
  waiting for transfers between devices  153 us (30%)
  starting transfers between devices  87.8 us (17%)
  local copies, waits for them, and re-layouts  39.2 us (8%)
  matrix products  27.4 us (5%)
  other arithmetic  25.4 us (5%)
    ppermute x40, waiting for transfers between devices, flip(): return lax.ppermute(x, axis, [(i, i ^ bit) for i in range(size)])  84.1 us
    pallas_call x2, Pallas kernels, attention_backward(): pl.pallas_call(functools.partial(backward_kernel, bk=bk, rows=rows), out_...  48.7 us
    pallas_call x3, Pallas kernels, mlp_call(): pl.pallas_call(functools.partial(kernel, tables=len(tables)), out_shape=[...  42.5 us
    ppermute x40, starting transfers between devices, flip(): return lax.ppermute(x, axis, [(i, i ^ bit) for i in range(size)])  34.8 us
    ppermute x12, waiting for transfers between devices, by_offset(): return lax.ppermute(x, AXES, sends)  27.7 us
    dot_general x8, matrix products, dot(): return lax.dot_general(left, right, dims, preferred_element_type=F32)  27.4 us
    all_to_all x1, waiting for transfers between devices, body(): vectors = lax.all_to_all(vectors, AXES, 0, 0, tiled=True)  20.3 us
    pallas_call x1, Pallas kernels, attention_forward(): pl.pallas_call(functools.partial(forward_kernel, bq=bq, bk=bk, rows=rows)...  19.5 us
  transfers between devices with their start and end apart: 64, of which 27 were waited for; matrix products, arithmetic and copies ran while one was open for 10% of the time, Pallas kernels for 30%

profile of v3, /device:TPU:1, one launch (start us, length us, event | category | flops | bytes accessed | tf_op | source)
XLA Modules:
  0.0 510.1 jit_solution(368369176398849925)
XLA Ops:
  3.9 5.7 %collective-permute-start = (bf16[256,1024]{1,0:T(8,128)(2,1)}, bf16[256,1024]{1,0:T(8,128)(2,1)S(1)}, u32[]{:S(2)}, u32[]{:S(2)}) collective-permute-start(bf16[256,1024]{1,0:T(8,128)(2,1)} %get-tuple-element.465), channel_id=1, source_target_pairs={{0,0},{1,1},{2,8},{3,9},{4,2},{5,3},{6,10},{7,11},{8,4},{9,5},{10,... | collective-permute-start | bytes 1572872 | tf_op jit(solution)/shard_map/ppermute | solution.py:896
  28.3 5.6 %fusion.11 = (f32[2048,128]{1,0:T(8,128)}, f32[2048,128]{1,0:T(8,128)}) fusion(f32[128]{0:T(128)S(1)} %get-tuple-element.498, f32[128]{0:T(128)S(1)} %get-tuple-element.499, f32[2048]{0:T(1024)S(1)} %iota_convert_fusion), kind=kLoop, calls=%fused_computation.30 | loop fusion | flops 524288 | bytes 2106368 | tf_op jit(solution)/shard_map/mul | solution.py:959
  36.2 20.3 %all-to-all-done.1 = bf16[32,2,128]{2,1,0:T(2,128)(2,1)S(1)} async-done(((bf16[32,2,128]{2,1,0:T(2,128)(2,1)}), bf16[32,2,128]{2,1,0:T(2,128)(2,1)S(1)}, u32[]{:S(2)}, u32[]{:S(2)}) %all-to-all-start.1) | async-done | bytes 16416 | tf_op jit(solution)/shard_map/all_to_all | solution.py:969
  59.6 13.5 %collective-permute-done.7 = bf16[2,160,1024]{2,1,0:T(8,128)(2,1)S(1)} collective-permute-done((bf16[2,160,1024]{2,1,0:T(8,128)(2,1)S(1)}, bf16[2,160,1024]{2,1,0:T(8,128)(2,1)S(1)}, u32[]{:S(2)}, u32[]{:S(2)}) %collective-permute-start.7) | collective-permute-done | bytes 655392 | tf_op jit(solution)/shard_map/ppermute | solution.py:789
  76.4 9.9 %collective-permute-done.9 = bf16[1,128,1024]{2,1,0:T(8,128)(2,1)S(1)} collective-permute-done((bf16[1,128,1024]{2,1,0:T(8,128)(2,1)S(1)}, bf16[1,128,1024]{2,1,0:T(8,128)(2,1)S(1)}, u32[]{:S(2)}, u32[]{:S(2)}) %collective-permute-start.9) | collective-permute-done | bytes 262176 | tf_op jit(solution)/shard_map/ppermute | solution.py:789
  94.6 13.8 %collective-permute-done.13 = bf16[4,80,1024]{2,1,0:T(8,128)(2,1)S(1)} collective-permute-done((bf16[4,80,1024]{2,1,0:T(8,128)(2,1)S(1)}, bf16[4,80,1024]{2,1,0:T(8,128)(2,1)S(1)}, u32[]{:S(2)}, u32[]{:S(2)}) %collective-permute-start.13) | collective-permute-done | bytes 655392 | tf_op jit(solution)/shard_map/ppermute | solution.py:789
  121.0 13.9 %qkv.1 = (bf16[2048,1024]{1,0:T(8,128)(2,1)}, bf16[2048,256]{1,0:T(8,128)(2,1)}, bf16[2048,256]{1,0:T(8,128)(2,1)}, bf16[2048,256]{1,0:T(8,128)(2,1)}, bf16[1024,768]{1,0:T(8,128)(2,1)}) custom-call(s32[8]{0:T(128)} %get-tuple-element.500.table, s32[8]{0:T(128)} %xor_add_fusion.2.order, bf16[2,256,1024]{2,1,0:T(8,128)(2,1)} %copy-done.40, ...), custom_call_target="tpu_custom_call" | custom-call | flops 11000000 | bytes 1024 | tf_op jit(solution)/shard_map/qkv/pallas_call | solution.py:86
  134.9 19.5 %attention_forward.1 = (bf16[8,256,256]{2,1,0:T(8,128)(2,1)}, f32[2048,256]{1,0:T(8,128)}) custom-call(s32[8]{0:T(128)} %get-tuple-element.501.table, bf16[2048,256]{1,0:T(8,128)(2,1)} %get-tuple-element.251.q_ref, bf16[2048,256]{1,0:T(8,128)(2,1)} %get-tuple-element.252.k_ref, bf16[2048,256]{1,0:T(8,128)(2,1)} %get-tuple-element.253.v_ref), custom_call_target="tpu_custom_call" | custom-call | flops 23000000 | bytes 1024 | tf_op jit(solution)/shard_map/attention_forward/pallas_call | solution.py:167
  165.7 6.5 %collective-permute-done.20.refs_3_ = bf16[512,256]{1,0:T(8,128)(2,1)S(1)} collective-permute-done((bf16[512,256]{1,0:T(8,128)(2,1)S(1)}, bf16[512,256]{1,0:T(8,128)(2,1)S(1)}, u32[]{:S(2)}, u32[]{:S(2)}) %collective-permute-start.20) | collective-permute-done | bytes 262176 | tf_op jit(solution)/shard_map/ppermute | solution.py:910
  181.0 11.7 %collective-permute-done.23.refs_3_.refs_9_ = bf16[4,128,1024]{2,1,0:T(8,128)(2,1)S(1)} collective-permute-done((bf16[4,128,1024]{2,1,0:T(8,128)(2,1)}, bf16[4,128,1024]{2,1,0:T(8,128)(2,1)S(1)}, u32[]{:S(2)}, u32[]{:S(2)}) %collective-permute-start.23) | collective-permute-done | bytes 1048608 | tf_op jit(solution)/shard_map/ppermute | solution.py:789
  195.7 12.9 %mlp_up.1 = (bf16[1024,2048]{1,0:T(8,128)(2,1)}, bf16[1024,2048]{1,0:T(8,128)(2,1)}) custom-call(s32[3,16]{1,0:T(4,128)} %copy-done.29, bf16[512,1024]{1,0:T(8,128)(2,1)} %copy-done.27, bf16[512,1024]{1,0:T(8,128)(2,1)} %collective-permute-done.22.refs_2_, bf16[8,80,1024]{2,1,0:T(8,128)(2,1)} %pad_maximum_fusion.2.refs_0_.refs_3_.refs_4_, ...), custom_call_target="tpu_custom_call" | custom-call | flops 11000000 | bytes 1024 | tf_op jit(solution)/shard_map/mlp_up/pallas_call | solution.py:451
  209.6 10.4 %mlp_down.1 = (f32[512,1024]{1,0:T(8,128)}, bf16[512,1024]{1,0:T(8,128)(2,1)}) custom-call(s32[3,16]{1,0:T(4,128)} %copy-done.29, bf16[1024,2048]{1,0:T(8,128)(2,1)} %get-tuple-element.271.refs_1_, bf16[4,128,1024]{2,1,0:T(8,128)(2,1)} %pad_maximum_fusion.7.refs_2_.refs_8_, bf16[4,128,1024]{2,1,0:T(8,128)(2,1)} %copy-done.38, ...), custom_call_target="tpu_custom_call" | custom-call | flops 9000000 | bytes 1024 | tf_op jit(solution)/shard_map/mlp_down/pallas_call | solution.py:451
  232.4 7.4 %convolution_convert_fusion.1 = bf16[2048,1024]{1,0:T(8,128)(2,1)S(1)} fusion(bf16[1024,2048]{1,0:T(8,128)(2,1)} %get-tuple-element.271.refs_1_, bf16[512,1024]{1,0:T(8,128)(2,1)S(1)} %collective-permute-done.29.refs_2_, bf16[512,1024]{1,0:T(8,128)(2,1)} %get-tuple-element.284.refs_1_), kind=kOutput, calls=%fused_computation.3 | convolution fusion | flops 4301258752 | bytes 10485760 | tf_op jit(solution)/shard_map/dot_general | solution.py:30
  250.3 19.3 %mlp_backward.1 = (bf16[1024,2048]{1,0:T(8,128)(2,1)}, f32[512,1024]{1,0:T(8,128)}, bf16[512,1024]{1,0:T(8,128)(2,1)}) custom-call(s32[3,16]{1,0:T(4,128)} %copy-done.29, bf16[512,1024]{1,0:T(8,128)(2,1)} %get-tuple-element.284.refs_1_, bf16[512,1024]{1,0:T(8,128)(2,1)} %copy-done.49, bf16[1024,2048]{1,0:T(8,128)(2,1)} %get-tuple-element.286.refs_3_, ...), custom_call_target="tpu_custom_call" | custom-call | flops 20000000 | bytes 1024 | tf_op jit(solution)/shard_map/mlp_backward/pallas_call | solution.py:451
  279.5 9.1 %turn.1 = (f32[512,1024]{1,0:T(8,128)}, bf16[512,1024]{1,0:T(8,128)(2,1)}, bf16[512,256]{1,0:T(8,128)(2,1)}, bf16[512,256]{1,0:T(8,128)(2,1)}, bf16[512,256]{1,0...) custom-call(f32[512,1024]{1,0:T(8,128)} %get-tuple-element.303.own_ref, bf16[512,1024]{1,0:T(8,128)(2,1)} %copy-done.50, ...), custom_call_target="tpu_custom_call" | custom-call | flops 6000000 | bytes 1024 | tf_op jit(solution)/shard_map/turn/pallas_call | solution.py:702
  304.0 7.1 %convolution_convert_fusion = bf16[1024,2048]{1,0:T(8,128)(2,1)S(1)} fusion(bf16[1024,2048]{1,0:T(8,128)(2,1)} %get-tuple-element.330, bf16[512,1024]{1,0:T(8,128)(2,1)} %collective-permute-done.22.refs_2_, bf16[512,1024]{1,0:T(8,128)(2,1)S(1)} %copy-done.28), kind=kOutput, calls=%fused_computation.2 | convolution fusion | flops 4301258752 | bytes 10485760 | tf_op jit(solution)/shard_map/dot_general | solution.py:30
  321.7 24.3 %attention_backward.2.refs_0_ = bf16[2048,384]{1,0:T(8,128)(2,1)} custom-call(s32[8]{0:T(128)} %get-tuple-element.501.table, bf16[2048,256]{1,0:T(8,128)(2,1)} %get-tuple-element.251.q_ref, bf16[2048,256]{1,0:T(8,128)(2,1)} %get-tuple-element.252.k_ref, bf16[2048,256]{1,0:T(8,128)(2,1)} %get-tuple-element.253.v_ref, ...), custom_call_target="tpu_custom_call" | custom-call | flops 44000000 | bytes 1024 | tf_op jit(solution)/shard_map/attention_backward/pallas_call | solution.py:302
  350.8 6.5 %convolution_convert_fusion.3 = bf16[1024,384]{1,0:T(8,128)(2,1)} fusion(bf16[2048,1024]{1,0:T(8,128)(2,1)} %get-tuple-element.356, bf16[2048,384]{1,0:T(8,128)(2,1)} %attention_backward.2.refs_0_), kind=kOutput, calls=%fused_computation.17 | convolution fusion | flops 1611005952 | bytes 6553600 | tf_op jit(solution)/shard_map/dot_general | solution.py:30
  363.2 5.7 %relay.7 = (bf16[4,32,2048]{2,1,0:T(8,128)(2,1)}, bf16[4,32,512]{2,1,0:T(8,128)(2,1)}, bf16[1,128,2048]{2,1,0:T(8,128)(2,1)}, bf16[1,128,512]{2,1,0:T(8,128)(2,1...) custom-call(s32[3]{0:T(128)} %pad_add_fusion.2.here, ...), custom_call_target="tpu_custom_call" | custom-call | flops 4000000 | bytes 1024 | tf_op jit(solution)/shard_map/relay/pallas_call | solution.py:530
  374.3 24.4 %attention_backward.3.refs_1_ = bf16[2048,384]{1,0:T(8,128)(2,1)} custom-call(s32[8]{0:T(128)} %get-tuple-element.501.table, bf16[2048,256]{1,0:T(8,128)(2,1)} %get-tuple-element.251.q_ref, bf16[2048,256]{1,0:T(8,128)(2,1)} %get-tuple-element.252.k_ref, bf16[2048,256]{1,0:T(8,128)(2,1)} %get-tuple-element.253.v_ref, ...), custom_call_target="tpu_custom_call" | custom-call | flops 44000000 | bytes 1024 | tf_op jit(solution)/shard_map/attention_backward/pallas_call | solution.py:302
  401.9 7.7 %input_grad.1 = (bf16[4,256,1024]{2,1,0:T(8,128)(2,1)}, bf16[4,256,1024]{2,1,0:T(8,128)(2,1)S(1)}) custom-call(s32[8]{0:T(128)S(1)} %gather_fusion, bf16[2048,384]{1,0:T(8,128)(2,1)S(1)} %copy-done.6, bf16[2048,384]{1,0:T(8,128)(2,1)S(1)} %copy-done.4, bf16[1024,768]{1,0:T(8,128)(2,1)S(1)} %copy-done.24), custom_call_target="tpu_custom_call" | custom-call | flops 6000000 | bytes 1024 | tf_op jit(solution)/shard_map/input_grad/pallas_call | solution.py:742
  441.8 10.9 %collective-permute-done.50.refs_1_ = bf16[256,1024]{1,0:T(8,128)(2,1)} collective-permute-done((bf16[256,1024]{1,0:T(8,128)(2,1)}, bf16[256,1024]{1,0:T(8,128)(2,1)}, u32[]{:S(2)}, u32[]{:S(2)}) %collective-permute-start.50) | collective-permute-done | bytes 524320 | tf_op jit(solution)/shard_map/ppermute | solution.py:910
  452.7 12.1 %collective-permute-done.51 = bf16[1,32,5120]{2,1,0:T(8,128)(2,1)S(1)} collective-permute-done((bf16[1,32,5120]{2,1,0:T(8,128)(2,1)}, bf16[1,32,5120]{2,1,0:T(8,128)(2,1)S(1)}, u32[]{:S(2)}, u32[]{:S(2)}) %collective-permute-start.51) | collective-permute-done | bytes 327712 | tf_op jit(solution)/shard_map/ppermute | solution.py:789
  497.7 11.1 %collective-permute-done.55 = bf16[256,1024]{1,0:T(8,128)(2,1)S(1)} collective-permute-done((bf16[256,1024]{1,0:T(8,128)(2,1)S(1)}, bf16[256,1024]{1,0:T(8,128)(2,1)S(1)}, u32[]{:S(2)}, u32[]{:S(2)}) %collective-permute-start.55) | collective-permute-done | bytes 524320 | tf_op jit(solution)/shard_map/ppermute | solution.py:899
  (425 shorter events, 218.5 us)
Async XLA Ops:
  3.9 53.5 %collective-permute-start = (bf16[256,1024]{1,0:T(8,128)(2,1)}, bf16[256,1024]{1,0:T(8,128)(2,1)S(1)}, u32[]{:S(2)}, u32[]{:S(2)}) collective-permute-start(bf16[256,1024]{1,0:T(8,128)(2,1)} %get-tuple-element.465), channel_id=1, source_target_pairs={{0,0},{1,1},{2,8},{3,9},{4,2},{5,3},{6,10},{7,11},{8,4},{9,5},{10,... | collective-permute-start | bytes 1572872 | tf_op jit(solution)/shard_map/ppermute | solution.py:896
  9.6 47.7 %collective-permute-start.1 = (bf16[256,1024]{1,0:T(8,128)(2,1)}, bf16[256,1024]{1,0:T(8,128)(2,1)S(1)}, u32[]{:S(2)}, u32[]{:S(2)}) collective-permute-start(bf16[256,1024]{1,0:T(8,128)(2,1)} %get-tuple-element.464), channel_id=1, source_target_pairs={{0,2},{1,3},{2,10},{3,11},{4,0},{5,1},{6,8},{7,9},{8,6},{9,7},{10,... | collective-permute-start | bytes 1572872 | tf_op jit(solution)/shard_map/ppermute | solution.py:896
  19.9 37.4 %collective-permute-start.3 = (bf16[1,160,1024]{2,1,0:T(8,128)(2,1)S(1)}, bf16[1,160,1024]{2,1,0:T(8,128)(2,1)S(1)}, u32[]{:S(2)}, u32[]{:S(2)}) collective-permute-start(bf16[1,160,1024]{2,1,0:T(8,128)(2,1)S(1)} %maximum_bitcast_fusion), channel_id=1, source_target_pairs={{0,4},{2,6},{4,0},{6,2},{1,5},{3,7},{5,1},{7,3},{8,12},{10,14},{12... | collective-permute-start | bytes 983048 | tf_op jit(solution)/shard_map/ppermute | solution.py:789
  23.9 32.5 %all-to-all-start.1 = ((bf16[32,2,128]{2,1,0:T(2,128)(2,1)}), bf16[32,2,128]{2,1,0:T(2,128)(2,1)S(1)}, u32[]{:S(2)}, u32[]{:S(2)}) async-start(bf16[32,2,128]{2,1,0:T(2,128)(2,1)} %reshape.318), calls=%async_computation.1 | async-start | bytes 32768 | tf_op jit(solution)/shard_map/all_to_all | solution.py:969
  58.0 30.5 %collective-permute-start.5 = (bf16[2,256,1024]{2,1,0:T(8,128)(2,1)S(1)}, bf16[2,256,1024]{2,1,0:T(8,128)(2,1)S(1)}, u32[]{:S(2)}, u32[]{:S(2)}) collective-permute-start(bf16[2,256,1024]{2,1,0:T(8,128)(2,1)S(1)} %pad_maximum_fusion.6.refs_0_), channel_id=1, source_target_pairs={{0,1},{1,0},{2,3},{3,2},{4,5},{5,4},{6,7},{7,6},{8,9},{9,8},{10,11... | collective-permute-start | bytes 3145736 | tf_op jit(solution)/shard_map/ppermute | solution.py:910
  58.3 30.2 %collective-permute-start.6 = (bf16[2,256,1024]{2,1,0:T(8,128)(2,1)S(1)}, bf16[2,256,1024]{2,1,0:T(8,128)(2,1)S(1)}, u32[]{:S(2)}, u32[]{:S(2)}) collective-permute-start(bf16[2,256,1024]{2,1,0:T(8,128)(2,1)S(1)} %pad_maximum_fusion.6.refs_0_), channel_id=1, source_target_pairs={{0,8},{1,9},{2,10},{3,11},{4,12},{5,13},{6,14},{7,15},{8,0},{9,1},... | collective-permute-start | bytes 3145736 | tf_op jit(solution)/shard_map/ppermute | solution.py:910
  112.5 41.9 %collective-permute-start.15 = (bf16[8,80,1024]{2,1,0:T(8,128)(2,1)}, bf16[8,80,1024]{2,1,0:T(8,128)(2,1)}, u32[]{:S(2)}, u32[]{:S(2)}) collective-permute-start(bf16[8,80,1024]{2,1,0:T(8,128)(2,1)} %pad_maximum_fusion.2.refs_0_.refs_3_.refs_4_), channel_id=1, source_target_pairs={{0,16},{16,0},{1,17},{17,1},{2,18},{18,2},{3,19},{19,3},{4,20},{20... | collective-permute-start | bytes 3932168 | tf_op jit(solution)/shard_map/ppermute | solution.py:789
  114.0 40.5 %collective-permute-start.16 = (bf16[8,80,1024]{2,1,0:T(8,128)(2,1)S(1)}, bf16[8,80,1024]{2,1,0:T(8,128)(2,1)}, u32[]{:S(2)}, u32[]{:S(2)}) collective-permute-start(bf16[8,80,1024]{2,1,0:T(8,128)(2,1)S(1)} %pad_maximum_fusion.3.refs_2_.refs_5_.refs_6_), channel_id=1, source_target_pairs={{0,1},{1,0},{2,3},{3,2},{4,5},{5,4},{6,7},{7,6},{8,9},{9,8},{10,11... | collective-permute-start | bytes 3932168 | tf_op jit(solution)/shard_map/ppermute | solution.py:789
  114.8 39.6 %collective-permute-start.17 = (bf16[256,1024]{1,0:T(8,128)(2,1)}, bf16[256,1024]{1,0:T(8,128)(2,1)S(1)}, u32[]{:S(2)}, u32[]{:S(2)}) collective-permute-start(bf16[256,1024]{1,0:T(8,128)(2,1)} %dynamic-slice_bitcast_fusion.6), channel_id=1, source_target_pairs={{0,0},{1,1},{2,8},{3,9},{4,2},{5,3},{6,10},{7,11},{8,4},{9,5},{10,... | collective-permute-start | bytes 1572872 | tf_op jit(solution)/shard_map/ppermute | solution.py:896
  159.5 33.3 %collective-permute-start.23 = (bf16[4,128,1024]{2,1,0:T(8,128)(2,1)}, bf16[4,128,1024]{2,1,0:T(8,128)(2,1)S(1)}, u32[]{:S(2)}, u32[]{:S(2)}) collective-permute-start(bf16[4,128,1024]{2,1,0:T(8,128)(2,1)} %pad_maximum_fusion.7.refs_2_.refs_8_), channel_id=1, source_target_pairs={{0,1},{1,0},{2,3},{3,2},{4,5},{5,4},{6,7},{7,6},{8,9},{9,8},{10,11... | collective-permute-start | bytes 3145736 | tf_op jit(solution)/shard_map/ppermute | solution.py:789
  164.7 28.1 %collective-permute-start.24 = (bf16[4,128,1024]{2,1,0:T(8,128)(2,1)}, bf16[4,128,1024]{2,1,0:T(8,128)(2,1)S(1)}, u32[]{:S(2)}, u32[]{:S(2)}) collective-permute-start(bf16[4,128,1024]{2,1,0:T(8,128)(2,1)} %pad_maximum_fusion.7.refs_2_.refs_8_), channel_id=1, source_target_pairs={{0,16},{16,0},{1,17},{17,1},{2,18},{18,2},{3,19},{19,3},{4,20},{20... | collective-permute-start | bytes 3145736 | tf_op jit(solution)/shard_map/ppermute | solution.py:789
  179.7 28.9 %collective-permute-start.25 = (bf16[256,1024]{1,0:T(8,128)(2,1)}, bf16[256,1024]{1,0:T(8,128)(2,1)S(1)}, u32[]{:S(2)}, u32[]{:S(2)}) collective-permute-start(bf16[256,1024]{1,0:T(8,128)(2,1)} %dynamic-slice_bitcast_fusion.5), channel_id=1, source_target_pairs={{0,2},{1,3},{2,10},{3,11},{4,0},{5,1},{6,8},{7,9},{8,6},{9,7},{10,... | collective-permute-start | bytes 1572872 | tf_op jit(solution)/shard_map/ppermute | solution.py:896
  242.9 29.1 %collective-permute-start.30 = (bf16[2,1,4,1,64,1024]{5,4,3,2,1,0:T(8,128)(2,1)S(1)}, bf16[2,1,4,1,64,1024]{5,4,3,2,1,0:T(8,128)(2,1)S(1)}, u32[]{:S(2)}, u32[]{:S(2)}) collective-permute-start(bf16[2,1,4,1,64,1024]{5,4,3,2,1,0:T(8,128)(2,1)S(1)} %get-tuple-element.290), channel_id=1, source_target_pairs={{0,1},{1,0},{2,3},{3,2},{4,5},{5,4},{6,7},{7,6},{8,9},{9,8},{10,11... | collective-permute-start | bytes 3145736 | tf_op jit(solution)/shard_map/ppermute | solution.py:789
  243.6 28.4 %collective-permute-start.31 = (bf16[1,1,4,2,64,1024]{5,4,3,2,1,0:T(8,128)(2,1)S(1)}, bf16[1,1,4,2,64,1024]{5,4,3,2,1,0:T(8,128)(2,1)S(1)}, u32[]{:S(2)}, u32[]{:S(2)}) collective-permute-start(bf16[1,1,4,2,64,1024]{5,4,3,2,1,0:T(8,128)(2,1)S(1)} %get-tuple-element.291), channel_id=1, source_target_pairs={{0,16},{16,0},{1,17},{17,1},{2,18},{18,2},{3,19},{19,3},{4,20},{20... | collective-permute-start | bytes 3145736 | tf_op jit(solution)/shard_map/ppermute | solution.py:789
  244.4 27.7 %collective-permute-start.32 = (bf16[256,1024]{1,0:T(8,128)(2,1)S(1)}, bf16[256,1024]{1,0:T(8,128)(2,1)S(1)}, u32[]{:S(2)}, u32[]{:S(2)}) collective-permute-start(bf16[256,1024]{1,0:T(8,128)(2,1)S(1)} %get-tuple-element.459), channel_id=1, source_target_pairs={{0,0},{1,1},{8,2},{9,3},{2,4},{3,5},{10,6},{11,7},{4,8},{5,9},{12,... | collective-permute-start | bytes 1572872 | tf_op jit(solution)/shard_map/ppermute | solution.py:899
  320.0 30.5 %collective-permute-start.42 = (bf16[1,1,4,2,32,2560]{5,4,3,2,1,0:T(8,128)(2,1)S(1)}, bf16[1,1,4,2,32,2560]{5,4,3,2,1,0:T(8,128)(2,1)S(1)}, u32[]{:S(2)}, u32[]{:S(2)}) collective-permute-start(bf16[1,1,4,2,32,2560]{5,4,3,2,1,0:T(8,128)(2,1)S(1)} %pad_maximum_fusion.4), channel_id=1, source_target_pairs={{0,16},{16,0},{1,17},{17,1},{2,18},{18,2},{3,19},{19,3},{4,20},{20... | collective-permute-start | bytes 3932168 | tf_op jit(solution)/shard_map/ppermute | solution.py:789
  320.7 30.1 %collective-permute-start.43 = (bf16[2,1,4,1,32,2560]{5,4,2,0,3,1:T(8,128)(2,1)S(1)}, bf16[2,1,4,1,32,2560]{5,4,2,0,3,1:T(8,128)(2,1)S(1)}, u32[]{:S(2)}, u32[]{:S(2)}) collective-permute-start(bf16[2,1,4,1,32,2560]{5,4,2,0,3,1:T(8,128)(2,1)S(1)} %pad_maximum_fusion.5), channel_id=1, source_target_pairs={{0,1},{1,0},{2,3},{3,2},{4,5},{5,4},{6,7},{7,6},{8,9},{9,8},{10,11... | collective-permute-start | bytes 3932168 | tf_op jit(solution)/shard_map/ppermute | solution.py:789
  357.3 41.3 %all-to-all-start.2 = ((bf16[32,32,384]{2,1,0:T(8,128)(2,1)}), bf16[32,32,384]{2,1,0:T(8,128)(2,1)S(1)}, u32[]{:S(2)}, u32[]{:S(2)}) async-start(bf16[32,32,384]{2,1,0:T(8,128)(2,1)} %bitcast.76), calls=%async_computation.2 | async-start | bytes 1572864 | tf_op jit(solution)/shard_map/all_to_all | solution.py:1202
  368.9 29.7 %collective-permute-start.45 = (bf16[4,32,2560]{2,1,0:T(8,128)(2,1)}, bf16[4,32,2560]{2,1,0:T(8,128)(2,1)}, u32[]{:S(2)}, u32[]{:S(2)}) collective-permute-start(bf16[4,32,2560]{2,1,0:T(8,128)(2,1)} %get-tuple-element.359), channel_id=1, source_target_pairs={{0,1},{1,0},{2,3},{3,2},{4,5},{5,4},{6,7},{7,6},{8,9},{9,8},{10,11... | collective-permute-start | bytes 1966088 | tf_op jit(solution)/shard_map/ppermute | solution.py:789
  370.3 28.4 %collective-permute-start.46 = (bf16[1,128,2560]{2,1,0:T(8,128)(2,1)}, bf16[1,128,2560]{2,1,0:T(8,128)(2,1)}, u32[]{:S(2)}, u32[]{:S(2)}) collective-permute-start(bf16[1,128,2560]{2,1,0:T(8,128)(2,1)} %get-tuple-element.360), channel_id=1, source_target_pairs={{0,16},{16,0},{1,17},{17,1},{2,18},{18,2},{3,19},{19,3},{4,20},{20... | collective-permute-start | bytes 1966088 | tf_op jit(solution)/shard_map/ppermute | solution.py:789
  371.5 27.2 %collective-permute-start.44 = (bf16[1,64,2048]{2,1,0:T(8,128)(2,1)}, bf16[1,64,2048]{2,1,0:T(8,128)(2,1)S(1)}, u32[]{:S(2)}, u32[]{:S(2)}) collective-permute-start(bf16[1,64,2048]{2,1,0:T(8,128)(2,1)} %get-tuple-element.358), channel_id=1, source_target_pairs={{0,4},{2,6},{4,0},{6,2},{1,5},{3,7},{5,1},{7,3},{8,12},{10,14},{12... | collective-permute-start | bytes 786440 | tf_op jit(solution)/shard_map/ppermute | solution.py:789
  421.7 31.0 %collective-permute-start.50 = (bf16[256,1024]{1,0:T(8,128)(2,1)}, bf16[256,1024]{1,0:T(8,128)(2,1)}, u32[]{:S(2)}, u32[]{:S(2)}) collective-permute-start(bf16[256,1024]{1,0:T(8,128)(2,1)} %get-tuple-element.400), channel_id=1, source_target_pairs={{0,1},{1,0},{2,3},{3,2},{4,5},{5,4},{6,7},{7,6},{8,9},{9,8},{10,11... | collective-permute-start | bytes 1572872 | tf_op jit(solution)/shard_map/ppermute | solution.py:910
  426.2 65.0 %all-to-all-start.3 = ((bf16[32,32,384]{2,1,0:T(8,128)(2,1)}), bf16[32,32,384]{2,1,0:T(8,128)(2,1)}, u32[]{:S(2)}, u32[]{:S(2)}) async-start(bf16[32,32,384]{2,1,0:T(8,128)(2,1)} %bitcast.232), calls=%async_computation.3 | async-start | bytes 1572864 | tf_op jit(solution)/shard_map/all_to_all | solution.py:1252
  438.1 26.7 %collective-permute-start.51 = (bf16[1,32,5120]{2,1,0:T(8,128)(2,1)}, bf16[1,32,5120]{2,1,0:T(8,128)(2,1)S(1)}, u32[]{:S(2)}, u32[]{:S(2)}) collective-permute-start(bf16[1,32,5120]{2,1,0:T(8,128)(2,1)} %get-tuple-element.406), channel_id=1, source_target_pairs={{0,4},{2,6},{4,0},{6,2},{1,5},{3,7},{5,1},{7,3},{8,12},{10,14},{12... | collective-permute-start | bytes 983048 | tf_op jit(solution)/shard_map/ppermute | solution.py:789
  (131 other events, 1486.5 us)

commit v4 on v3

--- a/solution.py
+++ b/solution.py
@@ -1215,21 +1215,20 @@
     grad_pairs, down_came, low_came, high_came, heads_in = together(
         grad_pairs, down_came, low_came, high_came, heads_in
     )
-    grad_give, grad_keep = input_grad(
-        positions_of[jnp.array(block_order, jnp.int32)], grad_pairs, w_heads, rows
-    )
-    grad_give, grad_keep, down_came, low_came, high_came, grad_pairs = together(
-        grad_give, grad_keep, down_came, low_came, high_came, grad_pairs
-    )
-    give_came = by_offset(grad_give, core_bit)
     rest_pieces = [
         (x, came, at)
         for (kept, _), came in ((low_sends, low_came), (high_sends, high_came))
         for x, at in zip(kept, (0, units))
     ]
     (rest_sends,) = relay([(low_bit, (na // 2, 2, part), rest_pieces)], views)
-    give_came, rest_sends, grad_keep = together(give_came, rest_sends, grad_keep)
+    grad_pairs, rest_sends = together(grad_pairs, rest_sends)
     rest_came = send(rest_sends, "a")
+    grad_give, grad_keep = input_grad(
+        positions_of[jnp.array(block_order, jnp.int32)], grad_pairs, w_heads, rows
+    )
+    grad_give, grad_keep, grad_pairs = together(grad_give, grad_keep, grad_pairs)
+    give_came = by_offset(grad_give, core_bit)
+    give_came, grad_keep = together(give_came, grad_keep)
 
     grad_keep = join(grad_keep, give_came)
     sums = {
@@ -1244,10 +1243,7 @@
     if far_bits:
         final = [by_offset(x, far_bits[-1]) for x in sums[far_bits[-1]]]
     weight_pairs = [dot(normed, x, TN).astype(BF) for x in grad_pairs[1:]]
-    if far_bits:
-        final[0], rest_came, down_came, block_came = together(
-            final[0], rest_came, down_came, block_came
-        )
+    weight_pairs, rest_came = together(weight_pairs, rest_came)
     for x in weight_pairs:
         heads_in.append(lax.all_to_all(x.reshape(devices, part, 384), AXES, 0, 0, tiled=True))
     starts = (0, units, units + model // 2, 2 * units + model // 2)
@@ -1255,6 +1251,7 @@
     (rest_sends,) = relay([(next_bit, (na // 4, 2, part), rest_pieces)], views)
     rest_came = flip(rest_sends[1], "a", 2)
     if far_bits:
+        final[0], down_came, block_came = together(final[0], down_came, block_came)
         final[1], rest_came = together(final[1], rest_came)
     down_parts = added_of(down_sends[0], down_came, (na // 4, cut))
     down_part = jnp.concatenate([scatter_axis(x, "a", 0, 4) for x in down_parts])
@@ -1272,14 +1269,11 @@
         if r == 0 and far_bits:
             total, final[1] = together(total, final[1])
         totals.append(total)
-    small = small.reshape(8, 2, nh, 2, na, nb, part).transpose(4, 3, 5, 1, 2, 0, 6)
-    small = scatter_axis(small, "a", 0, kind=F32)
-    small, totals = together(small, totals)
-    grad_tokens = [restore(totals[0], 0)]
-    grad_tokens.append(restore(totals[1], 1))
+    grad_tokens = [restore(total, r) for r, total in enumerate(totals)]
     rest_parts = added_of(rest_sends[0], rest_came, (na // 4, part))
     low_up, low_out, high_up, high_out = (scatter_axis(x, "a", 0, 4) for x in rest_parts)
-    for axis in ("c", "b", "j", "h"):
+    small = small.reshape(8, 2, nh, 2, na, nb, part).transpose(3, 5, 1, 2, 4, 0, 6)
+    for axis in ("c", "b", "j", "h", "a"):
         small = scatter_axis(small, axis, 0, kind=F32)
     grad_tokens = ordered(*grad_tokens)
 

time: 517 us -> 503 us (0.973)
  waiting for transfers between devices: 153 us -> 143 us
    ppermute x40, waiting for transfers between devices: 84.1 us -> 104 us  [flip(): return lax.ppermute(x, axis, [(i, i ^ bit) for i in range(size)])]
    ppermute x4, waiting for transfers between devices: 17.7 us -> 2.51 us  [restore(): return lax.ppermute(x, AXES, [(there, here) for here, there in moves[turn]])]
    ppermute x12, waiting for transfers between devices: 27.7 us -> 13.1 us  [by_offset(): return lax.ppermute(x, AXES, sends)]
    unnamed x188 -> x175, local copies, waits for them, and re-layouts: 15.5 us -> 13.9 us
  transfers between devices with their start and end apart: 64 -> 64, of which waited for: 27 -> 24; matrix products, arithmetic and copies ran while one was open for 10% -> 10% of each run, Pallas kernels for 30% -> 29%
where the time goes in v4:
time: 503 us; the launch traced here: 496 us
  Pallas kernels  174 us (35%)
  waiting for transfers between devices  143 us (28%)
  starting transfers between devices  86.7 us (17%)
  local copies, waits for them, and re-layouts  37.6 us (7%)
  matrix products  27.3 us (5%)
  other arithmetic  24.6 us (5%)
    ppermute x40, waiting for transfers between devices, flip(): return lax.ppermute(x, axis, [(i, i ^ bit) for i in range(size)])  104 us
    pallas_call x2, Pallas kernels, attention_backward(): pl.pallas_call(functools.partial(backward_kernel, bk=bk, rows=rows), out_...  48.5 us
    pallas_call x3, Pallas kernels, mlp_call(): pl.pallas_call(functools.partial(kernel, tables=len(tables)), out_shape=[...  42.4 us
    ppermute x40, starting transfers between devices, flip(): return lax.ppermute(x, axis, [(i, i ^ bit) for i in range(size)])  34.3 us
    dot_general x8, matrix products, dot(): return lax.dot_general(left, right, dims, preferred_element_type=F32)  27.3 us
    all_to_all x1, waiting for transfers between devices, body(): vectors = lax.all_to_all(vectors, AXES, 0, 0, tiled=True)  20.3 us
    pallas_call x1, Pallas kernels, attention_forward(): pl.pallas_call(functools.partial(forward_kernel, bq=bq, bk=bk, rows=rows)...  19.5 us
    pallas_call x5, Pallas kernels, relay(): pl.pallas_call(functools.partial(relay_kernel, layout=tuple(layout), arri...  18.5 us
  transfers between devices with their start and end apart: 64, of which 24 were waited for; matrix products, arithmetic and copies ran while one was open for 10% of the time, Pallas kernels for 29%

profile of v4, /device:TPU:1, one launch (start us, length us, event | category | flops | bytes accessed | tf_op | source)
XLA Modules:
  0.0 495.9 jit_solution(16531185129196024092)
XLA Ops:
  3.9 5.7 %collective-permute-start = (bf16[256,1024]{1,0:T(8,128)(2,1)}, bf16[256,1024]{1,0:T(8,128)(2,1)S(1)}, u32[]{:S(2)}, u32[]{:S(2)}) collective-permute-start(bf16[256,1024]{1,0:T(8,128)(2,1)} %get-tuple-element.459), channel_id=1, source_target_pairs={{0,0},{1,1},{2,8},{3,9},{4,2},{5,3},{6,10},{7,11},{8,4},{9,5},{10,... | collective-permute-start | bytes 1572872 | tf_op jit(solution)/shard_map/ppermute | solution.py:896
  28.3 5.6 %fusion.11 = (f32[2048,128]{1,0:T(8,128)}, f32[2048,128]{1,0:T(8,128)}) fusion(f32[128]{0:T(128)S(1)} %get-tuple-element.494, f32[128]{0:T(128)S(1)} %get-tuple-element.495, f32[2048]{0:T(1024)S(1)} %iota_convert_fusion), kind=kLoop, calls=%fused_computation.30 | loop fusion | flops 524288 | bytes 2106368 | tf_op jit(solution)/shard_map/mul | solution.py:959
  36.2 20.3 %all-to-all-done.1 = bf16[32,2,128]{2,1,0:T(2,128)(2,1)S(1)} async-done(((bf16[32,2,128]{2,1,0:T(2,128)(2,1)}), bf16[32,2,128]{2,1,0:T(2,128)(2,1)S(1)}, u32[]{:S(2)}, u32[]{:S(2)}) %all-to-all-start.1) | async-done | bytes 16416 | tf_op jit(solution)/shard_map/all_to_all | solution.py:969
  59.6 13.5 %collective-permute-done.7 = bf16[2,160,1024]{2,1,0:T(8,128)(2,1)S(1)} collective-permute-done((bf16[2,160,1024]{2,1,0:T(8,128)(2,1)S(1)}, bf16[2,160,1024]{2,1,0:T(8,128)(2,1)S(1)}, u32[]{:S(2)}, u32[]{:S(2)}) %collective-permute-start.7) | collective-permute-done | bytes 655392 | tf_op jit(solution)/shard_map/ppermute | solution.py:789
  76.4 9.9 %collective-permute-done.9 = bf16[1,128,1024]{2,1,0:T(8,128)(2,1)S(1)} collective-permute-done((bf16[1,128,1024]{2,1,0:T(8,128)(2,1)S(1)}, bf16[1,128,1024]{2,1,0:T(8,128)(2,1)S(1)}, u32[]{:S(2)}, u32[]{:S(2)}) %collective-permute-start.9) | collective-permute-done | bytes 262176 | tf_op jit(solution)/shard_map/ppermute | solution.py:789
  94.6 13.8 %collective-permute-done.13 = bf16[4,80,1024]{2,1,0:T(8,128)(2,1)S(1)} collective-permute-done((bf16[4,80,1024]{2,1,0:T(8,128)(2,1)S(1)}, bf16[4,80,1024]{2,1,0:T(8,128)(2,1)S(1)}, u32[]{:S(2)}, u32[]{:S(2)}) %collective-permute-start.13) | collective-permute-done | bytes 655392 | tf_op jit(solution)/shard_map/ppermute | solution.py:789
  120.9 13.9 %qkv.1 = (bf16[2048,1024]{1,0:T(8,128)(2,1)}, bf16[2048,256]{1,0:T(8,128)(2,1)}, bf16[2048,256]{1,0:T(8,128)(2,1)}, bf16[2048,256]{1,0:T(8,128)(2,1)}, bf16[1024,768]{1,0:T(8,128)(2,1)}) custom-call(s32[8]{0:T(128)} %get-tuple-element.496.table, s32[8]{0:T(128)} %xor_add_fusion.2.order, bf16[2,256,1024]{2,1,0:T(8,128)(2,1)} %copy-done.35, ...), custom_call_target="tpu_custom_call" | custom-call | flops 11000000 | bytes 1024 | tf_op jit(solution)/shard_map/qkv/pallas_call | solution.py:86
  134.9 19.5 %attention_forward.1 = (bf16[8,256,256]{2,1,0:T(8,128)(2,1)}, f32[2048,256]{1,0:T(8,128)}) custom-call(s32[8]{0:T(128)} %get-tuple-element.497.table, bf16[2048,256]{1,0:T(8,128)(2,1)} %get-tuple-element.248.q_ref, bf16[2048,256]{1,0:T(8,128)(2,1)} %get-tuple-element.249.k_ref, bf16[2048,256]{1,0:T(8,128)(2,1)} %get-tuple-element.250.v_ref), custom_call_target="tpu_custom_call" | custom-call | flops 23000000 | bytes 1024 | tf_op jit(solution)/shard_map/attention_forward/pallas_call | solution.py:167
  165.6 6.5 %collective-permute-done.20.refs_3_ = bf16[512,256]{1,0:T(8,128)(2,1)S(1)} collective-permute-done((bf16[512,256]{1,0:T(8,128)(2,1)S(1)}, bf16[512,256]{1,0:T(8,128)(2,1)S(1)}, u32[]{:S(2)}, u32[]{:S(2)}) %collective-permute-start.20) | collective-permute-done | bytes 262176 | tf_op jit(solution)/shard_map/ppermute | solution.py:910
  181.0 11.7 %collective-permute-done.23.refs_3_.refs_9_ = bf16[4,128,1024]{2,1,0:T(8,128)(2,1)S(1)} collective-permute-done((bf16[4,128,1024]{2,1,0:T(8,128)(2,1)}, bf16[4,128,1024]{2,1,0:T(8,128)(2,1)S(1)}, u32[]{:S(2)}, u32[]{:S(2)}) %collective-permute-start.23) | collective-permute-done | bytes 1048608 | tf_op jit(solution)/shard_map/ppermute | solution.py:789
  195.7 12.9 %mlp_up.1 = (bf16[1024,2048]{1,0:T(8,128)(2,1)}, bf16[1024,2048]{1,0:T(8,128)(2,1)}) custom-call(s32[3,16]{1,0:T(4,128)} %copy-done.27, bf16[512,1024]{1,0:T(8,128)(2,1)} %copy-done.25, bf16[512,1024]{1,0:T(8,128)(2,1)} %collective-permute-done.22.refs_2_, bf16[8,80,1024]{2,1,0:T(8,128)(2,1)} %pad_maximum_fusion.2.refs_0_.refs_3_.refs_4_, ...), custom_call_target="tpu_custom_call" | custom-call | flops 11000000 | bytes 1024 | tf_op jit(solution)/shard_map/mlp_up/pallas_call | solution.py:451
  209.6 10.4 %mlp_down.1 = (f32[512,1024]{1,0:T(8,128)}, bf16[512,1024]{1,0:T(8,128)(2,1)}) custom-call(s32[3,16]{1,0:T(4,128)} %copy-done.27, bf16[1024,2048]{1,0:T(8,128)(2,1)} %get-tuple-element.268.refs_1_, bf16[4,128,1024]{2,1,0:T(8,128)(2,1)} %pad_maximum_fusion.7.refs_2_.refs_8_, bf16[4,128,1024]{2,1,0:T(8,128)(2,1)} %copy-done.33, ...), custom_call_target="tpu_custom_call" | custom-call | flops 9000000 | bytes 1024 | tf_op jit(solution)/shard_map/mlp_down/pallas_call | solution.py:451
  232.3 7.4 %convolution_convert_fusion.1 = bf16[2048,1024]{1,0:T(8,128)(2,1)S(1)} fusion(bf16[1024,2048]{1,0:T(8,128)(2,1)} %get-tuple-element.268.refs_1_, bf16[512,1024]{1,0:T(8,128)(2,1)S(1)} %collective-permute-done.29.refs_2_, bf16[512,1024]{1,0:T(8,128)(2,1)} %get-tuple-element.281.refs_1_), kind=kOutput, calls=%fused_computation.3 | convolution fusion | flops 4301258752 | bytes 10485760 | tf_op jit(solution)/shard_map/dot_general | solution.py:30
  250.2 19.2 %mlp_backward.1 = (bf16[1024,2048]{1,0:T(8,128)(2,1)}, f32[512,1024]{1,0:T(8,128)}, bf16[512,1024]{1,0:T(8,128)(2,1)}) custom-call(s32[3,16]{1,0:T(4,128)} %copy-done.27, bf16[512,1024]{1,0:T(8,128)(2,1)} %get-tuple-element.281.refs_1_, bf16[512,1024]{1,0:T(8,128)(2,1)} %copy-done.44, bf16[1024,2048]{1,0:T(8,128)(2,1)} %get-tuple-element.283.refs_3_, ...), custom_call_target="tpu_custom_call" | custom-call | flops 20000000 | bytes 1024 | tf_op jit(solution)/shard_map/mlp_backward/pallas_call | solution.py:451
  279.4 9.0 %turn.1 = (f32[512,1024]{1,0:T(8,128)}, bf16[512,1024]{1,0:T(8,128)(2,1)}, bf16[512,256]{1,0:T(8,128)(2,1)}, bf16[512,256]{1,0:T(8,128)(2,1)}, bf16[512,256]{1,0...) custom-call(f32[512,1024]{1,0:T(8,128)} %get-tuple-element.300.own_ref, bf16[512,1024]{1,0:T(8,128)(2,1)} %copy-done.45, ...), custom_call_target="tpu_custom_call" | custom-call | flops 6000000 | bytes 1024 | tf_op jit(solution)/shard_map/turn/pallas_call | solution.py:702
  303.9 7.1 %convolution_convert_fusion = bf16[1024,2048]{1,0:T(8,128)(2,1)S(1)} fusion(bf16[1024,2048]{1,0:T(8,128)(2,1)} %get-tuple-element.327, bf16[512,1024]{1,0:T(8,128)(2,1)} %collective-permute-done.22.refs_2_, bf16[512,1024]{1,0:T(8,128)(2,1)S(1)} %copy-done.26), kind=kOutput, calls=%fused_computation.2 | convolution fusion | flops 4301258752 | bytes 10485760 | tf_op jit(solution)/shard_map/dot_general | solution.py:30
  321.7 24.3 %attention_backward.2.refs_0_ = bf16[2048,384]{1,0:T(8,128)(2,1)} custom-call(s32[8]{0:T(128)} %get-tuple-element.497.table, bf16[2048,256]{1,0:T(8,128)(2,1)} %get-tuple-element.248.q_ref, bf16[2048,256]{1,0:T(8,128)(2,1)} %get-tuple-element.249.k_ref, bf16[2048,256]{1,0:T(8,128)(2,1)} %get-tuple-element.250.v_ref, ...), custom_call_target="tpu_custom_call" | custom-call | flops 44000000 | bytes 1024 | tf_op jit(solution)/shard_map/attention_backward/pallas_call | solution.py:302
  350.7 6.5 %convolution_convert_fusion.3 = bf16[1024,384]{1,0:T(8,128)(2,1)} fusion(bf16[2048,1024]{1,0:T(8,128)(2,1)} %get-tuple-element.353, bf16[2048,384]{1,0:T(8,128)(2,1)} %attention_backward.2.refs_0_), kind=kOutput, calls=%fused_computation.17 | convolution fusion | flops 1611005952 | bytes 6553600 | tf_op jit(solution)/shard_map/dot_general | solution.py:30
  357.2 5.4 %all-to-all-start.2 = ((bf16[32,32,384]{2,1,0:T(8,128)(2,1)}), bf16[32,32,384]{2,1,0:T(8,128)(2,1)S(1)}, u32[]{:S(2)}, u32[]{:S(2)}) async-start(bf16[32,32,384]{2,1,0:T(8,128)(2,1)} %bitcast.76), calls=%async_computation.2 | async-start | bytes 1572864 | tf_op jit(solution)/shard_map/all_to_all | solution.py:1202
  363.3 5.7 %relay.7 = (bf16[4,32,2048]{2,1,0:T(8,128)(2,1)}, bf16[4,32,512]{2,1,0:T(8,128)(2,1)}, bf16[1,128,2048]{2,1,0:T(8,128)(2,1)}, bf16[1,128,512]{2,1,0:T(8,128)(2,1...) custom-call(s32[3]{0:T(128)} %pad_add_fusion.2.here, ...), custom_call_target="tpu_custom_call" | custom-call | flops 4000000 | bytes 1024 | tf_op jit(solution)/shard_map/relay/pallas_call | solution.py:530
  374.3 24.2 %attention_backward.3.refs_1_ = bf16[2048,384]{1,0:T(8,128)(2,1)} custom-call(s32[8]{0:T(128)} %get-tuple-element.497.table, bf16[2048,256]{1,0:T(8,128)(2,1)} %get-tuple-element.248.q_ref, bf16[2048,256]{1,0:T(8,128)(2,1)} %get-tuple-element.249.k_ref, bf16[2048,256]{1,0:T(8,128)(2,1)} %get-tuple-element.250.v_ref, ...), custom_call_target="tpu_custom_call" | custom-call | flops 44000000 | bytes 1024 | tf_op jit(solution)/shard_map/attention_backward/pallas_call | solution.py:302
  404.8 6.9 %input_grad.1 = (bf16[4,256,1024]{2,1,0:T(8,128)(2,1)S(1)}, bf16[4,256,1024]{2,1,0:T(8,128)(2,1)S(1)}) custom-call(s32[8]{0:T(128)S(1)} %gather_fusion, bf16[2048,384]{1,0:T(8,128)(2,1)S(1)} %copy-done.4, bf16[2048,384]{1,0:T(8,128)(2,1)S(1)} %copy-done.5, bf16[1024,768]{1,0:T(8,128)(2,1)S(1)} %copy-done.22), custom_call_target="tpu_custom_call" | custom-call | flops 6000000 | bytes 1024 | tf_op jit(solution)/shard_map/input_grad/pallas_call | solution.py:742
  423.9 5.5 %collective-permute-done.50 = bf16[2,32,5120]{2,1,0:T(8,128)(2,1)} collective-permute-done((bf16[2,32,5120]{2,1,0:T(8,128)(2,1)S(1)}, bf16[2,32,5120]{2,1,0:T(8,128)(2,1)}, u32[]{:S(2)}, u32[]{:S(2)}) %collective-permute-start.50) | collective-permute-done | bytes 655392 | tf_op jit(solution)/shard_map/ppermute | solution.py:789
  436.9 19.9 %collective-permute-done.51 = bf16[1,32,5120]{2,1,0:T(8,128)(2,1)S(1)} collective-permute-done((bf16[1,32,5120]{2,1,0:T(8,128)(2,1)}, bf16[1,32,5120]{2,1,0:T(8,128)(2,1)S(1)}, u32[]{:S(2)}, u32[]{:S(2)}) %collective-permute-start.51) | collective-permute-done | bytes 327712 | tf_op jit(solution)/shard_map/ppermute | solution.py:789
  (411 shorter events, 208.7 us)
Async XLA Ops:
  3.9 53.5 %collective-permute-start = (bf16[256,1024]{1,0:T(8,128)(2,1)}, bf16[256,1024]{1,0:T(8,128)(2,1)S(1)}, u32[]{:S(2)}, u32[]{:S(2)}) collective-permute-start(bf16[256,1024]{1,0:T(8,128)(2,1)} %get-tuple-element.459), channel_id=1, source_target_pairs={{0,0},{1,1},{2,8},{3,9},{4,2},{5,3},{6,10},{7,11},{8,4},{9,5},{10,... | collective-permute-start | bytes 1572872 | tf_op jit(solution)/shard_map/ppermute | solution.py:896
  9.6 47.8 %collective-permute-start.1 = (bf16[256,1024]{1,0:T(8,128)(2,1)}, bf16[256,1024]{1,0:T(8,128)(2,1)S(1)}, u32[]{:S(2)}, u32[]{:S(2)}) collective-permute-start(bf16[256,1024]{1,0:T(8,128)(2,1)} %get-tuple-element.458), channel_id=1, source_target_pairs={{0,2},{1,3},{2,10},{3,11},{4,0},{5,1},{6,8},{7,9},{8,6},{9,7},{10,... | collective-permute-start | bytes 1572872 | tf_op jit(solution)/shard_map/ppermute | solution.py:896
  19.9 37.4 %collective-permute-start.3 = (bf16[1,160,1024]{2,1,0:T(8,128)(2,1)S(1)}, bf16[1,160,1024]{2,1,0:T(8,128)(2,1)S(1)}, u32[]{:S(2)}, u32[]{:S(2)}) collective-permute-start(bf16[1,160,1024]{2,1,0:T(8,128)(2,1)S(1)} %maximum_bitcast_fusion), channel_id=1, source_target_pairs={{0,4},{2,6},{4,0},{6,2},{1,5},{3,7},{5,1},{7,3},{8,12},{10,14},{12... | collective-permute-start | bytes 983048 | tf_op jit(solution)/shard_map/ppermute | solution.py:789
  23.9 32.5 %all-to-all-start.1 = ((bf16[32,2,128]{2,1,0:T(2,128)(2,1)}), bf16[32,2,128]{2,1,0:T(2,128)(2,1)S(1)}, u32[]{:S(2)}, u32[]{:S(2)}) async-start(bf16[32,2,128]{2,1,0:T(2,128)(2,1)} %reshape.310), calls=%async_computation.1 | async-start | bytes 32768 | tf_op jit(solution)/shard_map/all_to_all | solution.py:969
  58.0 30.5 %collective-permute-start.5 = (bf16[2,256,1024]{2,1,0:T(8,128)(2,1)S(1)}, bf16[2,256,1024]{2,1,0:T(8,128)(2,1)S(1)}, u32[]{:S(2)}, u32[]{:S(2)}) collective-permute-start(bf16[2,256,1024]{2,1,0:T(8,128)(2,1)S(1)} %pad_maximum_fusion.6.refs_0_), channel_id=1, source_target_pairs={{0,1},{1,0},{2,3},{3,2},{4,5},{5,4},{6,7},{7,6},{8,9},{9,8},{10,11... | collective-permute-start | bytes 3145736 | tf_op jit(solution)/shard_map/ppermute | solution.py:910
  58.3 30.2 %collective-permute-start.6 = (bf16[2,256,1024]{2,1,0:T(8,128)(2,1)S(1)}, bf16[2,256,1024]{2,1,0:T(8,128)(2,1)S(1)}, u32[]{:S(2)}, u32[]{:S(2)}) collective-permute-start(bf16[2,256,1024]{2,1,0:T(8,128)(2,1)S(1)} %pad_maximum_fusion.6.refs_0_), channel_id=1, source_target_pairs={{0,8},{1,9},{2,10},{3,11},{4,12},{5,13},{6,14},{7,15},{8,0},{9,1},... | collective-permute-start | bytes 3145736 | tf_op jit(solution)/shard_map/ppermute | solution.py:910
  112.5 41.9 %collective-permute-start.15 = (bf16[8,80,1024]{2,1,0:T(8,128)(2,1)}, bf16[8,80,1024]{2,1,0:T(8,128)(2,1)}, u32[]{:S(2)}, u32[]{:S(2)}) collective-permute-start(bf16[8,80,1024]{2,1,0:T(8,128)(2,1)} %pad_maximum_fusion.2.refs_0_.refs_3_.refs_4_), channel_id=1, source_target_pairs={{0,16},{16,0},{1,17},{17,1},{2,18},{18,2},{3,19},{19,3},{4,20},{20... | collective-permute-start | bytes 3932168 | tf_op jit(solution)/shard_map/ppermute | solution.py:789
  113.9 40.5 %collective-permute-start.16 = (bf16[8,80,1024]{2,1,0:T(8,128)(2,1)S(1)}, bf16[8,80,1024]{2,1,0:T(8,128)(2,1)}, u32[]{:S(2)}, u32[]{:S(2)}) collective-permute-start(bf16[8,80,1024]{2,1,0:T(8,128)(2,1)S(1)} %pad_maximum_fusion.3.refs_2_.refs_5_.refs_6_), channel_id=1, source_target_pairs={{0,1},{1,0},{2,3},{3,2},{4,5},{5,4},{6,7},{7,6},{8,9},{9,8},{10,11... | collective-permute-start | bytes 3932168 | tf_op jit(solution)/shard_map/ppermute | solution.py:789
  114.8 39.6 %collective-permute-start.17 = (bf16[256,1024]{1,0:T(8,128)(2,1)}, bf16[256,1024]{1,0:T(8,128)(2,1)S(1)}, u32[]{:S(2)}, u32[]{:S(2)}) collective-permute-start(bf16[256,1024]{1,0:T(8,128)(2,1)} %dynamic-slice_bitcast_fusion.6), channel_id=1, source_target_pairs={{0,0},{1,1},{2,8},{3,9},{4,2},{5,3},{6,10},{7,11},{8,4},{9,5},{10,... | collective-permute-start | bytes 1572872 | tf_op jit(solution)/shard_map/ppermute | solution.py:896
  159.5 33.3 %collective-permute-start.23 = (bf16[4,128,1024]{2,1,0:T(8,128)(2,1)}, bf16[4,128,1024]{2,1,0:T(8,128)(2,1)S(1)}, u32[]{:S(2)}, u32[]{:S(2)}) collective-permute-start(bf16[4,128,1024]{2,1,0:T(8,128)(2,1)} %pad_maximum_fusion.7.refs_2_.refs_8_), channel_id=1, source_target_pairs={{0,1},{1,0},{2,3},{3,2},{4,5},{5,4},{6,7},{7,6},{8,9},{9,8},{10,11... | collective-permute-start | bytes 3145736 | tf_op jit(solution)/shard_map/ppermute | solution.py:789
  164.6 28.1 %collective-permute-start.24 = (bf16[4,128,1024]{2,1,0:T(8,128)(2,1)}, bf16[4,128,1024]{2,1,0:T(8,128)(2,1)S(1)}, u32[]{:S(2)}, u32[]{:S(2)}) collective-permute-start(bf16[4,128,1024]{2,1,0:T(8,128)(2,1)} %pad_maximum_fusion.7.refs_2_.refs_8_), channel_id=1, source_target_pairs={{0,16},{16,0},{1,17},{17,1},{2,18},{18,2},{3,19},{19,3},{4,20},{20... | collective-permute-start | bytes 3145736 | tf_op jit(solution)/shard_map/ppermute | solution.py:789
  179.6 28.9 %collective-permute-start.25 = (bf16[256,1024]{1,0:T(8,128)(2,1)}, bf16[256,1024]{1,0:T(8,128)(2,1)S(1)}, u32[]{:S(2)}, u32[]{:S(2)}) collective-permute-start(bf16[256,1024]{1,0:T(8,128)(2,1)} %dynamic-slice_bitcast_fusion.5), channel_id=1, source_target_pairs={{0,2},{1,3},{2,10},{3,11},{4,0},{5,1},{6,8},{7,9},{8,6},{9,7},{10,... | collective-permute-start | bytes 1572872 | tf_op jit(solution)/shard_map/ppermute | solution.py:896
  242.8 29.1 %collective-permute-start.30 = (bf16[2,1,4,1,64,1024]{5,4,3,2,1,0:T(8,128)(2,1)S(1)}, bf16[2,1,4,1,64,1024]{5,4,3,2,1,0:T(8,128)(2,1)S(1)}, u32[]{:S(2)}, u32[]{:S(2)}) collective-permute-start(bf16[2,1,4,1,64,1024]{5,4,3,2,1,0:T(8,128)(2,1)S(1)} %get-tuple-element.287), channel_id=1, source_target_pairs={{0,1},{1,0},{2,3},{3,2},{4,5},{5,4},{6,7},{7,6},{8,9},{9,8},{10,11... | collective-permute-start | bytes 3145736 | tf_op jit(solution)/shard_map/ppermute | solution.py:789
  243.5 28.4 %collective-permute-start.31 = (bf16[1,1,4,2,64,1024]{5,4,3,2,1,0:T(8,128)(2,1)S(1)}, bf16[1,1,4,2,64,1024]{5,4,3,2,1,0:T(8,128)(2,1)S(1)}, u32[]{:S(2)}, u32[]{:S(2)}) collective-permute-start(bf16[1,1,4,2,64,1024]{5,4,3,2,1,0:T(8,128)(2,1)S(1)} %get-tuple-element.288), channel_id=1, source_target_pairs={{0,16},{16,0},{1,17},{17,1},{2,18},{18,2},{3,19},{19,3},{4,20},{20... | collective-permute-start | bytes 3145736 | tf_op jit(solution)/shard_map/ppermute | solution.py:789
  244.3 27.6 %collective-permute-start.32 = (bf16[256,1024]{1,0:T(8,128)(2,1)S(1)}, bf16[256,1024]{1,0:T(8,128)(2,1)S(1)}, u32[]{:S(2)}, u32[]{:S(2)}) collective-permute-start(bf16[256,1024]{1,0:T(8,128)(2,1)S(1)} %get-tuple-element.453), channel_id=1, source_target_pairs={{0,0},{1,1},{8,2},{9,3},{2,4},{3,5},{10,6},{11,7},{4,8},{5,9},{12,... | collective-permute-start | bytes 1572872 | tf_op jit(solution)/shard_map/ppermute | solution.py:899
  319.9 30.5 %collective-permute-start.42 = (bf16[1,1,4,2,32,2560]{5,4,3,2,1,0:T(8,128)(2,1)S(1)}, bf16[1,1,4,2,32,2560]{5,4,3,2,1,0:T(8,128)(2,1)S(1)}, u32[]{:S(2)}, u32[]{:S(2)}) collective-permute-start(bf16[1,1,4,2,32,2560]{5,4,3,2,1,0:T(8,128)(2,1)S(1)} %pad_maximum_fusion.4), channel_id=1, source_target_pairs={{0,16},{16,0},{1,17},{17,1},{2,18},{18,2},{3,19},{19,3},{4,20},{20... | collective-permute-start | bytes 3932168 | tf_op jit(solution)/shard_map/ppermute | solution.py:789
  320.6 30.1 %collective-permute-start.43 = (bf16[2,1,4,1,32,2560]{5,4,2,0,3,1:T(8,128)(2,1)S(1)}, bf16[2,1,4,1,32,2560]{5,4,2,0,3,1:T(8,128)(2,1)S(1)}, u32[]{:S(2)}, u32[]{:S(2)}) collective-permute-start(bf16[2,1,4,1,32,2560]{5,4,2,0,3,1:T(8,128)(2,1)S(1)} %pad_maximum_fusion.5), channel_id=1, source_target_pairs={{0,1},{1,0},{2,3},{3,2},{4,5},{5,4},{6,7},{7,6},{8,9},{9,8},{10,11... | collective-permute-start | bytes 3932168 | tf_op jit(solution)/shard_map/ppermute | solution.py:789
  357.2 41.4 %all-to-all-start.2 = ((bf16[32,32,384]{2,1,0:T(8,128)(2,1)}), bf16[32,32,384]{2,1,0:T(8,128)(2,1)S(1)}, u32[]{:S(2)}, u32[]{:S(2)}) async-start(bf16[32,32,384]{2,1,0:T(8,128)(2,1)} %bitcast.76), calls=%async_computation.2 | async-start | bytes 1572864 | tf_op jit(solution)/shard_map/all_to_all | solution.py:1202
  369.0 29.6 %collective-permute-start.45 = (bf16[4,32,2560]{2,1,0:T(8,128)(2,1)}, bf16[4,32,2560]{2,1,0:T(8,128)(2,1)}, u32[]{:S(2)}, u32[]{:S(2)}) collective-permute-start(bf16[4,32,2560]{2,1,0:T(8,128)(2,1)} %get-tuple-element.356), channel_id=1, source_target_pairs={{0,1},{1,0},{2,3},{3,2},{4,5},{5,4},{6,7},{7,6},{8,9},{9,8},{10,11... | collective-permute-start | bytes 1966088 | tf_op jit(solution)/shard_map/ppermute | solution.py:789
  370.4 28.2 %collective-permute-start.46 = (bf16[1,128,2560]{2,1,0:T(8,128)(2,1)}, bf16[1,128,2560]{2,1,0:T(8,128)(2,1)}, u32[]{:S(2)}, u32[]{:S(2)}) collective-permute-start(bf16[1,128,2560]{2,1,0:T(8,128)(2,1)} %get-tuple-element.357), channel_id=1, source_target_pairs={{0,16},{16,0},{1,17},{17,1},{2,18},{18,2},{3,19},{19,3},{4,20},{20... | collective-permute-start | bytes 1966088 | tf_op jit(solution)/shard_map/ppermute | solution.py:789
  371.6 27.0 %collective-permute-start.44 = (bf16[1,64,2048]{2,1,0:T(8,128)(2,1)}, bf16[1,64,2048]{2,1,0:T(8,128)(2,1)S(1)}, u32[]{:S(2)}, u32[]{:S(2)}) collective-permute-start(bf16[1,64,2048]{2,1,0:T(8,128)(2,1)} %get-tuple-element.355), channel_id=1, source_target_pairs={{0,4},{2,6},{4,0},{6,2},{1,5},{3,7},{5,1},{7,3},{8,12},{10,14},{12... | collective-permute-start | bytes 786440 | tf_op jit(solution)/shard_map/ppermute | solution.py:789
  419.1 37.6 %collective-permute-start.49 = (bf16[256,1024]{1,0:T(8,128)(2,1)}, bf16[256,1024]{1,0:T(8,128)(2,1)}, u32[]{:S(2)}, u32[]{:S(2)}) collective-permute-start(bf16[256,1024]{1,0:T(8,128)(2,1)} %get-tuple-element.392), channel_id=1, source_target_pairs={{0,1},{1,0},{2,3},{3,2},{4,5},{5,4},{6,7},{7,6},{8,9},{9,8},{10,11... | collective-permute-start | bytes 1572872 | tf_op jit(solution)/shard_map/ppermute | solution.py:910
  419.4 37.4 %collective-permute-start.48 = (bf16[256,1024]{1,0:T(8,128)(2,1)}, bf16[256,1024]{1,0:T(8,128)(2,1)}, u32[]{:S(2)}, u32[]{:S(2)}) collective-permute-start(bf16[256,1024]{1,0:T(8,128)(2,1)} %get-tuple-element.381), channel_id=1, source_target_pairs={{0,1},{1,0},{2,3},{3,2},{4,5},{5,4},{6,7},{7,6},{8,9},{9,8},{10,11... | collective-permute-start | bytes 1572872 | tf_op jit(solution)/shard_map/ppermute | solution.py:910
  431.8 61.7 %all-to-all-start.3 = ((bf16[32,32,384]{2,1,0:T(8,128)(2,1)}), bf16[32,32,384]{2,1,0:T(8,128)(2,1)}, u32[]{:S(2)}, u32[]{:S(2)}) async-start(bf16[32,32,384]{2,1,0:T(8,128)(2,1)} %bitcast.233), calls=%async_computation.3 | async-start | bytes 1572864 | tf_op jit(solution)/shard_map/all_to_all | solution.py:1248
  (124 other events, 1496.7 us)

commit v5 on v4

--- a/solution.py
+++ b/solution.py
@@ -320,7 +320,7 @@
             ],
         ),
         compiler_params=pltpu.CompilerParams(
-            dimension_semantics=("arbitrary",), vmem_limit_bytes=56 << 20
+            dimension_semantics=("arbitrary",), vmem_limit_bytes=28 << 20
         ),
         cost_estimate=cost(44),
         name="attention_backward",
@@ -1183,10 +1183,10 @@
     low_came, high_came = send(low_sends, "j"), send(high_sends, "b")
     down_came = send(down_sends, "a")
     grad_pairs = [backward(0, grad_heads)]
-    grad_pairs, down_came, low_came, high_came = together(
-        grad_pairs, down_came, low_came, high_came
-    )
     weight_pairs = [dot(normed, grad_pairs[0], TN).astype(BF)]
+    weight_pairs, down_came, low_came, high_came = together(
+        weight_pairs, down_came, low_came, high_came
+    )
     low_pieces = [(low_sends[0][0], low_came, 0), (low_sends[0][1], low_came, units)]
     high_pieces = [(high_sends[0][0], high_came, 0), (high_sends[0][1], high_came, units)]
     down_pieces = [(down_sends[0][0], down_came, 0), (down_sends[0][1], down_came, model)]

time: 503 us -> 501 us (level)
  local copies, waits for them, and re-layouts: 37.6 us -> 46.7 us
  Pallas kernels: 174 us -> 167 us
    unnamed x175 -> x205, local copies, waits for them, and re-layouts: 13.9 us -> 23.6 us
    pallas_call x2, Pallas kernels: 48.5 us -> 41.5 us  [attention_backward(): pl.pallas_call(functools.partial(backward_kernel, bk=bk, rows=rows), out_...]
  transfers between devices with their start and end apart: 64 -> 64, of which waited for: 24 -> 24; matrix products, arithmetic and copies ran while one was open for 10% -> 10% of each run, Pallas kernels for 29% -> 28%
where the time goes in v5:
time: 501 us; the launch traced here: 493 us
  Pallas kernels  167 us (33%)
  waiting for transfers between devices  143 us (29%)
  starting transfers between devices  86.6 us (17%)
  local copies, waits for them, and re-layouts  46.7 us (9%)
  matrix products  24.1 us (5%)
  other arithmetic  23.7 us (5%)
    ppermute x40, waiting for transfers between devices, flip(): return lax.ppermute(x, axis, [(i, i ^ bit) for i in range(size)])  104 us
    pallas_call x3, Pallas kernels, mlp_call(): pl.pallas_call(functools.partial(kernel, tables=len(tables)), out_shape=[...  42.4 us
    pallas_call x2, Pallas kernels, attention_backward(): pl.pallas_call(functools.partial(backward_kernel, bk=bk, rows=rows), out_...  41.5 us
    ppermute x40, starting transfers between devices, flip(): return lax.ppermute(x, axis, [(i, i ^ bit) for i in range(size)])  34.4 us
    dot_general x8, matrix products, dot(): return lax.dot_general(left, right, dims, preferred_element_type=F32)  24.1 us
    unnamed x205, local copies, waits for them, and re-layouts  23.6 us
    all_to_all x1, waiting for transfers between devices, body(): vectors = lax.all_to_all(vectors, AXES, 0, 0, tiled=True)  20.3 us
    pallas_call x1, Pallas kernels, attention_forward(): pl.pallas_call(functools.partial(forward_kernel, bq=bq, bk=bk, rows=rows)...  19.5 us
  transfers between devices with their start and end apart: 64, of which 24 were waited for; matrix products, arithmetic and copies ran while one was open for 10% of the time, Pallas kernels for 28%

profile of v5, /device:TPU:1, one launch (start us, length us, event | category | flops | bytes accessed | tf_op | source)
XLA Modules:
  0.0 493.4 jit_solution(13076366486115326873)
XLA Ops:
  3.9 5.7 %collective-permute-start = (bf16[256,1024]{1,0:T(8,128)(2,1)}, bf16[256,1024]{1,0:T(8,128)(2,1)S(1)}, u32[]{:S(2)}, u32[]{:S(2)}) collective-permute-start(bf16[256,1024]{1,0:T(8,128)(2,1)} %get-tuple-element.459), channel_id=1, source_target_pairs={{0,0},{1,1},{2,8},{3,9},{4,2},{5,3},{6,10},{7,11},{8,4},{9,5},{10,... | collective-permute-start | bytes 1572872 | tf_op jit(solution)/shard_map/ppermute | solution.py:896
  28.3 5.6 %fusion.11 = (f32[2048,128]{1,0:T(8,128)}, f32[2048,128]{1,0:T(8,128)}) fusion(f32[128]{0:T(128)S(1)} %get-tuple-element.494, f32[128]{0:T(128)S(1)} %get-tuple-element.495, f32[2048]{0:T(1024)S(1)} %iota_convert_fusion), kind=kLoop, calls=%fused_computation.30 | loop fusion | flops 524288 | bytes 2106368 | tf_op jit(solution)/shard_map/mul | solution.py:959
  36.2 20.3 %all-to-all-done.1 = bf16[32,2,128]{2,1,0:T(2,128)(2,1)S(1)} async-done(((bf16[32,2,128]{2,1,0:T(2,128)(2,1)}), bf16[32,2,128]{2,1,0:T(2,128)(2,1)S(1)}, u32[]{:S(2)}, u32[]{:S(2)}) %all-to-all-start.1) | async-done | bytes 16416 | tf_op jit(solution)/shard_map/all_to_all | solution.py:969
  59.6 13.5 %collective-permute-done.7 = bf16[2,160,1024]{2,1,0:T(8,128)(2,1)S(1)} collective-permute-done((bf16[2,160,1024]{2,1,0:T(8,128)(2,1)S(1)}, bf16[2,160,1024]{2,1,0:T(8,128)(2,1)S(1)}, u32[]{:S(2)}, u32[]{:S(2)}) %collective-permute-start.7) | collective-permute-done | bytes 655392 | tf_op jit(solution)/shard_map/ppermute | solution.py:789
  76.4 9.8 %collective-permute-done.9 = bf16[1,128,1024]{2,1,0:T(8,128)(2,1)S(1)} collective-permute-done((bf16[1,128,1024]{2,1,0:T(8,128)(2,1)S(1)}, bf16[1,128,1024]{2,1,0:T(8,128)(2,1)S(1)}, u32[]{:S(2)}, u32[]{:S(2)}) %collective-permute-start.9) | collective-permute-done | bytes 262176 | tf_op jit(solution)/shard_map/ppermute | solution.py:789
  94.6 13.8 %collective-permute-done.13 = bf16[4,80,1024]{2,1,0:T(8,128)(2,1)S(1)} collective-permute-done((bf16[4,80,1024]{2,1,0:T(8,128)(2,1)S(1)}, bf16[4,80,1024]{2,1,0:T(8,128)(2,1)S(1)}, u32[]{:S(2)}, u32[]{:S(2)}) %collective-permute-start.13) | collective-permute-done | bytes 655392 | tf_op jit(solution)/shard_map/ppermute | solution.py:789
  114.0 5.1 %collective-permute-start.17 = (bf16[256,1024]{1,0:T(8,128)(2,1)S(1)}, bf16[256,1024]{1,0:T(8,128)(2,1)S(1)}, u32[]{:S(2)}, u32[]{:S(2)}) collective-permute-start(bf16[256,1024]{1,0:T(8,128)(2,1)S(1)} %dynamic-slice_bitcast_fusion.6), channel_id=1, source_target_pairs={{0,0},{1,1},{2,8},{3,9},{4,2},{5,3},{6,10},{7,11},{8,4},{9,5},{10,... | collective-permute-start | bytes 1572872 | tf_op jit(solution)/shard_map/ppermute | solution.py:896
  120.2 14.0 %qkv.1 = (bf16[2048,1024]{1,0:T(8,128)(2,1)}, bf16[2048,256]{1,0:T(8,128)(2,1)}, bf16[2048,256]{1,0:T(8,128)(2,1)}, bf16[2048,256]{1,0:T(8,128)(2,1)}, bf16[1024,768]{1,0:T(8,128)(2,1)}) custom-call(s32[8]{0:T(128)} %get-tuple-element.496.table, s32[8]{0:T(128)} %xor_add_fusion.2.order, bf16[2,256,1024]{2,1,0:T(8,128)(2,1)} %copy-done.51, ...), custom_call_target="tpu_custom_call" | custom-call | flops 11000000 | bytes 1024 | tf_op jit(solution)/shard_map/qkv/pallas_call | solution.py:86
  134.2 19.5 %attention_forward.1 = (bf16[8,256,256]{2,1,0:T(8,128)(2,1)}, f32[2048,256]{1,0:T(8,128)}) custom-call(s32[8]{0:T(128)} %get-tuple-element.497.table, bf16[2048,256]{1,0:T(8,128)(2,1)} %get-tuple-element.248.q_ref, bf16[2048,256]{1,0:T(8,128)(2,1)} %get-tuple-element.249.k_ref, bf16[2048,256]{1,0:T(8,128)(2,1)} %get-tuple-element.250.v_ref), custom_call_target="tpu_custom_call" | custom-call | flops 23000000 | bytes 1024 | tf_op jit(solution)/shard_map/attention_forward/pallas_call | solution.py:167
  164.9 6.5 %collective-permute-done.20.refs_3_ = bf16[512,256]{1,0:T(8,128)(2,1)S(1)} collective-permute-done((bf16[512,256]{1,0:T(8,128)(2,1)S(1)}, bf16[512,256]{1,0:T(8,128)(2,1)S(1)}, u32[]{:S(2)}, u32[]{:S(2)}) %collective-permute-start.20) | collective-permute-done | bytes 262176 | tf_op jit(solution)/shard_map/ppermute | solution.py:910
  180.3 11.8 %collective-permute-done.23.refs_3_.refs_9_ = bf16[4,128,1024]{2,1,0:T(8,128)(2,1)S(1)} collective-permute-done((bf16[4,128,1024]{2,1,0:T(8,128)(2,1)}, bf16[4,128,1024]{2,1,0:T(8,128)(2,1)S(1)}, u32[]{:S(2)}, u32[]{:S(2)}) %collective-permute-start.23) | collective-permute-done | bytes 1048608 | tf_op jit(solution)/shard_map/ppermute | solution.py:789
  194.9 12.9 %mlp_up.1 = (bf16[1024,2048]{1,0:T(8,128)(2,1)}, bf16[1024,2048]{1,0:T(8,128)(2,1)}) custom-call(s32[3,16]{1,0:T(4,128)} %copy-done.43, bf16[512,1024]{1,0:T(8,128)(2,1)} %copy-done.41, bf16[512,1024]{1,0:T(8,128)(2,1)} %collective-permute-done.22.refs_2_, bf16[8,80,1024]{2,1,0:T(8,128)(2,1)} %pad_maximum_fusion.2.refs_0_.refs_3_.refs_4_, ...), custom_call_target="tpu_custom_call" | custom-call | flops 11000000 | bytes 1024 | tf_op jit(solution)/shard_map/mlp_up/pallas_call | solution.py:451
  208.8 10.4 %mlp_down.1 = (f32[512,1024]{1,0:T(8,128)}, bf16[512,1024]{1,0:T(8,128)(2,1)}) custom-call(s32[3,16]{1,0:T(4,128)} %copy-done.43, bf16[1024,2048]{1,0:T(8,128)(2,1)} %get-tuple-element.268.refs_1_, bf16[4,128,1024]{2,1,0:T(8,128)(2,1)} %pad_maximum_fusion.7.refs_2_.refs_8_, bf16[4,128,1024]{2,1,0:T(8,128)(2,1)} %copy-done.49, ...), custom_call_target="tpu_custom_call" | custom-call | flops 9000000 | bytes 1024 | tf_op jit(solution)/shard_map/mlp_down/pallas_call | solution.py:451
  231.5 7.4 %convolution_convert_fusion.1 = bf16[2048,1024]{1,0:T(8,128)(2,1)S(1)} fusion(bf16[1024,2048]{1,0:T(8,128)(2,1)} %get-tuple-element.268.refs_1_, bf16[512,1024]{1,0:T(8,128)(2,1)S(1)} %collective-permute-done.29.refs_2_, bf16[512,1024]{1,0:T(8,128)(2,1)} %get-tuple-element.281.refs_1_), kind=kOutput, calls=%fused_computation.3 | convolution fusion | flops 4301258752 | bytes 10485760 | tf_op jit(solution)/shard_map/dot_general | solution.py:30
  249.4 19.2 %mlp_backward.1 = (bf16[1024,2048]{1,0:T(8,128)(2,1)}, f32[512,1024]{1,0:T(8,128)}, bf16[512,1024]{1,0:T(8,128)(2,1)}) custom-call(s32[3,16]{1,0:T(4,128)} %copy-done.43, bf16[512,1024]{1,0:T(8,128)(2,1)} %get-tuple-element.281.refs_1_, bf16[512,1024]{1,0:T(8,128)(2,1)} %copy-done.59, bf16[1024,2048]{1,0:T(8,128)(2,1)} %get-tuple-element.283.refs_3_, ...), custom_call_target="tpu_custom_call" | custom-call | flops 20000000 | bytes 1024 | tf_op jit(solution)/shard_map/mlp_backward/pallas_call | solution.py:451
  278.4 9.0 %turn.1 = (f32[512,1024]{1,0:T(8,128)}, bf16[512,1024]{1,0:T(8,128)(2,1)}, bf16[512,256]{1,0:T(8,128)(2,1)}, bf16[512,256]{1,0:T(8,128)(2,1)}, bf16[512,256]{1,0...) custom-call(f32[512,1024]{1,0:T(8,128)} %get-tuple-element.300.own_ref, bf16[512,1024]{1,0:T(8,128)(2,1)} %copy-done.60, ...), custom_call_target="tpu_custom_call" | custom-call | flops 6000000 | bytes 1024 | tf_op jit(solution)/shard_map/turn/pallas_call | solution.py:702
  302.8 7.1 %convolution_convert_fusion = bf16[1024,2048]{1,0:T(8,128)(2,1)S(1)} fusion(bf16[1024,2048]{1,0:T(8,128)(2,1)} %get-tuple-element.327, bf16[512,1024]{1,0:T(8,128)(2,1)} %collective-permute-done.22.refs_2_, bf16[512,1024]{1,0:T(8,128)(2,1)S(1)} %copy-done.42), kind=kOutput, calls=%fused_computation.2 | convolution fusion | flops 4301258752 | bytes 10485760 | tf_op jit(solution)/shard_map/dot_general | solution.py:30
  320.4 20.9 %attention_backward.2.refs_0_ = bf16[2048,384]{1,0:T(8,128)(2,1)S(1)} custom-call(s32[8]{0:T(128)S(1)} %copy-done.44, bf16[2048,256]{1,0:T(8,128)(2,1)S(1)} %copy-done.4, bf16[2048,256]{1,0:T(8,128)(2,1)S(1)} %copy-done.5, bf16[2048,256]{1,0:T(8,128)(2,1)S(1)} %copy-done.7, bf16[8,256,256]{2,1,0:T(8,128)(2,1)S(1)} %copy-done.10, ...), custom_call_target="tpu_custom_call" | custom-call | flops 44000000 | bytes 1024 | tf_op jit(solution)/shard_map/attention_backward/pallas_call | solution.py:302
  350.8 5.5 %all-to-all-start.2 = ((bf16[32,32,384]{2,1,0:T(8,128)(2,1)}), bf16[32,32,384]{2,1,0:T(8,128)(2,1)}, u32[]{:S(2)}, u32[]{:S(2)}) async-start(bf16[32,32,384]{2,1,0:T(8,128)(2,1)} %bitcast.234), calls=%async_computation.2 | async-start | bytes 1572864 | tf_op jit(solution)/shard_map/all_to_all | solution.py:1202
  356.9 5.7 %relay.7 = (bf16[4,32,2048]{2,1,0:T(8,128)(2,1)}, bf16[4,32,512]{2,1,0:T(8,128)(2,1)}, bf16[1,128,2048]{2,1,0:T(8,128)(2,1)}, bf16[1,128,512]{2,1,0:T(8,128)(2,1...) custom-call(s32[3]{0:T(128)} %pad_add_fusion.2.here, ...), custom_call_target="tpu_custom_call" | custom-call | flops 4000000 | bytes 1024 | tf_op jit(solution)/shard_map/relay/pallas_call | solution.py:530
  374.5 20.6 %attention_backward.3.refs_1_ = bf16[2048,384]{1,0:T(8,128)(2,1)S(1)} custom-call(s32[8]{0:T(128)S(1)} %copy-done.44, bf16[2048,256]{1,0:T(8,128)(2,1)S(1)} %copy-done.4, bf16[2048,256]{1,0:T(8,128)(2,1)S(1)} %copy-done.6, bf16[2048,256]{1,0:T(8,128)(2,1)S(1)} %copy-done.8, bf16[8,256,256]{2,1,0:T(8,128)(2,1)S(1)} %copy-done.11, ...), custom_call_target="tpu_custom_call" | custom-call | flops 44000000 | bytes 1024 | tf_op jit(solution)/shard_map/attention_backward/pallas_call | solution.py:302
  402.2 6.9 %input_grad.1 = (bf16[4,256,1024]{2,1,0:T(8,128)(2,1)S(1)}, bf16[4,256,1024]{2,1,0:T(8,128)(2,1)S(1)}) custom-call(s32[8]{0:T(128)S(1)} %gather_fusion, bf16[2048,384]{1,0:T(8,128)(2,1)S(1)} %copy-done.19, bf16[2048,384]{1,0:T(8,128)(2,1)S(1)} %copy-done.21, bf16[1024,768]{1,0:T(8,128)(2,1)S(1)} %copy-done.38), custom_call_target="tpu_custom_call" | custom-call | flops 6000000 | bytes 1024 | tf_op jit(solution)/shard_map/input_grad/pallas_call | solution.py:742
  421.3 5.4 %collective-permute-done.50 = bf16[2,32,5120]{2,1,0:T(8,128)(2,1)} collective-permute-done((bf16[2,32,5120]{2,1,0:T(8,128)(2,1)S(1)}, bf16[2,32,5120]{2,1,0:T(8,128)(2,1)}, u32[]{:S(2)}, u32[]{:S(2)}) %collective-permute-start.50) | collective-permute-done | bytes 655392 | tf_op jit(solution)/shard_map/ppermute | solution.py:789
  434.3 19.9 %collective-permute-done.51 = bf16[1,32,5120]{2,1,0:T(8,128)(2,1)S(1)} collective-permute-done((bf16[1,32,5120]{2,1,0:T(8,128)(2,1)}, bf16[1,32,5120]{2,1,0:T(8,128)(2,1)S(1)}, u32[]{:S(2)}, u32[]{:S(2)}) %collective-permute-start.51) | collective-permute-done | bytes 327712 | tf_op jit(solution)/shard_map/ppermute | solution.py:789
  (441 shorter events, 214.5 us)
Async XLA Ops:
  3.9 53.5 %collective-permute-start = (bf16[256,1024]{1,0:T(8,128)(2,1)}, bf16[256,1024]{1,0:T(8,128)(2,1)S(1)}, u32[]{:S(2)}, u32[]{:S(2)}) collective-permute-start(bf16[256,1024]{1,0:T(8,128)(2,1)} %get-tuple-element.459), channel_id=1, source_target_pairs={{0,0},{1,1},{2,8},{3,9},{4,2},{5,3},{6,10},{7,11},{8,4},{9,5},{10,... | collective-permute-start | bytes 1572872 | tf_op jit(solution)/shard_map/ppermute | solution.py:896
  9.6 47.7 %collective-permute-start.1 = (bf16[256,1024]{1,0:T(8,128)(2,1)}, bf16[256,1024]{1,0:T(8,128)(2,1)S(1)}, u32[]{:S(2)}, u32[]{:S(2)}) collective-permute-start(bf16[256,1024]{1,0:T(8,128)(2,1)} %get-tuple-element.458), channel_id=1, source_target_pairs={{0,2},{1,3},{2,10},{3,11},{4,0},{5,1},{6,8},{7,9},{8,6},{9,7},{10,... | collective-permute-start | bytes 1572872 | tf_op jit(solution)/shard_map/ppermute | solution.py:896
  19.9 37.4 %collective-permute-start.3 = (bf16[1,160,1024]{2,1,0:T(8,128)(2,1)S(1)}, bf16[1,160,1024]{2,1,0:T(8,128)(2,1)S(1)}, u32[]{:S(2)}, u32[]{:S(2)}) collective-permute-start(bf16[1,160,1024]{2,1,0:T(8,128)(2,1)S(1)} %maximum_bitcast_fusion), channel_id=1, source_target_pairs={{0,4},{2,6},{4,0},{6,2},{1,5},{3,7},{5,1},{7,3},{8,12},{10,14},{12... | collective-permute-start | bytes 983048 | tf_op jit(solution)/shard_map/ppermute | solution.py:789
  23.9 32.5 %all-to-all-start.1 = ((bf16[32,2,128]{2,1,0:T(2,128)(2,1)}), bf16[32,2,128]{2,1,0:T(2,128)(2,1)S(1)}, u32[]{:S(2)}, u32[]{:S(2)}) async-start(bf16[32,2,128]{2,1,0:T(2,128)(2,1)} %reshape.310), calls=%async_computation.1 | async-start | bytes 32768 | tf_op jit(solution)/shard_map/all_to_all | solution.py:969
  58.0 30.5 %collective-permute-start.5 = (bf16[2,256,1024]{2,1,0:T(8,128)(2,1)S(1)}, bf16[2,256,1024]{2,1,0:T(8,128)(2,1)S(1)}, u32[]{:S(2)}, u32[]{:S(2)}) collective-permute-start(bf16[2,256,1024]{2,1,0:T(8,128)(2,1)S(1)} %pad_maximum_fusion.6.refs_0_), channel_id=1, source_target_pairs={{0,1},{1,0},{2,3},{3,2},{4,5},{5,4},{6,7},{7,6},{8,9},{9,8},{10,11... | collective-permute-start | bytes 3145736 | tf_op jit(solution)/shard_map/ppermute | solution.py:910
  58.3 30.2 %collective-permute-start.6 = (bf16[2,256,1024]{2,1,0:T(8,128)(2,1)S(1)}, bf16[2,256,1024]{2,1,0:T(8,128)(2,1)S(1)}, u32[]{:S(2)}, u32[]{:S(2)}) collective-permute-start(bf16[2,256,1024]{2,1,0:T(8,128)(2,1)S(1)} %pad_maximum_fusion.6.refs_0_), channel_id=1, source_target_pairs={{0,8},{1,9},{2,10},{3,11},{4,12},{5,13},{6,14},{7,15},{8,0},{9,1},... | collective-permute-start | bytes 3145736 | tf_op jit(solution)/shard_map/ppermute | solution.py:910
  112.5 41.2 %collective-permute-start.15 = (bf16[8,80,1024]{2,1,0:T(8,128)(2,1)}, bf16[8,80,1024]{2,1,0:T(8,128)(2,1)}, u32[]{:S(2)}, u32[]{:S(2)}) collective-permute-start(bf16[8,80,1024]{2,1,0:T(8,128)(2,1)} %pad_maximum_fusion.2.refs_0_.refs_3_.refs_4_), channel_id=1, source_target_pairs={{0,16},{16,0},{1,17},{17,1},{2,18},{18,2},{3,19},{19,3},{4,20},{20... | collective-permute-start | bytes 3932168 | tf_op jit(solution)/shard_map/ppermute | solution.py:789
  114.0 39.8 %collective-permute-start.16 = (bf16[8,80,1024]{2,1,0:T(8,128)(2,1)S(1)}, bf16[8,80,1024]{2,1,0:T(8,128)(2,1)}, u32[]{:S(2)}, u32[]{:S(2)}) collective-permute-start(bf16[8,80,1024]{2,1,0:T(8,128)(2,1)S(1)} %pad_maximum_fusion.3.refs_2_.refs_5_.refs_6_), channel_id=1, source_target_pairs={{0,1},{1,0},{2,3},{3,2},{4,5},{5,4},{6,7},{7,6},{8,9},{9,8},{10,11... | collective-permute-start | bytes 3932168 | tf_op jit(solution)/shard_map/ppermute | solution.py:789
  114.0 39.7 %collective-permute-start.17 = (bf16[256,1024]{1,0:T(8,128)(2,1)S(1)}, bf16[256,1024]{1,0:T(8,128)(2,1)S(1)}, u32[]{:S(2)}, u32[]{:S(2)}) collective-permute-start(bf16[256,1024]{1,0:T(8,128)(2,1)S(1)} %dynamic-slice_bitcast_fusion.6), channel_id=1, source_target_pairs={{0,0},{1,1},{2,8},{3,9},{4,2},{5,3},{6,10},{7,11},{8,4},{9,5},{10,... | collective-permute-start | bytes 1572872 | tf_op jit(solution)/shard_map/ppermute | solution.py:896
  158.8 33.3 %collective-permute-start.23 = (bf16[4,128,1024]{2,1,0:T(8,128)(2,1)}, bf16[4,128,1024]{2,1,0:T(8,128)(2,1)S(1)}, u32[]{:S(2)}, u32[]{:S(2)}) collective-permute-start(bf16[4,128,1024]{2,1,0:T(8,128)(2,1)} %pad_maximum_fusion.7.refs_2_.refs_8_), channel_id=1, source_target_pairs={{0,1},{1,0},{2,3},{3,2},{4,5},{5,4},{6,7},{7,6},{8,9},{9,8},{10,11... | collective-permute-start | bytes 3145736 | tf_op jit(solution)/shard_map/ppermute | solution.py:789
  163.9 28.1 %collective-permute-start.24 = (bf16[4,128,1024]{2,1,0:T(8,128)(2,1)}, bf16[4,128,1024]{2,1,0:T(8,128)(2,1)S(1)}, u32[]{:S(2)}, u32[]{:S(2)}) collective-permute-start(bf16[4,128,1024]{2,1,0:T(8,128)(2,1)} %pad_maximum_fusion.7.refs_2_.refs_8_), channel_id=1, source_target_pairs={{0,16},{16,0},{1,17},{17,1},{2,18},{18,2},{3,19},{19,3},{4,20},{20... | collective-permute-start | bytes 3145736 | tf_op jit(solution)/shard_map/ppermute | solution.py:789
  178.9 28.8 %collective-permute-start.25 = (bf16[256,1024]{1,0:T(8,128)(2,1)}, bf16[256,1024]{1,0:T(8,128)(2,1)S(1)}, u32[]{:S(2)}, u32[]{:S(2)}) collective-permute-start(bf16[256,1024]{1,0:T(8,128)(2,1)} %dynamic-slice_bitcast_fusion.5), channel_id=1, source_target_pairs={{0,2},{1,3},{2,10},{3,11},{4,0},{5,1},{6,8},{7,9},{8,6},{9,7},{10,... | collective-permute-start | bytes 1572872 | tf_op jit(solution)/shard_map/ppermute | solution.py:896
  242.0 29.1 %collective-permute-start.30 = (bf16[2,1,4,1,64,1024]{5,4,3,2,1,0:T(8,128)(2,1)S(1)}, bf16[2,1,4,1,64,1024]{5,4,3,2,1,0:T(8,128)(2,1)S(1)}, u32[]{:S(2)}, u32[]{:S(2)}) collective-permute-start(bf16[2,1,4,1,64,1024]{5,4,3,2,1,0:T(8,128)(2,1)S(1)} %get-tuple-element.287), channel_id=1, source_target_pairs={{0,1},{1,0},{2,3},{3,2},{4,5},{5,4},{6,7},{7,6},{8,9},{9,8},{10,11... | collective-permute-start | bytes 3145736 | tf_op jit(solution)/shard_map/ppermute | solution.py:789
  242.8 28.3 %collective-permute-start.31 = (bf16[1,1,4,2,64,1024]{5,4,3,2,1,0:T(8,128)(2,1)S(1)}, bf16[1,1,4,2,64,1024]{5,4,3,2,1,0:T(8,128)(2,1)S(1)}, u32[]{:S(2)}, u32[]{:S(2)}) collective-permute-start(bf16[1,1,4,2,64,1024]{5,4,3,2,1,0:T(8,128)(2,1)S(1)} %get-tuple-element.288), channel_id=1, source_target_pairs={{0,16},{16,0},{1,17},{17,1},{2,18},{18,2},{3,19},{19,3},{4,20},{20... | collective-permute-start | bytes 3145736 | tf_op jit(solution)/shard_map/ppermute | solution.py:789
  243.5 27.6 %collective-permute-start.32 = (bf16[256,1024]{1,0:T(8,128)(2,1)S(1)}, bf16[256,1024]{1,0:T(8,128)(2,1)S(1)}, u32[]{:S(2)}, u32[]{:S(2)}) collective-permute-start(bf16[256,1024]{1,0:T(8,128)(2,1)S(1)} %get-tuple-element.453), channel_id=1, source_target_pairs={{0,0},{1,1},{8,2},{9,3},{2,4},{3,5},{10,6},{11,7},{4,8},{5,9},{12,... | collective-permute-start | bytes 1572872 | tf_op jit(solution)/shard_map/ppermute | solution.py:899
  318.1 30.5 %collective-permute-start.42 = (bf16[1,1,4,2,32,2560]{5,4,3,2,1,0:T(8,128)(2,1)S(1)}, bf16[1,1,4,2,32,2560]{5,4,3,2,1,0:T(8,128)(2,1)S(1)}, u32[]{:S(2)}, u32[]{:S(2)}) collective-permute-start(bf16[1,1,4,2,32,2560]{5,4,3,2,1,0:T(8,128)(2,1)S(1)} %pad_maximum_fusion.4), channel_id=1, source_target_pairs={{0,16},{16,0},{1,17},{17,1},{2,18},{18,2},{3,19},{19,3},{4,20},{20... | collective-permute-start | bytes 3932168 | tf_op jit(solution)/shard_map/ppermute | solution.py:789
  318.8 30.1 %collective-permute-start.43 = (bf16[2,1,4,1,32,2560]{5,4,2,0,3,1:T(8,128)(2,1)S(1)}, bf16[2,1,4,1,32,2560]{5,4,2,0,3,1:T(8,128)(2,1)S(1)}, u32[]{:S(2)}, u32[]{:S(2)}) collective-permute-start(bf16[2,1,4,1,32,2560]{5,4,2,0,3,1:T(8,128)(2,1)S(1)} %pad_maximum_fusion.5), channel_id=1, source_target_pairs={{0,1},{1,0},{2,3},{3,2},{4,5},{5,4},{6,7},{7,6},{8,9},{9,8},{10,11... | collective-permute-start | bytes 3932168 | tf_op jit(solution)/shard_map/ppermute | solution.py:789
  350.8 45.6 %all-to-all-start.2 = ((bf16[32,32,384]{2,1,0:T(8,128)(2,1)}), bf16[32,32,384]{2,1,0:T(8,128)(2,1)}, u32[]{:S(2)}, u32[]{:S(2)}) async-start(bf16[32,32,384]{2,1,0:T(8,128)(2,1)} %bitcast.234), calls=%async_computation.2 | async-start | bytes 1572864 | tf_op jit(solution)/shard_map/all_to_all | solution.py:1202
  362.6 33.7 %collective-permute-start.45 = (bf16[4,32,2560]{2,1,0:T(8,128)(2,1)}, bf16[4,32,2560]{2,1,0:T(8,128)(2,1)}, u32[]{:S(2)}, u32[]{:S(2)}) collective-permute-start(bf16[4,32,2560]{2,1,0:T(8,128)(2,1)} %get-tuple-element.356), channel_id=1, source_target_pairs={{0,1},{1,0},{2,3},{3,2},{4,5},{5,4},{6,7},{7,6},{8,9},{9,8},{10,11... | collective-permute-start | bytes 1966088 | tf_op jit(solution)/shard_map/ppermute | solution.py:789
  364.0 32.3 %collective-permute-start.46 = (bf16[1,128,2560]{2,1,0:T(8,128)(2,1)}, bf16[1,128,2560]{2,1,0:T(8,128)(2,1)}, u32[]{:S(2)}, u32[]{:S(2)}) collective-permute-start(bf16[1,128,2560]{2,1,0:T(8,128)(2,1)} %get-tuple-element.357), channel_id=1, source_target_pairs={{0,16},{16,0},{1,17},{17,1},{2,18},{18,2},{3,19},{19,3},{4,20},{20... | collective-permute-start | bytes 1966088 | tf_op jit(solution)/shard_map/ppermute | solution.py:789
  365.2 31.1 %collective-permute-start.44 = (bf16[1,64,2048]{2,1,0:T(8,128)(2,1)}, bf16[1,64,2048]{2,1,0:T(8,128)(2,1)S(1)}, u32[]{:S(2)}, u32[]{:S(2)}) collective-permute-start(bf16[1,64,2048]{2,1,0:T(8,128)(2,1)} %get-tuple-element.355), channel_id=1, source_target_pairs={{0,4},{2,6},{4,0},{6,2},{1,5},{3,7},{5,1},{7,3},{8,12},{10,14},{12... | collective-permute-start | bytes 786440 | tf_op jit(solution)/shard_map/ppermute | solution.py:789
  416.5 37.7 %collective-permute-start.49 = (bf16[256,1024]{1,0:T(8,128)(2,1)}, bf16[256,1024]{1,0:T(8,128)(2,1)}, u32[]{:S(2)}, u32[]{:S(2)}) collective-permute-start(bf16[256,1024]{1,0:T(8,128)(2,1)} %get-tuple-element.392), channel_id=1, source_target_pairs={{0,1},{1,0},{2,3},{3,2},{4,5},{5,4},{6,7},{7,6},{8,9},{9,8},{10,11... | collective-permute-start | bytes 1572872 | tf_op jit(solution)/shard_map/ppermute | solution.py:910
  416.8 37.5 %collective-permute-start.48 = (bf16[256,1024]{1,0:T(8,128)(2,1)}, bf16[256,1024]{1,0:T(8,128)(2,1)}, u32[]{:S(2)}, u32[]{:S(2)}) collective-permute-start(bf16[256,1024]{1,0:T(8,128)(2,1)} %get-tuple-element.381), channel_id=1, source_target_pairs={{0,1},{1,0},{2,3},{3,2},{4,5},{5,4},{6,7},{7,6},{8,9},{9,8},{10,11... | collective-permute-start | bytes 1572872 | tf_op jit(solution)/shard_map/ppermute | solution.py:910
  429.3 61.7 %all-to-all-start.3 = ((bf16[32,32,384]{2,1,0:T(8,128)(2,1)}), bf16[32,32,384]{2,1,0:T(8,128)(2,1)}, u32[]{:S(2)}, u32[]{:S(2)}) async-start(bf16[32,32,384]{2,1,0:T(8,128)(2,1)} %bitcast.233), calls=%async_computation.3 | async-start | bytes 1572864 | tf_op jit(solution)/shard_map/all_to_all | solution.py:1248
  (139 other events, 1542.0 us)

commit v6 on v5

--- a/solution.py
+++ b/solution.py
@@ -320,7 +320,7 @@
             ],
         ),
         compiler_params=pltpu.CompilerParams(
-            dimension_semantics=("arbitrary",), vmem_limit_bytes=28 << 20
+            dimension_semantics=("arbitrary",), vmem_limit_bytes=(56 if pair else 28) << 20
         ),
         cost_estimate=cost(44),
         name="attention_backward",

time: 501 us -> 497 us (level)
  local copies, waits for them, and re-layouts: 46.7 us -> 39.1 us
    unnamed x205 -> x195, local copies, waits for them, and re-layouts: 23.6 us -> 15.9 us
  transfers between devices with their start and end apart: 64 -> 64, of which waited for: 24 -> 24; matrix products, arithmetic and copies ran while one was open for 10% -> 11% of each run, Pallas kernels for 28% -> 29%
where the time goes in v6:
time: 497 us; the launch traced here: 490 us
  Pallas kernels  171 us (34%)
  waiting for transfers between devices  143 us (29%)
  starting transfers between devices  86.4 us (17%)
  local copies, waits for them, and re-layouts  39.1 us (8%)
  matrix products  24.1 us (5%)
  other arithmetic  23.7 us (5%)
    ppermute x40, waiting for transfers between devices, flip(): return lax.ppermute(x, axis, [(i, i ^ bit) for i in range(size)])  104 us
    pallas_call x2, Pallas kernels, attention_backward(): pl.pallas_call(functools.partial(backward_kernel, bk=bk, rows=rows), out_...  45.1 us
    pallas_call x3, Pallas kernels, mlp_call(): pl.pallas_call(functools.partial(kernel, tables=len(tables)), out_shape=[...  42.4 us
    ppermute x40, starting transfers between devices, flip(): return lax.ppermute(x, axis, [(i, i ^ bit) for i in range(size)])  34.3 us
    dot_general x8, matrix products, dot(): return lax.dot_general(left, right, dims, preferred_element_type=F32)  24.1 us
    all_to_all x1, waiting for transfers between devices, body(): vectors = lax.all_to_all(vectors, AXES, 0, 0, tiled=True)  20.2 us
    pallas_call x1, Pallas kernels, attention_forward(): pl.pallas_call(functools.partial(forward_kernel, bq=bq, bk=bk, rows=rows)...  19.5 us
    pallas_call x5, Pallas kernels, relay(): pl.pallas_call(functools.partial(relay_kernel, layout=tuple(layout), arri...  18.5 us
  transfers between devices with their start and end apart: 64, of which 24 were waited for; matrix products, arithmetic and copies ran while one was open for 11% of the time, Pallas kernels for 29%

profile of v6, /device:TPU:1, one launch (start us, length us, event | category | flops | bytes accessed | tf_op | source)
XLA Modules:
  0.0 489.6 jit_solution(17205925306782894616)
XLA Ops:
  3.9 5.7 %collective-permute-start = (bf16[256,1024]{1,0:T(8,128)(2,1)}, bf16[256,1024]{1,0:T(8,128)(2,1)S(1)}, u32[]{:S(2)}, u32[]{:S(2)}) collective-permute-start(bf16[256,1024]{1,0:T(8,128)(2,1)} %get-tuple-element.459), channel_id=1, source_target_pairs={{0,0},{1,1},{2,8},{3,9},{4,2},{5,3},{6,10},{7,11},{8,4},{9,5},{10,... | collective-permute-start | bytes 1572872 | tf_op jit(solution)/shard_map/ppermute | solution.py:896
  28.3 5.6 %fusion.11 = (f32[2048,128]{1,0:T(8,128)}, f32[2048,128]{1,0:T(8,128)}) fusion(f32[128]{0:T(128)S(1)} %get-tuple-element.494, f32[128]{0:T(128)S(1)} %get-tuple-element.495, f32[2048]{0:T(1024)S(1)} %iota_convert_fusion), kind=kLoop, calls=%fused_computation.30 | loop fusion | flops 524288 | bytes 2106368 | tf_op jit(solution)/shard_map/mul | solution.py:959
  36.3 20.2 %all-to-all-done.1 = bf16[32,2,128]{2,1,0:T(2,128)(2,1)S(1)} async-done(((bf16[32,2,128]{2,1,0:T(2,128)(2,1)}), bf16[32,2,128]{2,1,0:T(2,128)(2,1)S(1)}, u32[]{:S(2)}, u32[]{:S(2)}) %all-to-all-start.1) | async-done | bytes 16416 | tf_op jit(solution)/shard_map/all_to_all | solution.py:969
  59.6 13.5 %collective-permute-done.7 = bf16[2,160,1024]{2,1,0:T(8,128)(2,1)S(1)} collective-permute-done((bf16[2,160,1024]{2,1,0:T(8,128)(2,1)S(1)}, bf16[2,160,1024]{2,1,0:T(8,128)(2,1)S(1)}, u32[]{:S(2)}, u32[]{:S(2)}) %collective-permute-start.7) | collective-permute-done | bytes 655392 | tf_op jit(solution)/shard_map/ppermute | solution.py:789
  76.4 9.9 %collective-permute-done.9 = bf16[1,128,1024]{2,1,0:T(8,128)(2,1)S(1)} collective-permute-done((bf16[1,128,1024]{2,1,0:T(8,128)(2,1)S(1)}, bf16[1,128,1024]{2,1,0:T(8,128)(2,1)S(1)}, u32[]{:S(2)}, u32[]{:S(2)}) %collective-permute-start.9) | collective-permute-done | bytes 262176 | tf_op jit(solution)/shard_map/ppermute | solution.py:789
  94.6 13.8 %collective-permute-done.13 = bf16[4,80,1024]{2,1,0:T(8,128)(2,1)S(1)} collective-permute-done((bf16[4,80,1024]{2,1,0:T(8,128)(2,1)S(1)}, bf16[4,80,1024]{2,1,0:T(8,128)(2,1)S(1)}, u32[]{:S(2)}, u32[]{:S(2)}) %collective-permute-start.13) | collective-permute-done | bytes 655392 | tf_op jit(solution)/shard_map/ppermute | solution.py:789
  114.0 5.1 %collective-permute-start.17 = (bf16[256,1024]{1,0:T(8,128)(2,1)S(1)}, bf16[256,1024]{1,0:T(8,128)(2,1)S(1)}, u32[]{:S(2)}, u32[]{:S(2)}) collective-permute-start(bf16[256,1024]{1,0:T(8,128)(2,1)S(1)} %dynamic-slice_bitcast_fusion.6), channel_id=1, source_target_pairs={{0,0},{1,1},{2,8},{3,9},{4,2},{5,3},{6,10},{7,11},{8,4},{9,5},{10,... | collective-permute-start | bytes 1572872 | tf_op jit(solution)/shard_map/ppermute | solution.py:896
  120.2 14.0 %qkv.1 = (bf16[2048,1024]{1,0:T(8,128)(2,1)}, bf16[2048,256]{1,0:T(8,128)(2,1)}, bf16[2048,256]{1,0:T(8,128)(2,1)}, bf16[2048,256]{1,0:T(8,128)(2,1)}, bf16[1024,768]{1,0:T(8,128)(2,1)}) custom-call(s32[8]{0:T(128)} %get-tuple-element.496.table, s32[8]{0:T(128)} %xor_add_fusion.2.order, bf16[2,256,1024]{2,1,0:T(8,128)(2,1)} %copy-done.45, ...), custom_call_target="tpu_custom_call" | custom-call | flops 11000000 | bytes 1024 | tf_op jit(solution)/shard_map/qkv/pallas_call | solution.py:86
  134.2 19.5 %attention_forward.1 = (bf16[8,256,256]{2,1,0:T(8,128)(2,1)}, f32[2048,256]{1,0:T(8,128)}) custom-call(s32[8]{0:T(128)} %get-tuple-element.497.table, bf16[2048,256]{1,0:T(8,128)(2,1)} %get-tuple-element.248.q_ref, bf16[2048,256]{1,0:T(8,128)(2,1)} %get-tuple-element.249.k_ref, bf16[2048,256]{1,0:T(8,128)(2,1)} %get-tuple-element.250.v_ref), custom_call_target="tpu_custom_call" | custom-call | flops 23000000 | bytes 1024 | tf_op jit(solution)/shard_map/attention_forward/pallas_call | solution.py:167
  164.9 6.5 %collective-permute-done.20.refs_3_ = bf16[512,256]{1,0:T(8,128)(2,1)S(1)} collective-permute-done((bf16[512,256]{1,0:T(8,128)(2,1)S(1)}, bf16[512,256]{1,0:T(8,128)(2,1)S(1)}, u32[]{:S(2)}, u32[]{:S(2)}) %collective-permute-start.20) | collective-permute-done | bytes 262176 | tf_op jit(solution)/shard_map/ppermute | solution.py:910
  180.3 11.8 %collective-permute-done.23.refs_3_.refs_9_ = bf16[4,128,1024]{2,1,0:T(8,128)(2,1)S(1)} collective-permute-done((bf16[4,128,1024]{2,1,0:T(8,128)(2,1)}, bf16[4,128,1024]{2,1,0:T(8,128)(2,1)S(1)}, u32[]{:S(2)}, u32[]{:S(2)}) %collective-permute-start.23) | collective-permute-done | bytes 1048608 | tf_op jit(solution)/shard_map/ppermute | solution.py:789
  194.9 12.9 %mlp_up.1 = (bf16[1024,2048]{1,0:T(8,128)(2,1)}, bf16[1024,2048]{1,0:T(8,128)(2,1)}) custom-call(s32[3,16]{1,0:T(4,128)} %copy-done.37, bf16[512,1024]{1,0:T(8,128)(2,1)} %copy-done.35, bf16[512,1024]{1,0:T(8,128)(2,1)} %collective-permute-done.22.refs_2_, bf16[8,80,1024]{2,1,0:T(8,128)(2,1)} %pad_maximum_fusion.2.refs_0_.refs_3_.refs_4_, ...), custom_call_target="tpu_custom_call" | custom-call | flops 11000000 | bytes 1024 | tf_op jit(solution)/shard_map/mlp_up/pallas_call | solution.py:451
  208.9 10.3 %mlp_down.1 = (f32[512,1024]{1,0:T(8,128)}, bf16[512,1024]{1,0:T(8,128)(2,1)}) custom-call(s32[3,16]{1,0:T(4,128)} %copy-done.37, bf16[1024,2048]{1,0:T(8,128)(2,1)} %get-tuple-element.268.refs_1_, bf16[4,128,1024]{2,1,0:T(8,128)(2,1)} %pad_maximum_fusion.7.refs_2_.refs_8_, bf16[4,128,1024]{2,1,0:T(8,128)(2,1)} %copy-done.43, ...), custom_call_target="tpu_custom_call" | custom-call | flops 9000000 | bytes 1024 | tf_op jit(solution)/shard_map/mlp_down/pallas_call | solution.py:451
  231.6 7.4 %convolution_convert_fusion.1 = bf16[2048,1024]{1,0:T(8,128)(2,1)S(1)} fusion(bf16[1024,2048]{1,0:T(8,128)(2,1)} %get-tuple-element.268.refs_1_, bf16[512,1024]{1,0:T(8,128)(2,1)S(1)} %collective-permute-done.29.refs_2_, bf16[512,1024]{1,0:T(8,128)(2,1)} %get-tuple-element.281.refs_1_), kind=kOutput, calls=%fused_computation.3 | convolution fusion | flops 4301258752 | bytes 10485760 | tf_op jit(solution)/shard_map/dot_general | solution.py:30
  249.5 19.2 %mlp_backward.1 = (bf16[1024,2048]{1,0:T(8,128)(2,1)}, f32[512,1024]{1,0:T(8,128)}, bf16[512,1024]{1,0:T(8,128)(2,1)}) custom-call(s32[3,16]{1,0:T(4,128)} %copy-done.37, bf16[512,1024]{1,0:T(8,128)(2,1)} %get-tuple-element.281.refs_1_, bf16[512,1024]{1,0:T(8,128)(2,1)} %copy-done.54, bf16[1024,2048]{1,0:T(8,128)(2,1)} %get-tuple-element.283.refs_3_, ...), custom_call_target="tpu_custom_call" | custom-call | flops 20000000 | bytes 1024 | tf_op jit(solution)/shard_map/mlp_backward/pallas_call | solution.py:451
  278.6 9.1 %turn.1 = (f32[512,1024]{1,0:T(8,128)}, bf16[512,1024]{1,0:T(8,128)(2,1)}, bf16[512,256]{1,0:T(8,128)(2,1)}, bf16[512,256]{1,0:T(8,128)(2,1)}, bf16[512,256]{1,0...) custom-call(f32[512,1024]{1,0:T(8,128)} %get-tuple-element.300.own_ref, bf16[512,1024]{1,0:T(8,128)(2,1)} %copy-done.55, ...), custom_call_target="tpu_custom_call" | custom-call | flops 6000000 | bytes 1024 | tf_op jit(solution)/shard_map/turn/pallas_call | solution.py:702
  302.9 7.1 %convolution_convert_fusion = bf16[1024,2048]{1,0:T(8,128)(2,1)S(1)} fusion(bf16[1024,2048]{1,0:T(8,128)(2,1)} %get-tuple-element.327, bf16[512,1024]{1,0:T(8,128)(2,1)} %collective-permute-done.22.refs_2_, bf16[512,1024]{1,0:T(8,128)(2,1)S(1)} %copy-done.36), kind=kOutput, calls=%fused_computation.2 | convolution fusion | flops 4301258752 | bytes 10485760 | tf_op jit(solution)/shard_map/dot_general | solution.py:30
  320.5 20.9 %attention_backward.2.refs_0_ = bf16[2048,384]{1,0:T(8,128)(2,1)S(1)} custom-call(s32[8]{0:T(128)S(1)} %copy-done.38, bf16[2048,256]{1,0:T(8,128)(2,1)S(1)} %copy-done.4, bf16[2048,256]{1,0:T(8,128)(2,1)S(1)} %copy-done.5, bf16[2048,256]{1,0:T(8,128)(2,1)S(1)} %copy-done.6, bf16[8,256,256]{2,1,0:T(8,128)(2,1)S(1)} %copy-done.8, ...), custom_call_target="tpu_custom_call" | custom-call | flops 44000000 | bytes 1024 | tf_op jit(solution)/shard_map/attention_backward/pallas_call | solution.py:302
  350.9 5.3 %all-to-all-start.2 = ((bf16[32,32,384]{2,1,0:T(8,128)(2,1)}), bf16[32,32,384]{2,1,0:T(8,128)(2,1)S(1)}, u32[]{:S(2)}, u32[]{:S(2)}) async-start(bf16[32,32,384]{2,1,0:T(8,128)(2,1)} %bitcast.76), calls=%async_computation.2 | async-start | bytes 1572864 | tf_op jit(solution)/shard_map/all_to_all | solution.py:1202
  356.9 5.7 %relay.7 = (bf16[4,32,2048]{2,1,0:T(8,128)(2,1)}, bf16[4,32,512]{2,1,0:T(8,128)(2,1)}, bf16[1,128,2048]{2,1,0:T(8,128)(2,1)}, bf16[1,128,512]{2,1,0:T(8,128)(2,1...) custom-call(s32[3]{0:T(128)} %pad_add_fusion.2.here, ...), custom_call_target="tpu_custom_call" | custom-call | flops 4000000 | bytes 1024 | tf_op jit(solution)/shard_map/relay/pallas_call | solution.py:530
  367.9 24.3 %attention_backward.3.refs_1_ = bf16[2048,384]{1,0:T(8,128)(2,1)} custom-call(s32[8]{0:T(128)} %get-tuple-element.497.table, bf16[2048,256]{1,0:T(8,128)(2,1)} %get-tuple-element.248.q_ref, bf16[2048,256]{1,0:T(8,128)(2,1)} %get-tuple-element.249.k_ref, bf16[2048,256]{1,0:T(8,128)(2,1)} %get-tuple-element.250.v_ref, ...), custom_call_target="tpu_custom_call" | custom-call | flops 44000000 | bytes 1024 | tf_op jit(solution)/shard_map/attention_backward/pallas_call | solution.py:302
  398.4 6.9 %input_grad.1 = (bf16[4,256,1024]{2,1,0:T(8,128)(2,1)S(1)}, bf16[4,256,1024]{2,1,0:T(8,128)(2,1)S(1)}) custom-call(s32[8]{0:T(128)S(1)} %gather_fusion, bf16[2048,384]{1,0:T(8,128)(2,1)S(1)} %copy-done.14, bf16[2048,384]{1,0:T(8,128)(2,1)S(1)} %copy-done.15, bf16[1024,768]{1,0:T(8,128)(2,1)S(1)} %copy-done.32), custom_call_target="tpu_custom_call" | custom-call | flops 6000000 | bytes 1024 | tf_op jit(solution)/shard_map/input_grad/pallas_call | solution.py:742
  417.6 5.4 %collective-permute-done.50 = bf16[2,32,5120]{2,1,0:T(8,128)(2,1)} collective-permute-done((bf16[2,32,5120]{2,1,0:T(8,128)(2,1)S(1)}, bf16[2,32,5120]{2,1,0:T(8,128)(2,1)}, u32[]{:S(2)}, u32[]{:S(2)}) %collective-permute-start.50) | collective-permute-done | bytes 655392 | tf_op jit(solution)/shard_map/ppermute | solution.py:789
  430.5 19.9 %collective-permute-done.51 = bf16[1,32,5120]{2,1,0:T(8,128)(2,1)S(1)} collective-permute-done((bf16[1,32,5120]{2,1,0:T(8,128)(2,1)}, bf16[1,32,5120]{2,1,0:T(8,128)(2,1)S(1)}, u32[]{:S(2)}, u32[]{:S(2)}) %collective-permute-start.51) | collective-permute-done | bytes 327712 | tf_op jit(solution)/shard_map/ppermute | solution.py:789
  (431 shorter events, 207.1 us)
Async XLA Ops:
  3.9 53.5 %collective-permute-start = (bf16[256,1024]{1,0:T(8,128)(2,1)}, bf16[256,1024]{1,0:T(8,128)(2,1)S(1)}, u32[]{:S(2)}, u32[]{:S(2)}) collective-permute-start(bf16[256,1024]{1,0:T(8,128)(2,1)} %get-tuple-element.459), channel_id=1, source_target_pairs={{0,0},{1,1},{2,8},{3,9},{4,2},{5,3},{6,10},{7,11},{8,4},{9,5},{10,... | collective-permute-start | bytes 1572872 | tf_op jit(solution)/shard_map/ppermute | solution.py:896
  9.6 47.7 %collective-permute-start.1 = (bf16[256,1024]{1,0:T(8,128)(2,1)}, bf16[256,1024]{1,0:T(8,128)(2,1)S(1)}, u32[]{:S(2)}, u32[]{:S(2)}) collective-permute-start(bf16[256,1024]{1,0:T(8,128)(2,1)} %get-tuple-element.458), channel_id=1, source_target_pairs={{0,2},{1,3},{2,10},{3,11},{4,0},{5,1},{6,8},{7,9},{8,6},{9,7},{10,... | collective-permute-start | bytes 1572872 | tf_op jit(solution)/shard_map/ppermute | solution.py:896
  19.9 37.4 %collective-permute-start.3 = (bf16[1,160,1024]{2,1,0:T(8,128)(2,1)S(1)}, bf16[1,160,1024]{2,1,0:T(8,128)(2,1)S(1)}, u32[]{:S(2)}, u32[]{:S(2)}) collective-permute-start(bf16[1,160,1024]{2,1,0:T(8,128)(2,1)S(1)} %maximum_bitcast_fusion), channel_id=1, source_target_pairs={{0,4},{2,6},{4,0},{6,2},{1,5},{3,7},{5,1},{7,3},{8,12},{10,14},{12... | collective-permute-start | bytes 983048 | tf_op jit(solution)/shard_map/ppermute | solution.py:789
  23.9 32.5 %all-to-all-start.1 = ((bf16[32,2,128]{2,1,0:T(2,128)(2,1)}), bf16[32,2,128]{2,1,0:T(2,128)(2,1)S(1)}, u32[]{:S(2)}, u32[]{:S(2)}) async-start(bf16[32,2,128]{2,1,0:T(2,128)(2,1)} %reshape.310), calls=%async_computation.1 | async-start | bytes 32768 | tf_op jit(solution)/shard_map/all_to_all | solution.py:969
  58.0 30.5 %collective-permute-start.5 = (bf16[2,256,1024]{2,1,0:T(8,128)(2,1)S(1)}, bf16[2,256,1024]{2,1,0:T(8,128)(2,1)S(1)}, u32[]{:S(2)}, u32[]{:S(2)}) collective-permute-start(bf16[2,256,1024]{2,1,0:T(8,128)(2,1)S(1)} %pad_maximum_fusion.6.refs_0_), channel_id=1, source_target_pairs={{0,1},{1,0},{2,3},{3,2},{4,5},{5,4},{6,7},{7,6},{8,9},{9,8},{10,11... | collective-permute-start | bytes 3145736 | tf_op jit(solution)/shard_map/ppermute | solution.py:910
  58.3 30.2 %collective-permute-start.6 = (bf16[2,256,1024]{2,1,0:T(8,128)(2,1)S(1)}, bf16[2,256,1024]{2,1,0:T(8,128)(2,1)S(1)}, u32[]{:S(2)}, u32[]{:S(2)}) collective-permute-start(bf16[2,256,1024]{2,1,0:T(8,128)(2,1)S(1)} %pad_maximum_fusion.6.refs_0_), channel_id=1, source_target_pairs={{0,8},{1,9},{2,10},{3,11},{4,12},{5,13},{6,14},{7,15},{8,0},{9,1},... | collective-permute-start | bytes 3145736 | tf_op jit(solution)/shard_map/ppermute | solution.py:910
  112.5 41.2 %collective-permute-start.15 = (bf16[8,80,1024]{2,1,0:T(8,128)(2,1)}, bf16[8,80,1024]{2,1,0:T(8,128)(2,1)}, u32[]{:S(2)}, u32[]{:S(2)}) collective-permute-start(bf16[8,80,1024]{2,1,0:T(8,128)(2,1)} %pad_maximum_fusion.2.refs_0_.refs_3_.refs_4_), channel_id=1, source_target_pairs={{0,16},{16,0},{1,17},{17,1},{2,18},{18,2},{3,19},{19,3},{4,20},{20... | collective-permute-start | bytes 3932168 | tf_op jit(solution)/shard_map/ppermute | solution.py:789
  114.0 39.8 %collective-permute-start.16 = (bf16[8,80,1024]{2,1,0:T(8,128)(2,1)S(1)}, bf16[8,80,1024]{2,1,0:T(8,128)(2,1)}, u32[]{:S(2)}, u32[]{:S(2)}) collective-permute-start(bf16[8,80,1024]{2,1,0:T(8,128)(2,1)S(1)} %pad_maximum_fusion.3.refs_2_.refs_5_.refs_6_), channel_id=1, source_target_pairs={{0,1},{1,0},{2,3},{3,2},{4,5},{5,4},{6,7},{7,6},{8,9},{9,8},{10,11... | collective-permute-start | bytes 3932168 | tf_op jit(solution)/shard_map/ppermute | solution.py:789
  114.0 39.7 %collective-permute-start.17 = (bf16[256,1024]{1,0:T(8,128)(2,1)S(1)}, bf16[256,1024]{1,0:T(8,128)(2,1)S(1)}, u32[]{:S(2)}, u32[]{:S(2)}) collective-permute-start(bf16[256,1024]{1,0:T(8,128)(2,1)S(1)} %dynamic-slice_bitcast_fusion.6), channel_id=1, source_target_pairs={{0,0},{1,1},{2,8},{3,9},{4,2},{5,3},{6,10},{7,11},{8,4},{9,5},{10,... | collective-permute-start | bytes 1572872 | tf_op jit(solution)/shard_map/ppermute | solution.py:896
  158.8 33.3 %collective-permute-start.23 = (bf16[4,128,1024]{2,1,0:T(8,128)(2,1)}, bf16[4,128,1024]{2,1,0:T(8,128)(2,1)S(1)}, u32[]{:S(2)}, u32[]{:S(2)}) collective-permute-start(bf16[4,128,1024]{2,1,0:T(8,128)(2,1)} %pad_maximum_fusion.7.refs_2_.refs_8_), channel_id=1, source_target_pairs={{0,1},{1,0},{2,3},{3,2},{4,5},{5,4},{6,7},{7,6},{8,9},{9,8},{10,11... | collective-permute-start | bytes 3145736 | tf_op jit(solution)/shard_map/ppermute | solution.py:789
  164.0 28.1 %collective-permute-start.24 = (bf16[4,128,1024]{2,1,0:T(8,128)(2,1)}, bf16[4,128,1024]{2,1,0:T(8,128)(2,1)S(1)}, u32[]{:S(2)}, u32[]{:S(2)}) collective-permute-start(bf16[4,128,1024]{2,1,0:T(8,128)(2,1)} %pad_maximum_fusion.7.refs_2_.refs_8_), channel_id=1, source_target_pairs={{0,16},{16,0},{1,17},{17,1},{2,18},{18,2},{3,19},{19,3},{4,20},{20... | collective-permute-start | bytes 3145736 | tf_op jit(solution)/shard_map/ppermute | solution.py:789
  179.0 28.8 %collective-permute-start.25 = (bf16[256,1024]{1,0:T(8,128)(2,1)}, bf16[256,1024]{1,0:T(8,128)(2,1)S(1)}, u32[]{:S(2)}, u32[]{:S(2)}) collective-permute-start(bf16[256,1024]{1,0:T(8,128)(2,1)} %dynamic-slice_bitcast_fusion.5), channel_id=1, source_target_pairs={{0,2},{1,3},{2,10},{3,11},{4,0},{5,1},{6,8},{7,9},{8,6},{9,7},{10,... | collective-permute-start | bytes 1572872 | tf_op jit(solution)/shard_map/ppermute | solution.py:896
  242.1 29.1 %collective-permute-start.30 = (bf16[2,1,4,1,64,1024]{5,4,3,2,1,0:T(8,128)(2,1)S(1)}, bf16[2,1,4,1,64,1024]{5,4,3,2,1,0:T(8,128)(2,1)S(1)}, u32[]{:S(2)}, u32[]{:S(2)}) collective-permute-start(bf16[2,1,4,1,64,1024]{5,4,3,2,1,0:T(8,128)(2,1)S(1)} %get-tuple-element.287), channel_id=1, source_target_pairs={{0,1},{1,0},{2,3},{3,2},{4,5},{5,4},{6,7},{7,6},{8,9},{9,8},{10,11... | collective-permute-start | bytes 3145736 | tf_op jit(solution)/shard_map/ppermute | solution.py:789
  242.9 28.3 %collective-permute-start.31 = (bf16[1,1,4,2,64,1024]{5,4,3,2,1,0:T(8,128)(2,1)S(1)}, bf16[1,1,4,2,64,1024]{5,4,3,2,1,0:T(8,128)(2,1)S(1)}, u32[]{:S(2)}, u32[]{:S(2)}) collective-permute-start(bf16[1,1,4,2,64,1024]{5,4,3,2,1,0:T(8,128)(2,1)S(1)} %get-tuple-element.288), channel_id=1, source_target_pairs={{0,16},{16,0},{1,17},{17,1},{2,18},{18,2},{3,19},{19,3},{4,20},{20... | collective-permute-start | bytes 3145736 | tf_op jit(solution)/shard_map/ppermute | solution.py:789
  243.6 27.6 %collective-permute-start.32 = (bf16[256,1024]{1,0:T(8,128)(2,1)S(1)}, bf16[256,1024]{1,0:T(8,128)(2,1)S(1)}, u32[]{:S(2)}, u32[]{:S(2)}) collective-permute-start(bf16[256,1024]{1,0:T(8,128)(2,1)S(1)} %get-tuple-element.453), channel_id=1, source_target_pairs={{0,0},{1,1},{8,2},{9,3},{2,4},{3,5},{10,6},{11,7},{4,8},{5,9},{12,... | collective-permute-start | bytes 1572872 | tf_op jit(solution)/shard_map/ppermute | solution.py:899
  318.2 30.5 %collective-permute-start.42 = (bf16[1,1,4,2,32,2560]{5,4,3,2,1,0:T(8,128)(2,1)S(1)}, bf16[1,1,4,2,32,2560]{5,4,3,2,1,0:T(8,128)(2,1)S(1)}, u32[]{:S(2)}, u32[]{:S(2)}) collective-permute-start(bf16[1,1,4,2,32,2560]{5,4,3,2,1,0:T(8,128)(2,1)S(1)} %pad_maximum_fusion.4), channel_id=1, source_target_pairs={{0,16},{16,0},{1,17},{17,1},{2,18},{18,2},{3,19},{19,3},{4,20},{20... | collective-permute-start | bytes 3932168 | tf_op jit(solution)/shard_map/ppermute | solution.py:789
  318.9 30.1 %collective-permute-start.43 = (bf16[2,1,4,1,32,2560]{5,4,2,0,3,1:T(8,128)(2,1)S(1)}, bf16[2,1,4,1,32,2560]{5,4,2,0,3,1:T(8,128)(2,1)S(1)}, u32[]{:S(2)}, u32[]{:S(2)}) collective-permute-start(bf16[2,1,4,1,32,2560]{5,4,2,0,3,1:T(8,128)(2,1)S(1)} %pad_maximum_fusion.5), channel_id=1, source_target_pairs={{0,1},{1,0},{2,3},{3,2},{4,5},{5,4},{6,7},{7,6},{8,9},{9,8},{10,11... | collective-permute-start | bytes 3932168 | tf_op jit(solution)/shard_map/ppermute | solution.py:789
  350.9 41.3 %all-to-all-start.2 = ((bf16[32,32,384]{2,1,0:T(8,128)(2,1)}), bf16[32,32,384]{2,1,0:T(8,128)(2,1)S(1)}, u32[]{:S(2)}, u32[]{:S(2)}) async-start(bf16[32,32,384]{2,1,0:T(8,128)(2,1)} %bitcast.76), calls=%async_computation.2 | async-start | bytes 1572864 | tf_op jit(solution)/shard_map/all_to_all | solution.py:1202
  362.6 29.6 %collective-permute-start.45 = (bf16[4,32,2560]{2,1,0:T(8,128)(2,1)}, bf16[4,32,2560]{2,1,0:T(8,128)(2,1)}, u32[]{:S(2)}, u32[]{:S(2)}) collective-permute-start(bf16[4,32,2560]{2,1,0:T(8,128)(2,1)} %get-tuple-element.356), channel_id=1, source_target_pairs={{0,1},{1,0},{2,3},{3,2},{4,5},{5,4},{6,7},{7,6},{8,9},{9,8},{10,11... | collective-permute-start | bytes 1966088 | tf_op jit(solution)/shard_map/ppermute | solution.py:789
  364.0 28.3 %collective-permute-start.46 = (bf16[1,128,2560]{2,1,0:T(8,128)(2,1)}, bf16[1,128,2560]{2,1,0:T(8,128)(2,1)}, u32[]{:S(2)}, u32[]{:S(2)}) collective-permute-start(bf16[1,128,2560]{2,1,0:T(8,128)(2,1)} %get-tuple-element.357), channel_id=1, source_target_pairs={{0,16},{16,0},{1,17},{17,1},{2,18},{18,2},{3,19},{19,3},{4,20},{20... | collective-permute-start | bytes 1966088 | tf_op jit(solution)/shard_map/ppermute | solution.py:789
  365.2 27.0 %collective-permute-start.44 = (bf16[1,64,2048]{2,1,0:T(8,128)(2,1)}, bf16[1,64,2048]{2,1,0:T(8,128)(2,1)S(1)}, u32[]{:S(2)}, u32[]{:S(2)}) collective-permute-start(bf16[1,64,2048]{2,1,0:T(8,128)(2,1)} %get-tuple-element.355), channel_id=1, source_target_pairs={{0,4},{2,6},{4,0},{6,2},{1,5},{3,7},{5,1},{7,3},{8,12},{10,14},{12... | collective-permute-start | bytes 786440 | tf_op jit(solution)/shard_map/ppermute | solution.py:789
  412.8 37.6 %collective-permute-start.49 = (bf16[256,1024]{1,0:T(8,128)(2,1)}, bf16[256,1024]{1,0:T(8,128)(2,1)}, u32[]{:S(2)}, u32[]{:S(2)}) collective-permute-start(bf16[256,1024]{1,0:T(8,128)(2,1)} %get-tuple-element.392), channel_id=1, source_target_pairs={{0,1},{1,0},{2,3},{3,2},{4,5},{5,4},{6,7},{7,6},{8,9},{9,8},{10,11... | collective-permute-start | bytes 1572872 | tf_op jit(solution)/shard_map/ppermute | solution.py:910
  413.0 37.4 %collective-permute-start.48 = (bf16[256,1024]{1,0:T(8,128)(2,1)}, bf16[256,1024]{1,0:T(8,128)(2,1)}, u32[]{:S(2)}, u32[]{:S(2)}) collective-permute-start(bf16[256,1024]{1,0:T(8,128)(2,1)} %get-tuple-element.381), channel_id=1, source_target_pairs={{0,1},{1,0},{2,3},{3,2},{4,5},{5,4},{6,7},{7,6},{8,9},{9,8},{10,11... | collective-permute-start | bytes 1572872 | tf_op jit(solution)/shard_map/ppermute | solution.py:910
  425.5 61.7 %all-to-all-start.3 = ((bf16[32,32,384]{2,1,0:T(8,128)(2,1)}), bf16[32,32,384]{2,1,0:T(8,128)(2,1)}, u32[]{:S(2)}, u32[]{:S(2)}) async-start(bf16[32,32,384]{2,1,0:T(8,128)(2,1)} %bitcast.233), calls=%async_computation.3 | async-start | bytes 1572864 | tf_op jit(solution)/shard_map/all_to_all | solution.py:1248
  (134 other events, 1556.1 us)
